TPU v7x, 512 devices: a whole 4x8x8 slice. The times are simulated.
512 devices in a mesh: row: 32 (over y, x), col: 16 (over z, core).
Axes of the slice: x: 4, y: 8, z: 8, core: 2. Of those that a mesh axis runs over, the one named last changes fastest.
Arguments:
- gram_panel: float32 [8192, 1024], P('row', 'col'), may hold values from -2973.8 to 2973.8, as said below
- left_factor: bfloat16 [8192, 16384], P('row', 'col'), may hold values from -0.42426407 to 0.42426407
- solved_prev: bfloat16 [16384, 8192], P('row', 'col'), may hold values from -0.59765625 to 0.59765625
- right_block: float32 [1024, 8192], P('row', 'col'), may hold values from -6 to 6
Outputs:
- panel_factor: float32 [8192, 1024], P('row', 'col')
- solved_panel: float32 [1024, 8192], P('row', 'col')
Inputs may be any that keep to these rules, and one draw needn't show every extreme that they name: The rows of gram_panel at the panel's indices minus the product of the corresponding rows of left_factor with their transpose form a symmetric positive definite matrix.
All inputs are finite; a program needn't handle non-finite values.
Results may differ from a plain program's by a relative error of at most 0.0006.
Values may be sent and summed in bfloat16 or wider, within the bound.
No kernel may reach another device: no remote copies, remote signals or barrier semaphores. Data moves between devices by JAX's collectives and lax.ppermute only.
A program may use at most 64 MiB of HBM per device.

v0:
```python
import jax
import jax.numpy as jnp
from jax import lax
from jax.sharding import PartitionSpec as P


def spread(value, axis, source):
    kept = jnp.where(lax.axis_index(axis) == source, value, 0).astype(value.dtype)
    return lax.psum(kept, axis)


def invert(diagonal):
    factor = jnp.linalg.cholesky(diagonal)
    identity = jnp.eye(diagonal.shape[0], dtype=jnp.float32)
    return jax.scipy.linalg.solve_triangular(factor, identity, lower=True)


def body(gram_panel, left_factor, solved_prev, right_block):
    row_count = lax.axis_size("row")
    col_count = lax.axis_size("col")
    row_place = lax.axis_index("row")
    col_place = lax.axis_index("col")
    block_rows = right_block.shape[0]
    col_width = gram_panel.shape[1]
    per_column = row_count // col_count
    strip_width = left_factor.shape[1] // per_column
    chosen = lax.all_gather(left_factor[:block_rows], "row", axis=0, tiled=True)
    portion = chosen
    summed = lax.psum_scatter(
        jnp.einsum("pk,mk->pm", portion, left_factor, preferred_element_type=jnp.float32),
        "col",
        scatter_dimension=0,
        tiled=True,
    )
    update = gram_panel - summed.T
    diag_part = lax.all_gather(update[:block_rows], "row", axis=0, tiled=True)
    diagonal = lax.all_gather(diag_part, "col", axis=1, tiled=True)
    inverse = invert(diagonal)
    inverse_cols = lax.dynamic_slice_in_dim(inverse, col_place * col_width, col_width, 0)
    inverse_part = inverse_cols
    panel_factor = lax.dot_general(
        lax.all_gather(update, "col", axis=1, tiled=True),
        inverse_part,
        (((1,), (1,)), ((), ())),
        precision=lax.Precision.HIGHEST,
    )
    strip_piece = lax.dynamic_slice_in_dim(
        chosen, row_place % per_column * strip_width, strip_width, 1
    )
    strip_piece = spread(strip_piece, "col", row_place // per_column)
    portion = strip_piece
    reduced = right_block - lax.psum_scatter(
        jnp.dot(portion, solved_prev, preferred_element_type=jnp.float32),
        "row",
        scatter_dimension=0,
        tiled=True,
    )
    inverse_rows = lax.dynamic_slice_in_dim(inverse, row_place * block_rows, block_rows, 0)
    inverse_part = inverse_rows
    solved_panel = jnp.dot(
        inverse_part,
        lax.all_gather(reduced, "row", axis=0, tiled=True),
        precision=lax.Precision.HIGHEST,
    )
    return (panel_factor, solved_panel)


def solution(mesh):
    in_specs = (P("row", "col"), P("row", "col"), P("row", "col"), P("row", "col"))
    out_specs = (P("row", "col"), P("row", "col"))
    return jax.shard_map(body, mesh=mesh, in_specs=in_specs, out_specs=out_specs, check_vma=False)
```

profile of v0, /device:TPU:1, one launch (start us, length us, event | category | flops | bytes accessed | tf_op | source)
XLA Modules:
  0.0 915.2 jit_solution(4656776217967420164)
XLA Ops:
  8.8 87.9 %all-gather.5.cloned.1.call-done = bf16[1024,1024]{1,0:T(8,128)(2,1)} async-done(((bf16[32,1024]{1,0:T(8,128)(2,1)}), bf16[1024,1024]{1,0:T(8,128)(2,1)}) %all-gather.5.cloned.1.call-update) | async-done | bytes 2097168 | tf_op jit(solution)/shard_map/all_gather | solution.py:27
  99.2 3.4 fusion.77
  102.7 115.2 %all-reduce.3.cloned.1.call-done = bf16[1024,512]{1,0:T(8,128)(2,1)} async-done(((bf16[1024,512]{1,0:T(8,128)(2,1)}), bf16[1024,512]{1,0:T(8,128)(2,1)}) %all-reduce.3.cloned.1.call-update) | async-done | bytes 1048592 | tf_op jit(solution)/shard_map/psum | solution.py:9
  218.0 3.3 fusion.78
  221.3 57.3 %reduce-scatter.3.cloned.1.call-done = f32[64,256]{1,0:T(8,128)} async-done(((f32[1024,256]{1,0:T(8,128)}), f32[64,256]{1,0:T(8,128)}) %reduce-scatter.3.cloned.1.call-update) | async-done | bytes 65552 | tf_op jit(solution)/shard_map/reduce_scatter | solution.py:29
  279.6 38.7 %all_gather.17 = f32[1024,64]{1,0:T(8,128)S(1)} all-gather(f32[32,64]{1,0:T(8,128)S(1)} %copy.7), channel_id=1, replica_groups=mesh['row'=32,'col'=16] {'row'}, dimensions={0}, use_global_device_ids=true | all-gather | bytes 270336 | tf_op jit(solution)/shard_map/all_gather | solution.py:36
  319.3 180.5 %reduce-scatter.5.cloned.1.call-done = f32[32,512]{1,0:T(8,128)} async-done(((f32[1024,512]{1,0:T(8,128)}), f32[32,512]{1,0:T(8,128)}) %reduce-scatter.5.cloned.1.call-update) | async-done | bytes 65552 | tf_op jit(solution)/shard_map/reduce_scatter | solution.py:52
  504.2 47.7 %all-gather.9.cloned.1.call-done = f32[1024,1024]{0,1:T(8,128)} async-done(((f32[1024,64]{0,1:T(8,128)}), f32[1024,1024]{0,1:T(8,128)}) %all-gather.9.cloned.1.call-update) | async-done | bytes 4194320 | tf_op jit(solution)/shard_map/all_gather | solution.py:37
  551.8 5.5 copy.9
  557.3 4.4 fusion
  563.8 11.7 %cholesky.223 = f32[128,128]{1,0:T(8,128)S(1)} custom-call(f32[128,128]{1,0:T(8,128)S(1)} %cholesky.580), custom_call_target="Cholesky" | custom-call | tf_op jit(solution)/shard_map/jit(cholesky)/cholesky | solution.py:13
  575.5 9.8 %custom-call.63 = f32[1,128,128]{1,2,0:T(8,128)S(1)} custom-call(f32[1,128,128]{2,1,0:T(8,128)S(1)} %get-tuple-element.66), custom_call_target="InvertDiagBlocksLowerTriangular" | custom-call | tf_op jit(solution)/shard_map/jit(cholesky)/cholesky | solution.py:13
  591.7 11.9 %cholesky.244 = f32[128,128]{1,0:T(8,128)S(1)} custom-call(f32[128,128]{1,0:T(8,128)S(1)} %cholesky.584), custom_call_target="Cholesky" | custom-call | tf_op jit(solution)/shard_map/jit(cholesky)/cholesky | solution.py:13
  604.3 9.8 %custom-call.64 = f32[1,128,128]{1,2,0:T(8,128)S(1)} custom-call(f32[1,128,128]{2,1,0:T(8,128)S(1)} %get-tuple-element.63), custom_call_target="InvertDiagBlocksLowerTriangular" | custom-call | tf_op jit(solution)/shard_map/jit(cholesky)/cholesky | solution.py:13
  617.5 11.7 %cholesky.468 = f32[128,128]{1,0:T(8,128)S(1)} custom-call(f32[128,128]{1,0:T(8,128)S(1)} %cholesky.589), custom_call_target="Cholesky" | custom-call | tf_op jit(solution)/shard_map/jit(cholesky)/cholesky | solution.py:13
  630.5 9.8 %custom-call.65 = f32[1,128,128]{1,2,0:T(8,128)S(1)} custom-call(f32[1,128,128]{2,1,0:T(8,128)S(1)} %get-tuple-element.60), custom_call_target="InvertDiagBlocksLowerTriangular" | custom-call | tf_op jit(solution)/shard_map/jit(cholesky)/cholesky | solution.py:13
  643.9 12.1 %cholesky.487 = f32[128,128]{1,0:T(8,128)S(1)} custom-call(f32[128,128]{1,0:T(8,128)S(1)} %cholesky.594), custom_call_target="Cholesky" | custom-call | tf_op jit(solution)/shard_map/jit(cholesky)/cholesky | solution.py:13
  657.2 9.8 %custom-call.66 = f32[1,128,128]{1,2,0:T(8,128)S(1)} custom-call(f32[1,128,128]{2,1,0:T(8,128)S(1)} %get-tuple-element.57), custom_call_target="InvertDiagBlocksLowerTriangular" | custom-call | tf_op jit(solution)/shard_map/jit(cholesky)/cholesky | solution.py:13
  670.5 11.7 %cholesky.506 = f32[128,128]{1,0:T(8,128)S(1)} custom-call(f32[128,128]{1,0:T(8,128)S(1)} %cholesky.599), custom_call_target="Cholesky" | custom-call | tf_op jit(solution)/shard_map/jit(cholesky)/cholesky | solution.py:13
  683.5 9.9 %custom-call.67 = f32[1,128,128]{1,2,0:T(8,128)S(1)} custom-call(f32[1,128,128]{2,1,0:T(8,128)S(1)} %get-tuple-element.54), custom_call_target="InvertDiagBlocksLowerTriangular" | custom-call | tf_op jit(solution)/shard_map/jit(cholesky)/cholesky | solution.py:13
  696.8 11.7 %cholesky.526 = f32[128,128]{1,0:T(8,128)S(1)} custom-call(f32[128,128]{1,0:T(8,128)S(1)} %cholesky.604), custom_call_target="Cholesky" | custom-call | tf_op jit(solution)/shard_map/jit(cholesky)/cholesky | solution.py:13
  709.8 9.8 %custom-call.68 = f32[1,128,128]{1,2,0:T(8,128)S(1)} custom-call(f32[1,128,128]{2,1,0:T(8,128)S(1)} %get-tuple-element.51), custom_call_target="InvertDiagBlocksLowerTriangular" | custom-call | tf_op jit(solution)/shard_map/jit(cholesky)/cholesky | solution.py:13
  722.7 11.9 %cholesky.546 = f32[128,128]{1,0:T(8,128)S(1)} custom-call(f32[128,128]{1,0:T(8,128)S(1)} %cholesky.609), custom_call_target="Cholesky" | custom-call | tf_op jit(solution)/shard_map/jit(cholesky)/cholesky | solution.py:13
  735.9 9.8 %custom-call.69 = f32[1,128,128]{1,2,0:T(8,128)S(1)} custom-call(f32[1,128,128]{2,1,0:T(8,128)S(1)} %get-tuple-element.48), custom_call_target="InvertDiagBlocksLowerTriangular" | custom-call | tf_op jit(solution)/shard_map/jit(cholesky)/cholesky | solution.py:13
  748.4 11.7 %cholesky.564 = f32[128,128]{1,0:T(8,128)S(1)} custom-call(f32[128,128]{1,0:T(8,128)S(1)} %convolution_subtract_fusion.11), custom_call_target="Cholesky" | custom-call | tf_op jit(solution)/shard_map/jit(cholesky)/cholesky | solution.py:13
  767.2 4.8 select_select_fusion
  772.0 22.5 %while.1 = (s32[]{:T(128)}, f32[1024,1024]{1,0:T(8,128)}, s32[8,2]{0,1:T(2,128)S(1)}, f32[8,128,128]{2,1,0:T(8,128)S(1)}, s32[]{:T(128)}) while((s32[]{:T(128)}, f32[1024,1024]{1,0:T(8,128)}, s32[8,2]{0,1:T(2,128)S(1)}, f32[8,128,128]{2,1,0:T(8,128)S(1)}, s32[]{:T(128)}) %tuple.61), condition=%wide.while_cond, body=%wide.while_body.sunk | while | flops 2 | bytes 131181 | solution.py:15
  794.5 79.0 %custom-call.70 = f32[8,128,128]{1,2,0:T(8,128)S(1)} custom-call(f32[8,128,128]{2,1,0:T(8,128)S(1)} %get-tuple-element.9), custom_call_target="InvertDiagBlocksLowerTriangular" | custom-call | tf_op jit(solution)/shard_map/jit(_solve_triangular)/triangular_solve | solution.py:15
  888.7 2.6 convolution_subtract_fusion.2
  892.8 2.8 convolution_subtract_fusion.1
  897.1 3.4 convolution_subtract_fusion.3
  902.0 3.6 fusion.53
  (114 shorter events, 91.8 us)
Async XLA Ops:
  7.2 210.8 %copy-start = (bf16[512,512]{1,0:T(8,128)(2,1)S(1)}, bf16[512,512]{1,0:T(8,128)(2,1)}, u32[]{:S(2)}) copy-start(bf16[512,512]{1,0:T(8,128)(2,1)} %param.6) | copy-start | bytes 1572868
  7.2 89.6 %all-gather.5.cloned.1.call-start = ((), (), s32[]{:S(2)}) async-start(), calls=%async_computation.2 | async-start | bytes 2162688 | tf_op jit(solution)/shard_map/all_gather | solution.py:27
  8.8 209.2 %all-reduce.3.cloned.1.call-start = ((), (), s32[]{:S(2)}) async-start(), calls=%async_computation.6 | async-start | bytes 2097152 | tf_op jit(solution)/shard_map/psum | solution.py:9
  99.2 179.5 %reduce-scatter.3.cloned.1.call-start = ((), (), s32[]{:S(2)}) async-start(), calls=%async_computation.3 | async-start | bytes 1114112 | tf_op jit(solution)/shard_map/reduce_scatter | solution.py:29
  102.6 176.0 %copy-start.4 = (f32[256,64]{0,1:T(8,128)S(1)}, f32[256,64]{0,1:T(8,128)}, u32[]{:S(2)}) copy-start(f32[256,64]{0,1:T(8,128)} %param.4) | copy-start | bytes 196612
  102.7 397.2 %copy-start.5 = (f32[32,512]{1,0:T(8,128)S(1)}, f32[32,512]{1,0:T(8,128)}, u32[]{:S(2)}) copy-start(f32[32,512]{1,0:T(8,128)} %param.7) | copy-start | bytes 196612
  102.7 397.1 %reduce-scatter.5.cloned.1.call-start = ((), (), s32[]{:S(2)}) async-start(), calls=%async_computation.7 | async-start | bytes 2162688 | tf_op jit(solution)/shard_map/reduce_scatter | solution.py:52
  221.3 330.6 %all-gather.9.cloned.1.call-start = ((), (), s32[]{:S(2)}) async-start(), calls=%async_computation.5 | async-start | bytes 4456448 | tf_op jit(solution)/shard_map/all_gather | solution.py:37
  279.5 224.6 %copy-start.3 = (f32[256,64]{0,1:T(8,128)}, f32[256,64]{0,1:T(8,128)S(1)}, u32[]{:S(2)}) copy-start(f32[256,64]{0,1:T(8,128)S(1)} %bitcast_subtract_fusion) | copy-start | bytes 196612
  319.2 582.7 %all-gather.11.cloned.1.call-start = ((), (), s32[]{:S(2)}) async-start(), calls=%async_computation.8 | async-start | bytes 2162688 | tf_op jit(solution)/shard_map/all_gather | solution.py:62
  501.3 404.3 %all-gather.7.cloned.1.call-start = ((), (), s32[]{:S(2)}) async-start(), calls=%async_computation.4 | async-start | bytes 1114112 | tf_op jit(solution)/shard_map/all_gather | solution.py:42
  561.8 2.0 copy-start.2
  873.5 4.7 copy-start.1
Sparse Core Ops, SparseCore 0:
  11.8 84.9 all-gather.4
  99.3 118.6 all-reduce.2
  221.0 57.5 reduce-scatter.2
  282.9 216.8 reduce-scatter.4
  502.0 49.8 all-gather.8
  555.9 77.5 all-gather.10
  636.5 43.8 all-gather.6
where the time goes:
time: 920 us; the launch traced here: 915 us
  waiting for transfers between devices  489 us (53%)
  other arithmetic  268 us (29%)
  matrix products  64.5 us (7%)
  blocking collectives  38.7 us (4%)
  local copies, waits for them, and re-layouts  34.8 us (4%)
  between operations  19.7 us (2%)
    reduce_scatter x1, waiting for transfers between devices, body(): lax.psum_scatter(jnp.dot(portion, solved_prev, preferred_element_type=jnp...  181 us
    another operation x30, other arithmetic, invert(): factor = jnp.linalg.cholesky(diagonal)  173 us
    psum x1, waiting for transfers between devices, spread(): return lax.psum(kept, axis)  115 us
    all_gather x1, waiting for transfers between devices, body(): chosen = lax.all_gather(left_factor[:block_rows], 'row', axis=0, tiled=True)  87.9 us
    another operation x3, other arithmetic, invert(): return jax.scipy.linalg.solve_triangular(factor, identity, lower=True)  83.8 us
    reduce_scatter x1, waiting for transfers between devices, body(): lax.psum_scatter(jnp.einsum('pk,mk->pm', portion, left_factor, preferred_...  57.3 us
    all_gather x1, waiting for transfers between devices, body(): diagonal = lax.all_gather(diag_part, 'col', axis=1, tiled=True)  47.7 us
    all_gather x1, blocking collectives, body(): diag_part = lax.all_gather(update[:block_rows], 'row', axis=0, tiled=True)  38.7 us
  transfers between devices with their start and end apart: 7, of which 5 were waited for; matrix products, arithmetic and copies ran while one was open for 39% of the time, Pallas kernels for 0%

commit v1 on v0

v1 whole, which is shorter than its diff:
```python
import jax
import jax.numpy as jnp
from jax import lax
from jax.experimental import pallas as pl
from jax.experimental.pallas import tpu as pltpu
from jax.sharding import PartitionSpec as P

HI = lax.Precision.HIGHEST


def factor_block(s_ref):
    lane = lax.broadcasted_iota(jnp.int32, (8, 128), 1)
    sub = lax.broadcasted_iota(jnp.int32, (8, 128), 0)
    for g in range(16):
        base = 8 * g
        inside = (lane >= base) & (lane < base + 8)
        w = s_ref[base:base + 8, :]
        x = [[None] * 8 for _ in range(8)]
        for j in range(8):
            c = jnp.broadcast_to(w[:, base + j:base + j + 1], (8, 128))
            for i in range(j, 8):
                x[i][j] = jnp.broadcast_to(c[i:i + 1, :], (8, 128))
        start = jnp.where(lane == sub + base, 1.0, jnp.where(inside, 0.0, w))
        r = [jnp.broadcast_to(start[j:j + 1, :], (8, 128)) for j in range(8)]
        m = [[None] * 8 for _ in range(8)]
        q = [None] * 8
        top = None
        for j in range(8):
            s = lax.rsqrt(x[j][j])
            t = r[j] * s
            top = t if top is None else jnp.where(sub == j, t, top)
            m[j][j] = s
            for k in range(j):
                m[j][k] = m[j][k] * s
            for k in range(j + 1):
                part = m[j][k] * t
                q[k] = part if q[k] is None else q[k] + part
            col = {i: x[i][j] * s for i in range(j + 1, 8)}
            for i in range(j + 1, 8):
                for k in range(j + 1, i + 1):
                    x[i][k] = x[i][k] - col[i] * col[k]
                r[i] = r[i] - col[i] * t
                for k in range(j + 1):
                    part = col[i] * m[j][k]
                    m[i][k] = -part if m[i][k] is None else m[i][k] - part
        s_ref[base:base + 8, :] = top
        for v in range(g + 1, 16):
            wv = s_ref[8 * v:8 * v + 8, :]
            acc = jnp.where(inside, 0.0, wv)
            for j in range(8):
                acc = acc - jnp.broadcast_to(wv[:, base + j:base + j + 1], (8, 128)) * q[j]
            s_ref[8 * v:8 * v + 8, :] = acc
    rows = lax.broadcasted_iota(jnp.int32, (128, 128), 0)
    cols = lax.broadcasted_iota(jnp.int32, (128, 128), 1)
    s_ref[...] = jnp.where(cols <= rows, s_ref[...], 0.0)


def mm(a, b):
    return lax.dot_general(a, b, (((1,), (0,)), ((), ())), precision=HI, preferred_element_type=jnp.float32)


def mtm(a, b):
    return lax.dot_general(a, b, (((0,), (0,)), ((), ())), precision=HI, preferred_element_type=jnp.float32)


def kernel(a_ref, w_ref, s_ref, m_ref):
    n = a_ref.shape[0]
    big = n // 256
    for j in range(big):
        w_ref[j] = a_ref[:, 256 * j:256 * j + 256]

    def step(b, carry):
        top = pl.multiple_of(b * 256, 256)
        mid = pl.multiple_of(b * 256 + 128, 128)

        def half(h, carry):
            @pl.when(h == 0)
            def _():
                s_ref[...] = w_ref[b, pl.ds(top, 128), 0:128]

            @pl.when(h == 1)
            def _():
                m_ref[0:128, 0:128] = s_ref[...]
                upper = mm(s_ref[...], w_ref[b, pl.ds(top, 128), 128:256])
                m_ref[0:128, 128:256] = upper
                s_ref[...] = w_ref[b, pl.ds(mid, 128), 128:256] - mtm(upper, upper)

            factor_block(s_ref)
            return carry

        lax.fori_loop(0, 2, half, 0)
        lower = mtm(m_ref[0:128, 128:256], m_ref[0:128, 0:128])
        m_ref[128:256, 0:128] = -mm(s_ref[...], lower)
        m_ref[0:128, 128:256] = jnp.zeros((128, 128), jnp.float32)
        m_ref[128:256, 128:256] = s_ref[...]
        inv = m_ref[...]

        for j in range(big):
            w_ref[j, pl.ds(top, 256), :] = mm(inv, w_ref[j, pl.ds(top, 256), :])
        w_ref[b, pl.ds(top, 256), :] = inv

        def below(i, carry):
            at = pl.multiple_of(i * 256, 256)
            w_ref[b, pl.ds(at, 256), :] = jnp.zeros((256, 256), jnp.float32)
            lt = w_ref[i, pl.ds(top, 256), :]
            for j in range(big):
                @pl.when((j <= b) | (j >= i))
                def _():
                    w_ref[j, pl.ds(at, 256), :] = w_ref[j, pl.ds(at, 256), :] - mtm(lt, w_ref[j, pl.ds(top, 256), :])
            w_ref[i, pl.ds(top, 256), :] = jnp.zeros((256, 256), jnp.float32)
            return carry

        lax.fori_loop(b + 1, big, below, 0)
        return carry

    lax.fori_loop(0, big, step, 0)


def invert(diagonal):
    n = diagonal.shape[0]
    return pl.pallas_call(
        kernel,
        out_shape=jax.ShapeDtypeStruct((n // 256, n, 256), jnp.float32),
        in_specs=[pl.BlockSpec(memory_space=pltpu.VMEM)],
        out_specs=pl.BlockSpec(memory_space=pltpu.VMEM),
        scratch_shapes=[pltpu.VMEM((128, 128), jnp.float32), pltpu.VMEM((256, 256), jnp.float32)],
        compiler_params=pltpu.CompilerParams(vmem_limit_bytes=32 * 1024 * 1024),
    )(diagonal)


def split_three(value):
    high = lax.reduce_precision(value, 8, 7)
    rest = value - high
    middle = lax.reduce_precision(rest, 8, 7)
    return [part.astype(jnp.bfloat16) for part in (high, middle, rest - middle)]


def collect(value, axis, count, groups=None):
    many = jnp.broadcast_to(value[None], (count,) + value.shape)
    return lax.all_to_all(many, axis, 0, 0, axis_index_groups=groups)


def body(gram_panel, left_factor, solved_prev, right_block):
    row_count = lax.axis_size("row")
    col_count = lax.axis_size("col")
    row_place = lax.axis_index("row")
    col_place = lax.axis_index("col")
    block_rows = right_block.shape[0]
    col_width = gram_panel.shape[1]
    panel = block_rows * row_count
    depth = left_factor.shape[1]
    wide = 4
    tall = row_count // wide
    chips = col_count // 2
    x_place = row_place % wide
    along_x = [[y * wide + x for x in range(wide)] for y in range(tall)]
    along_y = [[y * wide + x for y in range(tall)] for x in range(wide)]
    along_z = [[z * 2 + core for z in range(chips)] for core in range(2)]
    own = left_factor[:block_rows]
    per_col = row_count // col_count
    strip = depth // per_col

    both = ("row", "col")
    pieces = []
    for turn in range(per_col):
        half = (row_place + turn) % per_col
        sent = lax.dynamic_slice_in_dim(own, half * strip, strip, 1)
        pairs = []
        for r in range(row_count):
            for c in range(col_count):
                to_row = per_col * c + (r + turn) % per_col
                pairs.append((r * col_count + c, to_row * col_count + r // per_col))
        pieces.append(lax.ppermute(sent, both, pairs))
    flip = (row_place % per_col) == 1
    mine = jnp.concatenate(
        [jnp.where(flip, pieces[1], pieces[0]), jnp.where(flip, pieces[0], pieces[1])], axis=0
    )
    strip_piece = lax.all_gather(mine, "col", axis=0, tiled=True)

    gram_parts = split_three(gram_panel[:block_rows])
    packed = jnp.concatenate([own] + gram_parts, axis=1)
    from_x = collect(packed, "row", wide, along_x)
    from_y = collect(own, "row", tall, along_y)
    rows_x = from_x[:, :, :depth].reshape(wide * block_rows, depth)
    rows_y = from_y.reshape(tall * block_rows, depth)
    gram_x = from_x[:, :, depth:].astype(jnp.float32).reshape(wide * block_rows, 3, per_col, block_rows)
    gram_x = gram_x[:, 0] + gram_x[:, 1] + gram_x[:, 2]
    per_x = wide // per_col
    gram_own = lax.dynamic_index_in_dim(gram_x, x_place % per_col, 1, keepdims=False)
    has_gram = (col_place % per_x) == (x_place // per_col)
    y_at = lax.broadcasted_iota(jnp.int32, (1, tall, 1), 1)
    placed = jnp.where(has_gram & (y_at == col_place // per_x), gram_own[:, None, :], 0.0)
    partial = placed.reshape(wide * block_rows, tall * block_rows) - lax.dot_general(
        rows_x, rows_y, (((1,), (1,)), ((), ())), preferred_element_type=jnp.float32
    )
    thin = wide * block_rows // col_count
    partial = partial.reshape(col_count, thin, tall * block_rows)
    own_diag = jnp.sum(lax.all_to_all(partial, "col", 0, 0), axis=0)
    diag_z = collect(own_diag, "col", chips, along_z)
    diag_row = collect(diag_z.reshape(chips * thin, tall * block_rows), "row", row_count)
    other = lax.ppermute(diag_row, "col", [(i, i ^ 1) for i in range(col_count)])
    even = (col_place % 2) == 0
    pair = jnp.stack([jnp.where(even, diag_row, other), jnp.where(even, other, diag_row)], axis=0)
    pair = pair.reshape(2, tall, wide, chips, thin, tall, block_rows)
    diagonal = pair.transpose(1, 3, 0, 4, 5, 2, 6).reshape(panel, panel)
    inverse = invert(diagonal)

    chosen = lax.all_gather(rows_y, "row", axis=0, tiled=False, axis_index_groups=along_x)
    chosen = chosen.reshape(wide, tall, block_rows, depth).transpose(1, 0, 2, 3).reshape(panel, depth)
    summed = lax.psum_scatter(
        lax.dot_general(chosen, left_factor, (((1,), (1,)), ((), ())), preferred_element_type=jnp.float32),
        "col",
        scatter_dimension=0,
        tiled=True,
    )
    update = lax.all_gather(gram_panel.T - summed, "col", axis=0, tiled=True)

    product = jnp.dot(strip_piece, solved_prev, preferred_element_type=jnp.float32)
    product = product.reshape(row_count, block_rows, product.shape[1])
    reduced = right_block - jnp.sum(lax.all_to_all(product, "row", 0, 0), axis=0)
    reduced = lax.all_gather(reduced, "row", axis=0, tiled=True)

    def rows_of_inverse(start, size):
        part = lax.dynamic_slice_in_dim(inverse, start, size, 1)
        return part.transpose(1, 0, 2).reshape(size, panel)

    panel_factor = mm(rows_of_inverse(col_place * col_width, col_width), update).T
    solved_panel = mm(rows_of_inverse(row_place * block_rows, block_rows), reduced)
    return (panel_factor, solved_panel)


def solution(mesh):
    in_specs = (P("row", "col"), P("row", "col"), P("row", "col"), P("row", "col"))
    out_specs = (P("row", "col"), P("row", "col"))
    return jax.shard_map(body, mesh=mesh, in_specs=in_specs, out_specs=out_specs, check_vma=False)
```

time: 920 us -> 343 us (0.37)
  waiting for transfers between devices: 489 us -> 136 us
  other arithmetic: 268 us -> 13.9 us
  starting transfers between devices: 0.29 us -> 61 us
  Pallas kernels: 0 us -> 53.4 us
  matrix products: 64.5 us -> 12.2 us
  blocking collectives: 38.7 us -> 0 us
  local copies, waits for them, and re-layouts: 34.8 us -> 51.7 us
    another operation x33 -> x0, other arithmetic: 256 us -> none  [the longest x30 173 us: invert(): factor = jnp.linalg.cholesky(diagonal)]
    reduce_scatter x2 -> x1, waiting for transfers between devices: 238 us -> 27.3 us  [body(): lax.psum_scatter(lax.dot_general(chosen, left_factor, (((1,), (1,)), ((),...]
    all_gather x4, waiting for transfers between devices: 136 us -> 18 us  [the longest x1 17.9 us: body(): lax.all_gather(rows_y, 'row', axis=0, tiled=False, axis_index_groups=alon...]
    psum x1 -> x0, waiting for transfers between devices: 115 us -> none  [spread(): return lax.psum(kept, axis)]
    all_to_all x0 -> x6, waiting for transfers between devices: none -> 81.1 us  [the longest x4 46 us: collect(): return lax.all_to_all(many, axis, 0, 0, axis_index_groups=groups)]
    pallas_call x0 -> x1, Pallas kernels: none -> 53.4 us  [invert(): pl.pallas_call(kernel, out_shape=jax.ShapeDtypeStruct((n // 256, n, 256),...]
    another operation x29 -> x0, matrix products: 51.6 us -> none  [the longest x15 28.4 us: invert(): return jax.scipy.linalg.solve_triangular(factor, identity, lower=True)]
    all_to_all x0 -> x6, starting transfers between devices: none -> 46.9 us  [the longest x4 37.5 us: collect(): return lax.all_to_all(many, axis, 0, 0, axis_index_groups=groups)]
  transfers between devices with their start and end apart: 7 -> 14, of which waited for: 5 -> 10; matrix products, arithmetic and copies ran while one was open for 39% -> 21% of each run, Pallas kernels for 0% -> 16%
where the time goes in v1:
time: 343 us; the launch traced here: 342 us
  waiting for transfers between devices  136 us (40%)
  starting transfers between devices  61 us (18%)
  Pallas kernels  53.4 us (16%)
  local copies, waits for them, and re-layouts  51.7 us (15%)
  between operations  14.2 us (4%)
  other arithmetic  13.9 us (4%)
  matrix products  12.2 us (4%)
    pallas_call x1, Pallas kernels, invert(): pl.pallas_call(kernel, out_shape=jax.ShapeDtypeStruct((n // 256, n, 256),...  53.4 us
    all_to_all x4, waiting for transfers between devices, collect(): return lax.all_to_all(many, axis, 0, 0, axis_index_groups=groups)  46 us
    all_to_all x4, starting transfers between devices, collect(): return lax.all_to_all(many, axis, 0, 0, axis_index_groups=groups)  37.5 us
    reduce_scatter x1, waiting for transfers between devices, body(): lax.psum_scatter(lax.dot_general(chosen, left_factor, (((1,), (1,)), ((),...  27.3 us
    all_to_all x1, waiting for transfers between devices, body(): lax.all_to_all(product, 'row', 0, 0)  26.7 us
    reshape x1, local copies, waits for them, and re-layouts, body(): diagonal = pair.transpose(1, 3, 0, 4, 5, 2, 6).reshape(panel, panel)  18.4 us
    all_gather x1, waiting for transfers between devices, body(): lax.all_gather(rows_y, 'row', axis=0, tiled=False, axis_index_groups=alon...  17.9 us
    transpose x1, local copies, waits for them, and re-layouts, body(): diagonal = pair.transpose(1, 3, 0, 4, 5, 2, 6).reshape(panel, panel)  12.1 us
  transfers between devices with their start and end apart: 14, of which 10 were waited for; matrix products, arithmetic and copies ran while one was open for 21% of the time, Pallas kernels for 16%

profile of v1, /device:TPU:1, one launch (start us, length us, event | category | flops | bytes accessed | tf_op | source)
XLA Modules:
  0.0 342.0 jit_solution(10898574189083603896)
XLA Ops:
  8.2 5.8 %collective-permute-start.1 = (bf16[32,512]{1,0:T(8,128)(2,1)S(1)}, bf16[32,512]{1,0:T(8,128)(2,1)S(1)}, u32[]{:S(2)}, u32[]{:S(2)}) collective-permute-start(bf16[32,512]{1,0:T(8,128)(2,1)S(1)} %get-tuple-element.9), channel_id=1, source_target_pairs={{0,16},{1,48},{2,80},{3,112},{4,144},{5,176},{6,208},{7,240},{8,27... | collective-permute-start | bytes 98312 | tf_op jit(solution)/shard_map/ppermute | solution.py:173
  13.9 2.2 collective-permute-start.2
  16.1 4.5 %collective-permute-done.2 = bf16[32,512]{1,0:T(8,128)(2,1)S(1)} collective-permute-done((bf16[32,512]{1,0:T(8,128)(2,1)S(1)}, bf16[32,512]{1,0:T(8,128)(2,1)S(1)}, u32[]{:S(2)}, u32[]{:S(2)}) %collective-permute-start.2) | collective-permute-done | bytes 32800 | tf_op jit(solution)/shard_map/ppermute | solution.py:173
  23.0 3.5 %all-to-all-start.1 = ((bf16[4,32,1216]{2,1,0:T(8,128)(2,1)}), bf16[4,32,1216]{2,1,0:T(8,128)(2,1)S(1)}, u32[]{:S(2)}, u32[]{:S(2)}) async-start(bf16[4,32,1216]{2,1,0:T(8,128)(2,1)} %broadcast_in_dim.58), calls=%async_computation.2 | async-start | bytes 655360 | tf_op jit(solution)/shard_map/all_to_all | solution.py:140
  26.7 7.1 %all-to-all-done.1 = bf16[4,32,1216]{2,1,0:T(8,128)(2,1)S(1)} async-done(((bf16[4,32,1216]{2,1,0:T(8,128)(2,1)}), bf16[4,32,1216]{2,1,0:T(8,128)(2,1)S(1)}, u32[]{:S(2)}, u32[]{:S(2)}) %all-to-all-start.1) | async-done | bytes 311328 | tf_op jit(solution)/shard_map/all_to_all | solution.py:140
  34.7 23.6 %all-to-all-start = ((bf16[8,32,1024]{2,1,0:T(8,128)(2,1)}), bf16[8,32,1024]{2,1,0:T(8,128)(2,1)S(1)}, u32[]{:S(2)}, u32[]{:S(2)}) async-start(bf16[8,32,1024]{2,1,0:T(8,128)(2,1)} %broadcast_in_dim.54), calls=%async_computation | async-start | bytes 1048576 | tf_op jit(solution)/shard_map/all_to_all | solution.py:140
  59.4 17.0 %all-to-all-done = bf16[8,32,1024]{2,1,0:T(8,128)(2,1)S(1)} async-done(((bf16[8,32,1024]{2,1,0:T(8,128)(2,1)}), bf16[8,32,1024]{2,1,0:T(8,128)(2,1)S(1)}, u32[]{:S(2)}, u32[]{:S(2)}) %all-to-all-start) | async-done | bytes 524320 | tf_op jit(solution)/shard_map/all_to_all | solution.py:140
  77.4 5.4 %all-to-all-start.2 = ((f32[16,8,256]{2,1,0:T(8,128)}), f32[16,8,256]{2,1,0:T(8,128)S(1)}, u32[]{:S(2)}, u32[]{:S(2)}) async-start(f32[16,8,256]{2,1,0:T(8,128)} %fusion), calls=%async_computation.3 | async-start | bytes 262144 | tf_op jit(solution)/shard_map/all_to_all | solution.py:198
  83.5 8.4 %all-to-all-done.2 = f32[16,8,256]{2,1,0:T(8,128)S(1)} async-done(((f32[16,8,256]{2,1,0:T(8,128)}), f32[16,8,256]{2,1,0:T(8,128)S(1)}, u32[]{:S(2)}, u32[]{:S(2)}) %all-to-all-start.2) | async-done | bytes 131104 | tf_op jit(solution)/shard_map/all_to_all | solution.py:198
  92.6 3.4 all-to-all-start.3
  96.0 3.3 fusion.5
  99.3 4.4 %all-to-all-done.3 = f32[8,8,256]{2,1,0:T(8,128)S(1)} async-done(((f32[8,8,256]{2,1,0:T(8,128)}), f32[8,8,256]{2,1,0:T(8,128)S(1)}, u32[]{:S(2)}, u32[]{:S(2)}) %all-to-all-start.3) | async-done | bytes 65568 | tf_op jit(solution)/shard_map/all_to_all | solution.py:140
  103.7 4.0 %all-to-all-start.5 = ((f32[32,32,512]{2,1,0:T(8,128)}), f32[32,32,512]{2,1,0:T(8,128)S(1)}, u32[]{:S(2)}, u32[]{:S(2)}) async-start(f32[32,32,512]{2,1,0:T(8,128)} %bitcast.14), calls=%async_computation.6 | async-start | bytes 4194304 | tf_op jit(solution)/shard_map/all_to_all | solution.py:220
  107.7 17.9 %all-gather.5.cloned.1.call-done = bf16[4,256,1024]{2,1,0:T(8,128)(2,1)} async-done(((bf16[1,256,1024]{2,1,0:T(8,128)(2,1)}), bf16[4,256,1024]{2,1,0:T(8,128)(2,1)}) %all-gather.5.cloned.1.call-update) | async-done | bytes 2097168 | tf_op jit(solution)/shard_map/all_gather | solution.py:208
  125.7 1.8 copy.20
  127.5 1.8 fusion.3
  129.3 26.7 %all-to-all-done.5 = f32[32,32,512]{2,1,0:T(8,128)S(1)} async-done(((f32[32,32,512]{2,1,0:T(8,128)}), f32[32,32,512]{2,1,0:T(8,128)S(1)}, u32[]{:S(2)}, u32[]{:S(2)}) %all-to-all-start.5) | async-done | bytes 2097184 | tf_op jit(solution)/shard_map/all_to_all | solution.py:220
  157.6 7.0 %all-to-all-start.4 = ((f32[32,64,256]{2,1,0:T(8,128)}), f32[32,64,256]{2,1,0:T(8,128)}, u32[]{:S(2)}, u32[]{:S(2)}) async-start(f32[32,64,256]{2,1,0:T(8,128)} %broadcast_in_dim.65), calls=%async_computation.5 | async-start | bytes 4194304 | tf_op jit(solution)/shard_map/all_to_all | solution.py:140
  164.7 27.3 %reduce-scatter.2.cloned.1.call-done = f32[64,256]{1,0:T(8,128)} async-done(((f32[1024,256]{1,0:T(8,128)}), f32[64,256]{1,0:T(8,128)}) %reduce-scatter.2.cloned.1.call-update) | async-done | bytes 65552 | tf_op jit(solution)/shard_map/reduce_scatter | solution.py:210
  194.4 17.5 %all-to-all-done.4 = f32[32,64,256]{2,1,0:T(8,128)} async-done(((f32[32,64,256]{2,1,0:T(8,128)}), f32[32,64,256]{2,1,0:T(8,128)}, u32[]{:S(2)}, u32[]{:S(2)}) %all-to-all-start.4) | async-done | bytes 2097184 | tf_op jit(solution)/shard_map/all_to_all | solution.py:140
  211.9 5.9 %collective-permute-start = (f32[32,64,256]{2,1,0:T(8,128)}, f32[32,64,256]{2,1,0:T(8,128)}, u32[]{:S(2)}, u32[]{:S(2)}) collective-permute-start(f32[32,64,256]{2,1,0:T(8,128)} %all-to-all-done.4), channel_id=1, source_target_pairs={{0,1},{1,0},{2,3},{3,2},{4,5},{5,4},{6,7},{7,6},{8,9},{9,8},{10,11... | collective-permute-start | bytes 6291464 | tf_op jit(solution)/shard_map/ppermute | solution.py:201
  217.8 3.9 %collective-permute-done = f32[32,64,256]{2,1,0:T(8,128)} collective-permute-done((f32[32,64,256]{2,1,0:T(8,128)}, f32[32,64,256]{2,1,0:T(8,128)}, u32[]{:S(2)}, u32[]{:S(2)}) %collective-permute-start) | collective-permute-done | bytes 2097184 | tf_op jit(solution)/shard_map/ppermute | solution.py:201
  221.7 4.1 %broadcast_select_fusion.1 = (f32[32,64,256]{2,1,0:T(8,128)S(1)}, f32[32,64,256]{2,1,0:T(8,128)}) fusion(f32[32,64,256]{2,1,0:T(8,128)} %all-to-all-done.4, f32[32,64,256]{2,1,0:T(8,128)} %collective-permute-done, pred[]{:T(512)S(6)} %eq.28), kind=kLoop, calls=%fused_computation.4 | loop fusion | flops 1048576 | bytes 8388609 | tf_op jit(solution)/shard_map/jit(_where)/select_n | solution.py:203
  225.8 6.1 %stack.10 = f32[1,8,4,8,8,8,32]{6,5,4,3,2,1,0:T(8,128)} reshape(f32[32,64,256]{2,1,0:T(8,128)} %get-tuple-element.3) | data formatting | bytes 4194304 | tf_op jit(solution)/shard_map/stack | solution.py:203
  231.9 4.3 %stack.9 = f32[1,8,4,8,8,8,32]{6,5,4,3,2,1,0:T(8,128)} reshape(f32[32,64,256]{2,1,0:T(8,128)S(1)} %get-tuple-element.2) | data formatting | bytes 4194304 | tf_op jit(solution)/shard_map/stack | solution.py:203
  236.2 6.8 %maximum_bitcast_fusion = f32[8,8,2,8,8,4,32]{6,4,3,1,5,0,2:T(8,128)S(1)} fusion(f32[1,8,4,8,8,8,32]{6,5,4,3,2,1,0:T(8,128)} %stack.10, f32[1,8,4,8,8,8,32]{6,5,4,3,2,1,0:T(8,128)} %stack.9), kind=kLoop, calls=%fused_computation | loop fusion | flops 1048576 | bytes 8388608 | tf_op jit(solution)/shard_map/transpose | solution.py:205
  243.0 12.1 %copy.24 = f32[8,8,2,8,8,4,32]{6,5,4,3,2,1,0:T(4,128)} copy(f32[8,8,2,8,8,4,32]{6,4,3,1,5,0,2:T(8,128)S(1)} %maximum_bitcast_fusion) | data formatting | bytes 8388608 | tf_op jit(solution)/shard_map/transpose | solution.py:205
  255.1 18.4 %reshape.67.a_ref = f32[1024,1024]{1,0:T(8,128)} reshape(f32[8,8,2,8,8,4,32]{6,5,4,3,2,1,0:T(4,128)} %copy.24) | data formatting | bytes 8388608 | tf_op jit(solution)/shard_map/reshape | solution.py:205
  273.5 2.2 copy-done.2
  275.7 53.4 %shard_map.59 = f32[4,1024,256]{2,1,0:T(8,128)S(1)} custom-call(f32[1024,1024]{1,0:T(8,128)S(1)} %copy-done.2), custom_call_target="tpu_custom_call" | custom-call | tf_op jit(solution)/shard_map/pallas_call | solution.py:121
  329.3 2.6 fusion.4
  332.0 3.5 %fusion.6 = f32[32,512]{1,0:T(8,128)} fusion(f32[32,1024]{1,0:T(8,128)S(1)} %bitcast.42, f32[1024,512]{1,0:T(8,128)} %all-gather.11.cloned.1.call-done), kind=kOutput, calls=%fused_computation.28 | convolution fusion | flops 201326592 | bytes 2293760 | tf_op jit(solution)/shard_map/dot_general | solution.py:59
  (63 shorter events, 11.8 us)
Async XLA Ops:
  7.2 88.8 %copy-start = (bf16[512,512]{1,0:T(8,128)(2,1)S(1)}, bf16[512,512]{1,0:T(8,128)(2,1)}, u32[]{:S(2)}) copy-start(bf16[512,512]{1,0:T(8,128)(2,1)} %param.6) | copy-start | bytes 1572868
  7.2 88.8 %all-gather.9.cloned.1.call-start = ((), (), s32[]{:S(2)}) async-start(), calls=%async_computation.10 | async-start | bytes 1114112 | tf_op jit(solution)/shard_map/all_gather | solution.py:178
  8.2 8.0 %collective-permute-start.1 = (bf16[32,512]{1,0:T(8,128)(2,1)S(1)}, bf16[32,512]{1,0:T(8,128)(2,1)S(1)}, u32[]{:S(2)}, u32[]{:S(2)}) collective-permute-start(bf16[32,512]{1,0:T(8,128)(2,1)S(1)} %get-tuple-element.9), channel_id=1, source_target_pairs={{0,16},{1,48},{2,80},{3,112},{4,144},{5,176},{6,208},{7,240},{8,27... | collective-permute-start | bytes 98312 | tf_op jit(solution)/shard_map/ppermute | solution.py:173
  13.9 6.7 %collective-permute-start.2 = (bf16[32,512]{1,0:T(8,128)(2,1)S(1)}, bf16[32,512]{1,0:T(8,128)(2,1)S(1)}, u32[]{:S(2)}, u32[]{:S(2)}) collective-permute-start(bf16[32,512]{1,0:T(8,128)(2,1)S(1)} %get-tuple-element.10), channel_id=1, source_target_pairs={{0,0},{1,32},{2,64},{3,96},{4,128},{5,160},{6,192},{7,224},{8,256}... | collective-permute-start | bytes 98312 | tf_op jit(solution)/shard_map/ppermute | solution.py:173
  23.0 10.8 %all-to-all-start.1 = ((bf16[4,32,1216]{2,1,0:T(8,128)(2,1)}), bf16[4,32,1216]{2,1,0:T(8,128)(2,1)S(1)}, u32[]{:S(2)}, u32[]{:S(2)}) async-start(bf16[4,32,1216]{2,1,0:T(8,128)(2,1)} %broadcast_in_dim.58), calls=%async_computation.2 | async-start | bytes 655360 | tf_op jit(solution)/shard_map/all_to_all | solution.py:140
  34.7 41.7 %all-to-all-start = ((bf16[8,32,1024]{2,1,0:T(8,128)(2,1)}), bf16[8,32,1024]{2,1,0:T(8,128)(2,1)S(1)}, u32[]{:S(2)}, u32[]{:S(2)}) async-start(bf16[8,32,1024]{2,1,0:T(8,128)(2,1)} %broadcast_in_dim.54), calls=%async_computation | async-start | bytes 1048576 | tf_op jit(solution)/shard_map/all_to_all | solution.py:140
  76.4 6.4 %copy-start.3 = (bf16[8,32,1024]{2,1,0:T(8,128)(2,1)}, bf16[8,32,1024]{2,1,0:T(8,128)(2,1)S(1)}, u32[]{:S(2)}) copy-start(bf16[8,32,1024]{2,1,0:T(8,128)(2,1)S(1)} %all-to-all-done) | copy-start | bytes 1572868
  77.4 14.6 %all-to-all-start.2 = ((f32[16,8,256]{2,1,0:T(8,128)}), f32[16,8,256]{2,1,0:T(8,128)S(1)}, u32[]{:S(2)}, u32[]{:S(2)}) async-start(f32[16,8,256]{2,1,0:T(8,128)} %fusion), calls=%async_computation.3 | async-start | bytes 262144 | tf_op jit(solution)/shard_map/all_to_all | solution.py:198
  82.7 42.9 %all-gather.5.cloned.1.call-start = ((), (), s32[]{:S(2)}) async-start(), calls=%async_computation.7 | async-start | bytes 2621440 | tf_op jit(solution)/shard_map/all_gather | solution.py:208
  92.6 11.1 %all-to-all-start.3 = ((f32[8,8,256]{2,1,0:T(8,128)}), f32[8,8,256]{2,1,0:T(8,128)S(1)}, u32[]{:S(2)}, u32[]{:S(2)}) async-start(f32[8,8,256]{2,1,0:T(8,128)} %broadcast_in_dim.63), calls=%async_computation.4 | async-start | bytes 131072 | tf_op jit(solution)/shard_map/all_to_all | solution.py:140
  103.7 52.4 %all-to-all-start.5 = ((f32[32,32,512]{2,1,0:T(8,128)}), f32[32,32,512]{2,1,0:T(8,128)S(1)}, u32[]{:S(2)}, u32[]{:S(2)}) async-start(f32[32,32,512]{2,1,0:T(8,128)} %bitcast.14), calls=%async_computation.6 | async-start | bytes 4194304 | tf_op jit(solution)/shard_map/all_to_all | solution.py:220
  107.7 84.3 %reduce-scatter.2.cloned.1.call-start = ((), (), s32[]{:S(2)}) async-start(), calls=%async_computation.8 | async-start | bytes 1114112 | tf_op jit(solution)/shard_map/reduce_scatter | solution.py:210
  125.7 1.8 copy-start.6
  157.6 34.4 %copy-start.4 = (f32[256,64]{0,1:T(8,128)S(1)}, f32[256,64]{0,1:T(8,128)}, u32[]{:S(2)}) copy-start(f32[256,64]{0,1:T(8,128)} %param.4) | copy-start | bytes 196612
  157.6 54.3 %all-to-all-start.4 = ((f32[32,64,256]{2,1,0:T(8,128)}), f32[32,64,256]{2,1,0:T(8,128)}, u32[]{:S(2)}, u32[]{:S(2)}) async-start(f32[32,64,256]{2,1,0:T(8,128)} %broadcast_in_dim.65), calls=%async_computation.5 | async-start | bytes 4194304 | tf_op jit(solution)/shard_map/all_to_all | solution.py:140
  164.6 29.1 %copy-start.5 = (f32[32,512]{1,0:T(8,128)S(1)}, f32[32,512]{1,0:T(8,128)}, u32[]{:S(2)}) copy-start(f32[32,512]{1,0:T(8,128)} %param.7) | copy-start | bytes 196612
  164.7 164.7 %all-gather.7.cloned.1.call-start = ((), (), s32[]{:S(2)}) async-start(), calls=%async_computation.9 | async-start | bytes 1114112 | tf_op jit(solution)/shard_map/all_gather | solution.py:216
  193.5 138.4 %all-gather.11.cloned.1.call-start = ((), (), s32[]{:S(2)}) async-start(), calls=%async_computation.11 | async-start | bytes 2162688 | tf_op jit(solution)/shard_map/all_gather | solution.py:221
  211.9 9.9 %collective-permute-start = (f32[32,64,256]{2,1,0:T(8,128)}, f32[32,64,256]{2,1,0:T(8,128)}, u32[]{:S(2)}, u32[]{:S(2)}) collective-permute-start(f32[32,64,256]{2,1,0:T(8,128)} %all-to-all-done.4), channel_id=1, source_target_pairs={{0,1},{1,0},{2,3},{3,2},{4,5},{5,4},{6,7},{7,6},{8,9},{9,8},{10,11... | collective-permute-start | bytes 6291464 | tf_op jit(solution)/shard_map/ppermute | solution.py:201
  273.5 2.2 copy-start.2
  329.2 6.3 %copy-start.1 = (bf16[512,512]{1,0:T(8,128)(2,1)S(1)}, bf16[512,512]{1,0:T(8,128)(2,1)}, u32[]{:S(2)}) copy-start(bf16[512,512]{1,0:T(8,128)(2,1)} %param.6) | copy-start | bytes 1572868
Sparse Core Ops, SparseCore 0:
  21.5 56.2 all-gather.8
  85.7 39.9 all-gather.4
  129.4 62.5 reduce-scatter.1
  194.8 43.3 all-gather.6
  241.7 77.3 all-gather.10

commit v2 on v1

--- a/solution.py
+++ b/solution.py
@@ -63,17 +63,28 @@
     return lax.dot_general(a, b, (((0,), (0,)), ((), ())), precision=HI, preferred_element_type=jnp.float32)
 
 
-def kernel(a_ref, w_ref, s_ref, m_ref):
-    n = a_ref.shape[0]
-    big = n // 256
-    for j in range(big):
-        w_ref[j] = a_ref[:, 256 * j:256 * j + 256]
+def mmt(a, b):
+    return lax.dot_general(a, b, (((1,), (1,)), ((), ())), precision=HI, preferred_element_type=jnp.float32)
+
+
+def factor_kernel(core_ref, mine_ref, other_ref, w_ref, s_ref, m_ref):
+    big = w_ref.shape[0]
+    rows, tall, half, lanes = mine_ref.shape
+    wide = rows // tall
+    core = core_ref[0]
+    for y in range(tall):
+        for z in range(y + 1):
+            for x in range(wide):
+                at = (wide * z + x) * 2 * half
+                cols = slice((y % 2) * lanes, (y % 2) * lanes + lanes)
+                w_ref[y // 2, pl.ds(pl.multiple_of(at + core * half, half), half), cols] = mine_ref[wide * y + x, z]
+                w_ref[y // 2, pl.ds(pl.multiple_of(at + (1 - core) * half, half), half), cols] = other_ref[wide * y + x, z]
 
     def step(b, carry):
         top = pl.multiple_of(b * 256, 256)
         mid = pl.multiple_of(b * 256 + 128, 128)
 
-        def half(h, carry):
+        def half_step(h, carry):
             @pl.when(h == 0)
             def _():
                 s_ref[...] = w_ref[b, pl.ds(top, 128), 0:128]
@@ -88,26 +99,26 @@
             factor_block(s_ref)
             return carry
 
-        lax.fori_loop(0, 2, half, 0)
+        lax.fori_loop(0, 2, half_step, 0)
         lower = mtm(m_ref[0:128, 128:256], m_ref[0:128, 0:128])
         m_ref[128:256, 0:128] = -mm(s_ref[...], lower)
         m_ref[0:128, 128:256] = jnp.zeros((128, 128), jnp.float32)
         m_ref[128:256, 128:256] = s_ref[...]
-        inv = m_ref[...]
-
-        for j in range(big):
-            w_ref[j, pl.ds(top, 256), :] = mm(inv, w_ref[j, pl.ds(top, 256), :])
-        w_ref[b, pl.ds(top, 256), :] = inv
+        w_ref[b, pl.ds(top, 256), :] = m_ref[...]
+
+        for j in range(1, big):
+            @pl.when(j > b)
+            def _():
+                w_ref[j, pl.ds(top, 256), :] = mm(m_ref[...], w_ref[j, pl.ds(top, 256), :])
 
         def below(i, carry):
             at = pl.multiple_of(i * 256, 256)
-            w_ref[b, pl.ds(at, 256), :] = jnp.zeros((256, 256), jnp.float32)
-            lt = w_ref[i, pl.ds(top, 256), :]
-            for j in range(big):
-                @pl.when((j <= b) | (j >= i))
+            for j in range(1, big):
+                @pl.when(j >= i)
                 def _():
-                    w_ref[j, pl.ds(at, 256), :] = w_ref[j, pl.ds(at, 256), :] - mtm(lt, w_ref[j, pl.ds(top, 256), :])
-            w_ref[i, pl.ds(top, 256), :] = jnp.zeros((256, 256), jnp.float32)
+                    w_ref[j, pl.ds(at, 256), :] = w_ref[j, pl.ds(at, 256), :] - mtm(
+                        w_ref[i, pl.ds(top, 256), :], w_ref[j, pl.ds(top, 256), :]
+                    )
             return carry
 
         lax.fori_loop(b + 1, big, below, 0)
@@ -116,16 +127,44 @@
     lax.fori_loop(0, big, step, 0)
 
 
-def invert(diagonal):
-    n = diagonal.shape[0]
+def solve_kernel(w_ref, u_ref, v_ref, out_u_ref, out_v_ref, x_ref):
+    big = w_ref.shape[0]
+    n = u_ref.shape[0]
+    x_ref[0:n, :] = u_ref[...]
+    x_ref[n:, :] = v_ref[...]
+    for b in range(big):
+        span = slice(256 * b, 256 * b + 256)
+        y = mmt(x_ref[:, span], w_ref[b, span, :])
+        out_u_ref[:, span] = y[0:n, :]
+        out_v_ref[:, span] = y[n:, :]
+        for j in range(b + 1, big):
+            right = slice(256 * j, 256 * j + 256)
+            x_ref[:, right] = x_ref[:, right] - mm(y, w_ref[j, span, :])
+
+
+def factor(core, mine, other, panel):
+    vmem = pl.BlockSpec(memory_space=pltpu.VMEM)
     return pl.pallas_call(
-        kernel,
-        out_shape=jax.ShapeDtypeStruct((n // 256, n, 256), jnp.float32),
-        in_specs=[pl.BlockSpec(memory_space=pltpu.VMEM)],
-        out_specs=pl.BlockSpec(memory_space=pltpu.VMEM),
+        factor_kernel,
+        out_shape=jax.ShapeDtypeStruct((panel // 256, panel, 256), jnp.float32),
+        in_specs=[pl.BlockSpec(memory_space=pltpu.SMEM), vmem, vmem],
+        out_specs=vmem,
         scratch_shapes=[pltpu.VMEM((128, 128), jnp.float32), pltpu.VMEM((256, 256), jnp.float32)],
         compiler_params=pltpu.CompilerParams(vmem_limit_bytes=32 * 1024 * 1024),
-    )(diagonal)
+        cost_estimate=pl.CostEstimate(flops=50_000_000_000, transcendentals=0, bytes_accessed=8_000_000),
+    )(core, mine, other)
+
+
+def forward(w, u, v):
+    vmem = pl.BlockSpec(memory_space=pltpu.VMEM)
+    return pl.pallas_call(
+        solve_kernel,
+        out_shape=[jax.ShapeDtypeStruct(u.shape, jnp.float32), jax.ShapeDtypeStruct(v.shape, jnp.float32)],
+        in_specs=[vmem, vmem, vmem],
+        out_specs=[vmem, vmem],
+        scratch_shapes=[pltpu.VMEM((u.shape[0] + v.shape[0], u.shape[1]), jnp.float32)],
+        compiler_params=pltpu.CompilerParams(vmem_limit_bytes=32 * 1024 * 1024),
+    )(w, u, v)
 
 
 def split_three(value):
@@ -188,44 +227,43 @@
     per_x = wide // per_col
     gram_own = lax.dynamic_index_in_dim(gram_x, x_place % per_col, 1, keepdims=False)
     has_gram = (col_place % per_x) == (x_place // per_col)
-    y_at = lax.broadcasted_iota(jnp.int32, (1, tall, 1), 1)
-    placed = jnp.where(has_gram & (y_at == col_place // per_x), gram_own[:, None, :], 0.0)
-    partial = placed.reshape(wide * block_rows, tall * block_rows) - lax.dot_general(
-        rows_x, rows_y, (((1,), (1,)), ((), ())), preferred_element_type=jnp.float32
-    )
-    thin = wide * block_rows // col_count
-    partial = partial.reshape(col_count, thin, tall * block_rows)
+    y_at = lax.broadcasted_iota(jnp.int32, (tall, 1, 1), 0)
+    placed = jnp.where(has_gram & (y_at == col_place // per_x), gram_own.T[None], 0.0)
+    partial = placed.reshape(tall * block_rows, wide * block_rows) - lax.dot_general(
+        rows_y, rows_x, (((1,), (1,)), ((), ())), preferred_element_type=jnp.float32
+    )
+    thin = tall * block_rows // col_count
+    partial = partial.reshape(col_count, thin, wide * block_rows)
     own_diag = jnp.sum(lax.all_to_all(partial, "col", 0, 0), axis=0)
     diag_z = collect(own_diag, "col", chips, along_z)
-    diag_row = collect(diag_z.reshape(chips * thin, tall * block_rows), "row", row_count)
+    diag_row = collect(diag_z, "row", row_count)
     other = lax.ppermute(diag_row, "col", [(i, i ^ 1) for i in range(col_count)])
-    even = (col_place % 2) == 0
-    pair = jnp.stack([jnp.where(even, diag_row, other), jnp.where(even, other, diag_row)], axis=0)
-    pair = pair.reshape(2, tall, wide, chips, thin, tall, block_rows)
-    diagonal = pair.transpose(1, 3, 0, 4, 5, 2, 6).reshape(panel, panel)
-    inverse = invert(diagonal)
 
     chosen = lax.all_gather(rows_y, "row", axis=0, tiled=False, axis_index_groups=along_x)
     chosen = chosen.reshape(wide, tall, block_rows, depth).transpose(1, 0, 2, 3).reshape(panel, depth)
-    summed = lax.psum_scatter(
-        lax.dot_general(chosen, left_factor, (((1,), (1,)), ((), ())), preferred_element_type=jnp.float32),
+    lane = lax.broadcasted_iota(jnp.int32, (1, panel), 1)
+    gram_placed = jnp.where(lane // col_width == col_place, jnp.tile(gram_panel, (1, col_count)), 0.0)
+    update = lax.psum_scatter(
+        gram_placed
+        - lax.dot_general(left_factor, chosen, (((1,), (1,)), ((), ())), preferred_element_type=jnp.float32),
         "col",
         scatter_dimension=0,
         tiled=True,
     )
-    update = lax.all_gather(gram_panel.T - summed, "col", axis=0, tiled=True)
-
-    product = jnp.dot(strip_piece, solved_prev, preferred_element_type=jnp.float32)
-    product = product.reshape(row_count, block_rows, product.shape[1])
-    reduced = right_block - jnp.sum(lax.all_to_all(product, "row", 0, 0), axis=0)
-    reduced = lax.all_gather(reduced, "row", axis=0, tiled=True)
-
-    def rows_of_inverse(start, size):
-        part = lax.dynamic_slice_in_dim(inverse, start, size, 1)
-        return part.transpose(1, 0, 2).reshape(size, panel)
-
-    panel_factor = mm(rows_of_inverse(col_place * col_width, col_width), update).T
-    solved_panel = mm(rows_of_inverse(row_place * block_rows, block_rows), reduced)
+
+    right_placed = jnp.where(lane // block_rows == row_place, jnp.tile(right_block.T, (1, row_count)), 0.0)
+    product = right_placed - lax.dot_general(
+        solved_prev, strip_piece, (((0,), (1,)), ((), ())), preferred_element_type=jnp.float32
+    )
+    product = product.reshape(row_count, product.shape[0] // row_count, panel)
+    reduced = jnp.sum(lax.all_to_all(product, "row", 0, 0), axis=0)
+
+    factored = factor((col_place % 2).reshape(1), diag_row, other, panel)
+    rows_out, vox_out = forward(factored, update, reduced)
+    rows_out = rows_out.reshape(-1, col_count, col_width).transpose(1, 0, 2)
+    panel_factor = lax.all_to_all(rows_out, "col", 0, 0).reshape(-1, col_width)
+    vox_out = vox_out.reshape(-1, row_count, block_rows).transpose(1, 0, 2)
+    solved_panel = lax.all_to_all(vox_out, "row", 0, 0).reshape(-1, block_rows).T
     return (panel_factor, solved_panel)
 
 

time: 343 us -> 350 us (1.020)
  blocking collectives: 0 us -> 33 us
  local copies, waits for them, and re-layouts: 51.7 us -> 25.6 us
  waiting for transfers between devices: 136 us -> 160 us
  other arithmetic: 13.9 us -> 4.03 us
  starting transfers between devices: 61 us -> 53.1 us
  matrix products: 12.2 us -> 6.11 us
    all_gather x1, waiting for transfers between devices: 0.02 us -> 74.8 us  [body(): strip_piece = lax.all_gather(mine, 'col', axis=0, tiled=True)]
    all_to_all x0 -> x2, blocking collectives: none -> 33 us  [the longest x1 23.3 us: body(): own_diag = jnp.sum(lax.all_to_all(partial, 'col', 0, 0), axis=0)]
    all_to_all x4 -> x3, waiting for transfers between devices: 46 us -> 19.1 us  [collect(): return lax.all_to_all(many, axis, 0, 0, axis_index_groups=groups)]
    all_gather x1, waiting for transfers between devices: 17.9 us -> 43.1 us  [body(): lax.all_gather(rows_y, 'row', axis=0, tiled=False, axis_index_groups=alon...]
    reduce_scatter x1, waiting for transfers between devices: 27.3 us -> 3.98 us  [body(): lax.psum_scatter(gram_placed - lax.dot_general(left_factor, chosen, (((1,...]
    all_to_all x2 -> x3, waiting for transfers between devices: 35.1 us -> 13.5 us  [the longest x1 6.74 us: body(): panel_factor = lax.all_to_all(rows_out, 'col', 0, 0).reshape(-1, col_width)]
    all_to_all x4 -> x3, starting transfers between devices: 37.5 us -> 16.1 us  [collect(): return lax.all_to_all(many, axis, 0, 0, axis_index_groups=groups)]
    reshape x3 -> x4, local copies, waits for them, and re-layouts: 18.4 us -> 0.43 us  [the longest x2 0.27 us: body(): vox_out = vox_out.reshape(-1, row_count, block_rows).transpose(1, 0, 2)]
  transfers between devices with their start and end apart: 14 -> 12, of which waited for: 10 -> 9; matrix products, arithmetic and copies ran while one was open for 21% -> 6% of each run, Pallas kernels for 16% -> 14%
where the time goes in v2:
time: 350 us; the launch traced here: 349 us
  waiting for transfers between devices  160 us (46%)
  starting transfers between devices  53.1 us (15%)
  Pallas kernels  51.3 us (15%)
  blocking collectives  33 us (9%)
  local copies, waits for them, and re-layouts  25.6 us (7%)
  between operations  15.8 us (5%)
  matrix products  6.11 us (2%)
  other arithmetic  4.03 us (1%)
    all_gather x1, waiting for transfers between devices, body(): strip_piece = lax.all_gather(mine, 'col', axis=0, tiled=True)  74.8 us
    pallas_call x1, Pallas kernels, factor(): pl.pallas_call(factor_kernel, out_shape=jax.ShapeDtypeStruct((panel // 25...  48.5 us
    all_gather x1, waiting for transfers between devices, body(): lax.all_gather(rows_y, 'row', axis=0, tiled=False, axis_index_groups=alon...  43.1 us
    all_to_all x1, blocking collectives, body(): own_diag = jnp.sum(lax.all_to_all(partial, 'col', 0, 0), axis=0)  23.3 us
    all_to_all x3, waiting for transfers between devices, collect(): return lax.all_to_all(many, axis, 0, 0, axis_index_groups=groups)  19.1 us
    all_to_all x3, starting transfers between devices, collect(): return lax.all_to_all(many, axis, 0, 0, axis_index_groups=groups)  16.1 us
    all_to_all x1, blocking collectives, collect(): return lax.all_to_all(many, axis, 0, 0, axis_index_groups=groups)  9.7 us
    all_to_all x1, starting transfers between devices, body(): reduced = jnp.sum(lax.all_to_all(product, 'row', 0, 0), axis=0)  9.52 us
  transfers between devices with their start and end apart: 12, of which 9 were waited for; matrix products, arithmetic and copies ran while one was open for 6% of the time, Pallas kernels for 14%

profile of v2, /device:TPU:1, one launch (start us, length us, event | category | flops | bytes accessed | tf_op | source)
XLA Modules:
  0.0 348.7 jit_solution(16196013269087854739)
XLA Ops:
  10.6 4.8 %all-to-all-start = ((bf16[4,32,1216]{2,1,0:T(8,128)(2,1)}), bf16[4,32,1216]{2,1,0:T(8,128)(2,1)S(1)}, u32[]{:S(2)}, u32[]{:S(2)}) async-start(bf16[4,32,1216]{2,1,0:T(8,128)(2,1)} %broadcast_in_dim.78), calls=%async_computation | async-start | bytes 655360 | tf_op jit(solution)/shard_map/all_to_all | solution.py:179
  15.6 5.7 %all-to-all-done = bf16[4,32,1216]{2,1,0:T(8,128)(2,1)S(1)} async-done(((bf16[4,32,1216]{2,1,0:T(8,128)(2,1)}), bf16[4,32,1216]{2,1,0:T(8,128)(2,1)S(1)}, u32[]{:S(2)}, u32[]{:S(2)}) %all-to-all-start) | async-done | bytes 311328 | tf_op jit(solution)/shard_map/all_to_all | solution.py:179
  22.2 7.1 %all-to-all-start.1 = ((bf16[8,32,1024]{2,1,0:T(8,128)(2,1)}), bf16[8,32,1024]{2,1,0:T(8,128)(2,1)S(1)}, u32[]{:S(2)}, u32[]{:S(2)}) async-start(bf16[8,32,1024]{2,1,0:T(8,128)(2,1)} %broadcast_in_dim.82), calls=%async_computation.1 | async-start | bytes 1048576 | tf_op jit(solution)/shard_map/all_to_all | solution.py:179
  30.3 13.4 %all-to-all-done.1 = bf16[8,32,1024]{2,1,0:T(8,128)(2,1)S(1)} async-done(((bf16[8,32,1024]{2,1,0:T(8,128)(2,1)}), bf16[8,32,1024]{2,1,0:T(8,128)(2,1)S(1)}, u32[]{:S(2)}, u32[]{:S(2)}) %all-to-all-start.1) | async-done | bytes 524320 | tf_op jit(solution)/shard_map/all_to_all | solution.py:179
  44.2 23.3 %all_to_all.40 = f32[16,16,128]{2,1,0:T(8,128)S(1)} all-to-all(f32[16,16,128]{2,1,0:T(8,128)S(1)} %bitcast.52), channel_id=1, replica_groups=mesh['row'=32,'col'=16] {'col'}, dimensions={0} | all-to-all | bytes 262144 | tf_op jit(solution)/shard_map/all_to_all | solution.py:237
  67.5 9.7 %all_to_all.41 = f32[8,16,128]{2,1,0:T(8,128)S(1)} all-to-all(f32[8,16,128]{2,1,0:T(8,128)S(1)} %broadcast_in_dim.83), channel_id=1, replica_groups={{0,2,4,6,8,10,12,14},{1,3,5,7,9,11,13,15},{16,18,20,22,24,26,28,30},{17..., dimensions={0} | all-to-all | bytes 131072 | tf_op jit(solution)/shard_map/all_to_all | solution.py:179
  77.2 1.6 broadcast_in_dim.84
  78.8 4.1 %all-to-all-start.4 = ((f32[32,8,16,128]{3,2,1,0:T(8,128)}), f32[32,8,16,128]{3,2,1,0:T(8,128)S(1)}, u32[]{:S(2)}, u32[]{:S(2)}) async-start(f32[32,8,16,128]{3,2,1,0:T(8,128)} %broadcast_in_dim.84), calls=%async_computation.4 | async-start | bytes 4194304 | tf_op jit(solution)/shard_map/all_to_all | solution.py:179
  83.0 5.7 %collective-permute-start.1 = (bf16[32,512]{1,0:T(8,128)(2,1)S(1)}, bf16[32,512]{1,0:T(8,128)(2,1)S(1)}, u32[]{:S(2)}, u32[]{:S(2)}) collective-permute-start(bf16[32,512]{1,0:T(8,128)(2,1)S(1)} %get-tuple-element.17), channel_id=1, source_target_pairs={{0,16},{1,48},{2,80},{3,112},{4,144},{5,176},{6,208},{7,240},{8,27... | collective-permute-start | bytes 98312 | tf_op jit(solution)/shard_map/ppermute | solution.py:212
  88.7 2.2 collective-permute-start.2
  91.2 4.6 %collective-permute-done.2 = bf16[32,512]{1,0:T(8,128)(2,1)S(1)} collective-permute-done((bf16[32,512]{1,0:T(8,128)(2,1)S(1)}, bf16[32,512]{1,0:T(8,128)(2,1)S(1)}, u32[]{:S(2)}, u32[]{:S(2)}) %collective-permute-start.2) | collective-permute-done | bytes 32800 | tf_op jit(solution)/shard_map/ppermute | solution.py:212
  96.5 1.6 tile.20
  98.0 3.0 copy.38
  101.0 74.8 %all-gather.5.cloned.1.call-done = bf16[1024,512]{1,0:T(8,128)(2,1)} async-done(((bf16[64,512]{1,0:T(8,128)(2,1)}), bf16[1024,512]{1,0:T(8,128)(2,1)}) %all-gather.5.cloned.1.call-update) | async-done | bytes 1048592 | tf_op jit(solution)/shard_map/all_gather | solution.py:217
  175.8 4.0 %bitcast_subtract_fusion = f32[512,1024]{1,0:T(8,128)} fusion(f32[512,1024]{1,0:T(8,128)} %copy.38, bf16[1024,512]{1,0:T(8,128)(2,1)} %all-gather.5.cloned.1.call-done, bf16[512,512]{1,0:T(8,128)(2,1)S(1)} %copy-done, pred[1024]{0:T(1024)(128)(4,1)S(1)} %fusion.4), kind=kOutput, calls=%fused_computation | convolution fusion | flops 537919488 | bytes 5768192 | tf_op jit(solution)/shard_map/dot_general | solution.py:255
  179.8 9.5 %all-to-all-start.5 = ((f32[32,16,1024]{2,1,0:T(8,128)}), f32[32,16,1024]{2,1,0:T(8,128)}, u32[]{:S(2)}, u32[]{:S(2)}) async-start(f32[32,16,1024]{2,1,0:T(8,128)} %bitcast.40), calls=%async_computation.6 | async-start | bytes 4194304 | tf_op jit(solution)/shard_map/all_to_all | solution.py:259
  190.0 2.6 collective-permute-start
  192.6 1.1 tile.8
  193.7 2.6 copy.36
  196.3 43.1 %all-gather.3.cloned.1.call-done = bf16[4,256,1024]{2,1,0:T(8,128)(2,1)} async-done(((bf16[1,256,1024]{2,1,0:T(8,128)(2,1)}), bf16[4,256,1024]{2,1,0:T(8,128)(2,1)}) %all-gather.3.cloned.1.call-update) | async-done | bytes 2097168 | tf_op jit(solution)/shard_map/all_gather | solution.py:242
  239.5 1.9 copy.37
  241.4 1.8 convolution_subtract_fusion
  243.2 1.7 reduce_sum.19.v_ref
  245.0 48.5 %shard_map.59.w_ref = f32[4,1024,256]{2,1,0:T(8,128)S(1)} custom-call(s32[1]{0:T(128)} %bitcast.core_ref, f32[32,8,16,128]{3,2,1,0:T(8,128)S(1)} %all-to-all-done.4.mine_ref, f32[32,8,16,128]{3,2,1,0:T(8,128)} %collective-permute-done.other_ref), custom_call_target="tpu_custom_call" | custom-call | flops 49999998976 | bytes 8000000 | tf_op jit(solution)/shard_map/pallas_call | solution.py:147
  293.5 1.9 copy-done.1
  295.4 4.0 %reduce-scatter.2.cloned.1.call-done.u_ref = f32[16,1024]{1,0:T(8,128)} async-done(((f32[256,1024]{1,0:T(8,128)}), f32[16,1024]{1,0:T(8,128)}) %reduce-scatter.2.cloned.1.call-update) | async-done | bytes 65552 | tf_op jit(solution)/shard_map/reduce_scatter | solution.py:246
  299.4 2.2 copy-done.2
  302.4 2.8 shard_map.60
  306.1 7.4 %all-to-all-start.6 = ((f32[16,1,1024]{2,1,0:T(1,128)}), f32[16,1,1024]{2,1,0:T(1,128)S(1)}, u32[]{:S(2)}, u32[]{:S(2)}) async-start(f32[16,1,1024]{2,1,0:T(1,128)} %reshape.160), calls=%async_computation.7 | async-start | bytes 131072 | tf_op jit(solution)/shard_map/all_to_all | solution.py:264
  314.6 6.7 %all-to-all-done.6 = f32[16,1,1024]{2,1,0:T(1,128)S(1)} async-done(((f32[16,1,1024]{2,1,0:T(1,128)}), f32[16,1,1024]{2,1,0:T(1,128)S(1)}, u32[]{:S(2)}, u32[]{:S(2)}) %all-to-all-start.6) | async-done | bytes 65568 | tf_op jit(solution)/shard_map/all_to_all | solution.py:264
  321.4 9.4 %all-to-all-start.7 = ((f32[32,1,512]{2,1,0:T(1,128)}), f32[32,1,512]{2,1,0:T(1,128)S(1)}, u32[]{:S(2)}, u32[]{:S(2)}) async-start(f32[32,1,512]{2,1,0:T(1,128)} %reshape.162), calls=%async_computation.8 | async-start | bytes 131072 | tf_op jit(solution)/shard_map/all_to_all | solution.py:266
  332.9 6.7 %all-to-all-done.7 = f32[32,1,512]{2,1,0:T(1,128)S(1)} async-done(((f32[32,1,512]{2,1,0:T(1,128)}), f32[32,1,512]{2,1,0:T(1,128)S(1)}, u32[]{:S(2)}, u32[]{:S(2)}) %all-to-all-start.7) | async-done | bytes 65568 | tf_op jit(solution)/shard_map/all_to_all | solution.py:266
  (70 shorter events, 13.3 us)
Async XLA Ops:
  8.0 167.8 %copy-start = (bf16[512,512]{1,0:T(8,128)(2,1)S(1)}, bf16[512,512]{1,0:T(8,128)(2,1)}, u32[]{:S(2)}) copy-start(bf16[512,512]{1,0:T(8,128)(2,1)} %param.6) | copy-start | bytes 1572868
  10.6 10.7 %all-to-all-start = ((bf16[4,32,1216]{2,1,0:T(8,128)(2,1)}), bf16[4,32,1216]{2,1,0:T(8,128)(2,1)S(1)}, u32[]{:S(2)}, u32[]{:S(2)}) async-start(bf16[4,32,1216]{2,1,0:T(8,128)(2,1)} %broadcast_in_dim.78), calls=%async_computation | async-start | bytes 655360 | tf_op jit(solution)/shard_map/all_to_all | solution.py:179
  22.2 21.6 %all-to-all-start.1 = ((bf16[8,32,1024]{2,1,0:T(8,128)(2,1)}), bf16[8,32,1024]{2,1,0:T(8,128)(2,1)S(1)}, u32[]{:S(2)}, u32[]{:S(2)}) async-start(bf16[8,32,1024]{2,1,0:T(8,128)(2,1)} %broadcast_in_dim.82), calls=%async_computation.1 | async-start | bytes 1048576 | tf_op jit(solution)/shard_map/all_to_all | solution.py:179
  43.8 35.0 %copy-start.4 = (bf16[8,32,1024]{2,1,0:T(8,128)(2,1)}, bf16[8,32,1024]{2,1,0:T(8,128)(2,1)S(1)}, u32[]{:S(2)}) copy-start(bf16[8,32,1024]{2,1,0:T(8,128)(2,1)S(1)} %all-to-all-done.1) | copy-start | bytes 1572868
  78.8 17.7 %copy-start.8 = (f32[32,512]{1,0:T(8,128)S(1)}, f32[32,512]{1,0:T(8,128)}, u32[]{:S(2)}) copy-start(f32[32,512]{1,0:T(8,128)} %param.7) | copy-start | bytes 196612
  78.8 101.0 %all-to-all-start.4 = ((f32[32,8,16,128]{3,2,1,0:T(8,128)}), f32[32,8,16,128]{3,2,1,0:T(8,128)S(1)}, u32[]{:S(2)}, u32[]{:S(2)}) async-start(f32[32,8,16,128]{3,2,1,0:T(8,128)} %broadcast_in_dim.84), calls=%async_computation.4 | async-start | bytes 4194304 | tf_op jit(solution)/shard_map/all_to_all | solution.py:179
  82.9 92.8 %all-gather.5.cloned.1.call-start = ((), (), s32[]{:S(2)}) async-start(), calls=%async_computation.11 | async-start | bytes 1114112 | tf_op jit(solution)/shard_map/all_gather | solution.py:217
  83.0 8.1 %collective-permute-start.1 = (bf16[32,512]{1,0:T(8,128)(2,1)S(1)}, bf16[32,512]{1,0:T(8,128)(2,1)S(1)}, u32[]{:S(2)}, u32[]{:S(2)}) collective-permute-start(bf16[32,512]{1,0:T(8,128)(2,1)S(1)} %get-tuple-element.17), channel_id=1, source_target_pairs={{0,16},{1,48},{2,80},{3,112},{4,144},{5,176},{6,208},{7,240},{8,27... | collective-permute-start | bytes 98312 | tf_op jit(solution)/shard_map/ppermute | solution.py:212
  88.7 7.0 %collective-permute-start.2 = (bf16[32,512]{1,0:T(8,128)(2,1)S(1)}, bf16[32,512]{1,0:T(8,128)(2,1)S(1)}, u32[]{:S(2)}, u32[]{:S(2)}) collective-permute-start(bf16[32,512]{1,0:T(8,128)(2,1)S(1)} %get-tuple-element.18), channel_id=1, source_target_pairs={{0,0},{1,32},{2,64},{3,96},{4,128},{5,160},{6,192},{7,224},{8,256}... | collective-permute-start | bytes 98312 | tf_op jit(solution)/shard_map/ppermute | solution.py:212
  179.8 12.8 %copy-start.7 = (f32[256,64]{0,1:T(8,128)S(1)}, f32[256,64]{0,1:T(8,128)}, u32[]{:S(2)}) copy-start(f32[256,64]{0,1:T(8,128)} %param.4) | copy-start | bytes 196612
  179.8 63.4 %all-to-all-start.5 = ((f32[32,16,1024]{2,1,0:T(8,128)}), f32[32,16,1024]{2,1,0:T(8,128)}, u32[]{:S(2)}, u32[]{:S(2)}) async-start(f32[32,16,1024]{2,1,0:T(8,128)} %bitcast.40), calls=%async_computation.6 | async-start | bytes 4194304 | tf_op jit(solution)/shard_map/all_to_all | solution.py:259
  189.3 50.1 %all-gather.3.cloned.1.call-start = ((), (), s32[]{:S(2)}) async-start(), calls=%async_computation.9 | async-start | bytes 2621440 | tf_op jit(solution)/shard_map/all_gather | solution.py:242
  189.9 109.5 %reduce-scatter.2.cloned.1.call-start = ((), (), s32[]{:S(2)}) async-start(), calls=%async_computation.10 | async-start | bytes 1114112 | tf_op jit(solution)/shard_map/reduce_scatter | solution.py:246
  190.0 55.0 %collective-permute-start = (f32[32,8,16,128]{3,2,1,0:T(8,128)S(1)}, f32[32,8,16,128]{3,2,1,0:T(8,128)}, u32[]{:S(2)}, u32[]{:S(2)}) collective-permute-start(f32[32,8,16,128]{3,2,1,0:T(8,128)S(1)} %all-to-all-done.4.mine_ref), channel_id=1, source_target_pairs={{0,1},{1,0},{2,3},{3,2},{4,5},{5,4},{6,7},{7,6},{8,9},{9,8},{10,11... | collective-permute-start | bytes 6291464 | tf_op jit(solution)/shard_map/ppermute | solution.py:240
  239.5 1.9 copy-start.5
  239.5 2.0 copy-start.6
  293.5 1.9 copy-start.1
  299.4 2.2 copy-start.2
  301.6 0.8 copy-start.3
  306.1 15.2 %all-to-all-start.6 = ((f32[16,1,1024]{2,1,0:T(1,128)}), f32[16,1,1024]{2,1,0:T(1,128)S(1)}, u32[]{:S(2)}, u32[]{:S(2)}) async-start(f32[16,1,1024]{2,1,0:T(1,128)} %reshape.160), calls=%async_computation.7 | async-start | bytes 131072 | tf_op jit(solution)/shard_map/all_to_all | solution.py:264
  321.4 18.2 %all-to-all-start.7 = ((f32[32,1,512]{2,1,0:T(1,128)}), f32[32,1,512]{2,1,0:T(1,128)S(1)}, u32[]{:S(2)}, u32[]{:S(2)}) async-start(f32[32,1,512]{2,1,0:T(1,128)} %reshape.162), calls=%async_computation.8 | async-start | bytes 131072 | tf_op jit(solution)/shard_map/all_to_all | solution.py:266
Sparse Core Ops, SparseCore 0:
  96.6 79.1 all-gather.4
  243.3 56.0 reduce-scatter.1
Sparse Core Ops, SparseCore 1:
  191.9 47.5 all-gather.2

commit v3 on v2

--- a/solution.py
+++ b/solution.py
@@ -150,7 +150,7 @@
         in_specs=[pl.BlockSpec(memory_space=pltpu.SMEM), vmem, vmem],
         out_specs=vmem,
         scratch_shapes=[pltpu.VMEM((128, 128), jnp.float32), pltpu.VMEM((256, 256), jnp.float32)],
-        compiler_params=pltpu.CompilerParams(vmem_limit_bytes=32 * 1024 * 1024),
+        compiler_params=pltpu.CompilerParams(vmem_limit_bytes=12 * 1024 * 1024),
         cost_estimate=pl.CostEstimate(flops=50_000_000_000, transcendentals=0, bytes_accessed=8_000_000),
     )(core, mine, other)
 
@@ -163,7 +163,7 @@
         in_specs=[vmem, vmem, vmem],
         out_specs=[vmem, vmem],
         scratch_shapes=[pltpu.VMEM((u.shape[0] + v.shape[0], u.shape[1]), jnp.float32)],
-        compiler_params=pltpu.CompilerParams(vmem_limit_bytes=32 * 1024 * 1024),
+        compiler_params=pltpu.CompilerParams(vmem_limit_bytes=12 * 1024 * 1024),
     )(w, u, v)
 
 
@@ -215,11 +215,12 @@
         [jnp.where(flip, pieces[1], pieces[0]), jnp.where(flip, pieces[0], pieces[1])], axis=0
     )
     strip_piece = lax.all_gather(mine, "col", axis=0, tiled=True)
+    own_late, _ = lax.optimization_barrier((own, mine))
 
     gram_parts = split_three(gram_panel[:block_rows])
     packed = jnp.concatenate([own] + gram_parts, axis=1)
     from_x = collect(packed, "row", wide, along_x)
-    from_y = collect(own, "row", tall, along_y)
+    from_y = collect(own_late, "row", tall, along_y)
     rows_x = from_x[:, :, :depth].reshape(wide * block_rows, depth)
     rows_y = from_y.reshape(tall * block_rows, depth)
     gram_x = from_x[:, :, depth:].astype(jnp.float32).reshape(wide * block_rows, 3, per_col, block_rows)
@@ -234,31 +235,34 @@
     )
     thin = tall * block_rows // col_count
     partial = partial.reshape(col_count, thin, wide * block_rows)
-    own_diag = jnp.sum(lax.all_to_all(partial, "col", 0, 0), axis=0)
-    diag_z = collect(own_diag, "col", chips, along_z)
-    diag_row = collect(diag_z, "row", row_count)
-    other = lax.ppermute(diag_row, "col", [(i, i ^ 1) for i in range(col_count)])
-
-    chosen = lax.all_gather(rows_y, "row", axis=0, tiled=False, axis_index_groups=along_x)
-    chosen = chosen.reshape(wide, tall, block_rows, depth).transpose(1, 0, 2, 3).reshape(panel, depth)
     lane = lax.broadcasted_iota(jnp.int32, (1, panel), 1)
-    gram_placed = jnp.where(lane // col_width == col_place, jnp.tile(gram_panel, (1, col_count)), 0.0)
-    update = lax.psum_scatter(
-        gram_placed
-        - lax.dot_general(left_factor, chosen, (((1,), (1,)), ((), ())), preferred_element_type=jnp.float32),
-        "col",
-        scatter_dimension=0,
-        tiled=True,
-    )
-
     right_placed = jnp.where(lane // block_rows == row_place, jnp.tile(right_block.T, (1, row_count)), 0.0)
     product = right_placed - lax.dot_general(
         solved_prev, strip_piece, (((0,), (1,)), ((), ())), preferred_element_type=jnp.float32
     )
     product = product.reshape(row_count, product.shape[0] // row_count, panel)
-    reduced = jnp.sum(lax.all_to_all(product, "row", 0, 0), axis=0)
-
+
+    own_diag = jnp.sum(lax.all_to_all(partial, "col", 0, 0), axis=0)
+    diag_z = collect(own_diag, "col", chips, along_z)
+    diag_z, product = lax.optimization_barrier((diag_z, product))
+    diag_row = collect(diag_z, "row", row_count)
+    other = lax.ppermute(diag_row, "col", [(i, i ^ 1) for i in range(col_count)])
+
+    chosen = lax.all_gather(rows_y, "row", axis=0, tiled=False, axis_index_groups=along_x)
+    chosen = chosen.reshape(wide, tall, block_rows, depth).transpose(1, 0, 2, 3).reshape(panel, depth)
+    gram_placed = jnp.where(lane // col_width == col_place, jnp.tile(gram_panel, (1, col_count)), 0.0)
+    update_part = gram_placed - lax.dot_general(
+        left_factor, chosen, (((1,), (1,)), ((), ())), preferred_element_type=jnp.float32
+    )
+    update = lax.psum_scatter(update_part, "col", scatter_dimension=0, tiled=True)
+
+    product, _ = lax.optimization_barrier((product, diag_row))
+    spread_out = lax.all_to_all(product, "row", 0, 0)
+
+    diag_row, other, _, _ = lax.optimization_barrier((diag_row, other, update_part, product))
     factored = factor((col_place % 2).reshape(1), diag_row, other, panel)
+    factored, spread_out, update = lax.optimization_barrier((factored, spread_out, update))
+    reduced = jnp.sum(spread_out, axis=0)
     rows_out, vox_out = forward(factored, update, reduced)
     rows_out = rows_out.reshape(-1, col_count, col_width).transpose(1, 0, 2)
     panel_factor = lax.all_to_all(rows_out, "col", 0, 0).reshape(-1, col_width)

time: 350 us -> 275 us (0.79)
  waiting for transfers between devices: 160 us -> 100 us
  blocking collectives: 33 us -> 0 us
  starting transfers between devices: 53.1 us -> 71.6 us
    all_gather x1, waiting for transfers between devices: 74.8 us -> 0.02 us  [body(): strip_piece = lax.all_gather(mine, 'col', axis=0, tiled=True)]
    all_to_all x3 -> x4, waiting for transfers between devices: 19.1 us -> 76.2 us  [collect(): return lax.all_to_all(many, axis, 0, 0, axis_index_groups=groups)]
    all_gather x1, waiting for transfers between devices: 43.1 us -> 0.01 us  [body(): lax.all_gather(rows_y, 'row', axis=0, tiled=False, axis_index_groups=alon...]
    all_to_all x2 -> x0, blocking collectives: 33 us -> none  [the longest x1 23.3 us: body(): own_diag = jnp.sum(lax.all_to_all(partial, 'col', 0, 0), axis=0)]
    all_to_all x3 -> x4, starting transfers between devices: 16.1 us -> 34.6 us  [collect(): return lax.all_to_all(many, axis, 0, 0, axis_index_groups=groups)]
    all_to_all x1 -> x2, waiting for transfers between devices: 0.01 us -> 5.61 us  [the longest x1 5.61 us: body(): own_diag = jnp.sum(lax.all_to_all(partial, 'col', 0, 0), axis=0)]
    reduce_scatter x1, waiting for transfers between devices: 3.98 us -> 0.01 us  [body(): lax.psum_scatter(update_part, 'col', scatter_dimension=0, tiled=True)]
    all_to_all x1, starting transfers between devices: 7.43 us -> 3.61 us  [body(): panel_factor = lax.all_to_all(rows_out, 'col', 0, 0).reshape(-1, col_width)]
  transfers between devices with their start and end apart: 12 -> 14, of which waited for: 9 -> 8; matrix products, arithmetic and copies ran while one was open for 6% -> 8% of each run, Pallas kernels for 14% -> 18%
where the time goes in v3:
time: 275 us; the launch traced here: 274 us
  waiting for transfers between devices  100 us (36%)
  starting transfers between devices  71.6 us (26%)
  Pallas kernels  51.3 us (19%)
  local copies, waits for them, and re-layouts  24.1 us (9%)
  between operations  15.9 us (6%)
  matrix products  6.1 us (2%)
  other arithmetic  4.17 us (2%)
    all_to_all x4, waiting for transfers between devices, collect(): return lax.all_to_all(many, axis, 0, 0, axis_index_groups=groups)  76.2 us
    pallas_call x1, Pallas kernels, factor(): pl.pallas_call(factor_kernel, out_shape=jax.ShapeDtypeStruct((panel // 25...  48.6 us
    all_to_all x4, starting transfers between devices, collect(): return lax.all_to_all(many, axis, 0, 0, axis_index_groups=groups)  34.6 us
    all_to_all x1, starting transfers between devices, body(): lax.all_to_all(vox_out, 'row', 0, 0).reshape(-1, block_rows)  9.32 us
    ppermute x2, starting transfers between devices, body(): pieces.append(lax.ppermute(sent, both, pairs))  7.96 us
    unnamed x28, local copies, waits for them, and re-layouts  7.67 us
    all_to_all x1, waiting for transfers between devices, body(): panel_factor = lax.all_to_all(rows_out, 'col', 0, 0).reshape(-1, col_width)  6.74 us
    all_to_all x1, waiting for transfers between devices, body(): lax.all_to_all(vox_out, 'row', 0, 0).reshape(-1, block_rows)  6.73 us
  transfers between devices with their start and end apart: 14, of which 8 were waited for; matrix products, arithmetic and copies ran while one was open for 8% of the time, Pallas kernels for 18%

profile of v3, /device:TPU:1, one launch (start us, length us, event | category | flops | bytes accessed | tf_op | source)
XLA Modules:
  0.0 273.7 jit_solution(11777000446892806673)
XLA Ops:
  9.0 5.8 %collective-permute-start = (bf16[32,512]{1,0:T(8,128)(2,1)S(1)}, bf16[32,512]{1,0:T(8,128)(2,1)S(1)}, u32[]{:S(2)}, u32[]{:S(2)}) collective-permute-start(bf16[32,512]{1,0:T(8,128)(2,1)S(1)} %get-tuple-element.35), channel_id=1, source_target_pairs={{0,16},{1,48},{2,80},{3,112},{4,144},{5,176},{6,208},{7,240},{8,27... | collective-permute-start | bytes 98312 | tf_op jit(solution)/shard_map/ppermute | solution.py:212
  14.8 2.2 collective-permute-start.1
  17.0 4.5 %collective-permute-done.1 = bf16[32,512]{1,0:T(8,128)(2,1)S(1)} collective-permute-done((bf16[32,512]{1,0:T(8,128)(2,1)S(1)}, bf16[32,512]{1,0:T(8,128)(2,1)S(1)}, u32[]{:S(2)}, u32[]{:S(2)}) %collective-permute-start.1) | collective-permute-done | bytes 32800 | tf_op jit(solution)/shard_map/ppermute | solution.py:212
  23.9 3.5 %all-to-all-start = ((bf16[4,32,1216]{2,1,0:T(8,128)(2,1)}), bf16[4,32,1216]{2,1,0:T(8,128)(2,1)S(1)}, u32[]{:S(2)}, u32[]{:S(2)}) async-start(bf16[4,32,1216]{2,1,0:T(8,128)(2,1)} %broadcast_in_dim.78), calls=%async_computation | async-start | bytes 655360 | tf_op jit(solution)/shard_map/all_to_all | solution.py:179
  27.6 7.1 %all-to-all-done = bf16[4,32,1216]{2,1,0:T(8,128)(2,1)S(1)} async-done(((bf16[4,32,1216]{2,1,0:T(8,128)(2,1)}), bf16[4,32,1216]{2,1,0:T(8,128)(2,1)S(1)}, u32[]{:S(2)}, u32[]{:S(2)}) %all-to-all-start) | async-done | bytes 311328 | tf_op jit(solution)/shard_map/all_to_all | solution.py:179
  35.5 23.6 %all-to-all-start.1 = ((bf16[8,32,1024]{2,1,0:T(8,128)(2,1)}), bf16[8,32,1024]{2,1,0:T(8,128)(2,1)S(1)}, u32[]{:S(2)}, u32[]{:S(2)}) async-start(bf16[8,32,1024]{2,1,0:T(8,128)(2,1)} %broadcast_in_dim.82), calls=%async_computation.1 | async-start | bytes 1048576 | tf_op jit(solution)/shard_map/all_to_all | solution.py:179
  60.2 17.0 %all-to-all-done.1 = bf16[8,32,1024]{2,1,0:T(8,128)(2,1)S(1)} async-done(((bf16[8,32,1024]{2,1,0:T(8,128)(2,1)}), bf16[8,32,1024]{2,1,0:T(8,128)(2,1)S(1)}, u32[]{:S(2)}, u32[]{:S(2)}) %all-to-all-start.1) | async-done | bytes 524320 | tf_op jit(solution)/shard_map/all_to_all | solution.py:179
  78.2 5.4 %all-to-all-start.2 = ((f32[16,16,128]{2,1,0:T(8,128)}), f32[16,16,128]{2,1,0:T(8,128)S(1)}, u32[]{:S(2)}, u32[]{:S(2)}) async-start(f32[16,16,128]{2,1,0:T(8,128)} %bitcast.6), calls=%async_computation.2 | async-start | bytes 262144 | tf_op jit(solution)/shard_map/all_to_all | solution.py:245
  83.6 1.6 tile.8
  85.2 1.9 copy.34
  87.1 5.6 %all-to-all-done.2 = f32[16,16,128]{2,1,0:T(8,128)S(1)} async-done(((f32[16,16,128]{2,1,0:T(8,128)}), f32[16,16,128]{2,1,0:T(8,128)S(1)}, u32[]{:S(2)}, u32[]{:S(2)}) %all-to-all-start.2) | async-done | bytes 131104 | tf_op jit(solution)/shard_map/all_to_all | solution.py:245
  93.4 3.4 %all-to-all-start.3 = ((f32[8,16,128]{2,1,0:T(8,128)}), f32[8,16,128]{2,1,0:T(8,128)S(1)}, u32[]{:S(2)}, u32[]{:S(2)}) async-start(f32[8,16,128]{2,1,0:T(8,128)} %broadcast_in_dim.83), calls=%async_computation.3 | async-start | bytes 131072 | tf_op jit(solution)/shard_map/all_to_all | solution.py:179
  96.8 3.3 %bitcast_subtract_fusion = f32[512,1024]{1,0:T(8,128)} fusion(f32[512,1024]{1,0:T(8,128)S(1)} %copy.34, bf16[1024,512]{1,0:T(8,128)(2,1)} %all-gather.3.cloned.1.call-done, bf16[512,512]{1,0:T(8,128)(2,1)S(1)} %copy-done, pred[1024]{0:T(1024)(128)(4,1)S(1)} %fusion.2), kind=kOutput, calls=%fused_computation | convolution fusion | flops 537919488 | bytes 5768192 | tf_op jit(solution)/shard_map/dot_general | solution.py:240
  100.1 4.4 %all-to-all-done.3 = f32[8,16,128]{2,1,0:T(8,128)S(1)} async-done(((f32[8,16,128]{2,1,0:T(8,128)}), f32[8,16,128]{2,1,0:T(8,128)S(1)}, u32[]{:S(2)}, u32[]{:S(2)}) %all-to-all-start.3) | async-done | bytes 65568 | tf_op jit(solution)/shard_map/all_to_all | solution.py:179
  104.5 1.6 broadcast_in_dim.86
  106.1 4.1 %all-to-all-start.4 = ((f32[32,8,16,128]{3,2,1,0:T(8,128)}), f32[32,8,16,128]{3,2,1,0:T(8,128)S(1)}, u32[]{:S(2)}, u32[]{:S(2)}) async-start(f32[32,8,16,128]{3,2,1,0:T(8,128)} %broadcast_in_dim.86), calls=%async_computation.4 | async-start | bytes 4194304 | tf_op jit(solution)/shard_map/all_to_all | solution.py:179
  110.9 47.7 %all-to-all-done.4.mine_ref = f32[32,8,16,128]{3,2,1,0:T(8,128)S(1)} async-done(((f32[32,8,16,128]{3,2,1,0:T(8,128)}), f32[32,8,16,128]{3,2,1,0:T(8,128)S(1)}, u32[]{:S(2)}, u32[]{:S(2)}) %all-to-all-start.4) | async-done | bytes 2097184 | tf_op jit(solution)/shard_map/all_to_all | solution.py:179
  158.6 5.3 %collective-permute-start.2 = (f32[32,8,16,128]{3,2,1,0:T(8,128)S(1)}, f32[32,8,16,128]{3,2,1,0:T(8,128)}, u32[]{:S(2)}, u32[]{:S(2)}) collective-permute-start(f32[32,8,16,128]{3,2,1,0:T(8,128)S(1)} %all-to-all-done.4.mine_ref), channel_id=1, source_target_pairs={{0,1},{1,0},{2,3},{3,2},{4,5},{5,4},{6,7},{7,6},{8,9},{9,8},{10,11... | collective-permute-start | bytes 6291464 | tf_op jit(solution)/shard_map/ppermute | solution.py:249
  163.9 1.2 tile.20
  165.1 2.5 copy.35
  167.7 1.9 copy.36
  169.7 1.8 fusion
  171.5 5.3 %all-to-all-start.5 = ((f32[32,16,1024]{2,1,0:T(8,128)}), f32[32,16,1024]{2,1,0:T(8,128)}, u32[]{:S(2)}, u32[]{:S(2)}) async-start(f32[32,16,1024]{2,1,0:T(8,128)} %bitcast.42), calls=%async_computation.5 | async-start | bytes 4194304 | tf_op jit(solution)/shard_map/all_to_all | solution.py:260
  176.8 48.6 %shard_map.59.w_ref = f32[4,1024,256]{2,1,0:T(8,128)S(1)} custom-call(s32[1]{0:T(128)} %bitcast.core_ref, f32[32,8,16,128]{3,2,1,0:T(8,128)S(1)} %all-to-all-done.4.mine_ref, f32[32,8,16,128]{3,2,1,0:T(8,128)} %collective-permute-done.2.other_ref), custom_call_target="tpu_custom_call" | custom-call | flops 49999998976 | bytes 8000000 | tf_op jit(solution)/shard_map/pallas_call | solution.py:147
  225.4 1.9 copy-done.1
  227.3 1.7 reduce_sum.19.v_ref
  229.1 2.2 copy-done.2
  231.3 2.8 %shard_map.60 = (f32[16,1024]{1,0:T(8,128)S(1)}, f32[16,1024]{1,0:T(8,128)S(1)}) custom-call(f32[4,1024,256]{2,1,0:T(8,128)S(1)} %copy-done.2, f32[16,1024]{1,0:T(8,128)S(1)} %copy-done.3, f32[16,1024]{1,0:T(8,128)S(1)} %reduce_sum.19.v_ref), custom_call_target="tpu_custom_call" | custom-call | tf_op jit(solution)/shard_map/pallas_call | solution.py:160
  235.0 3.6 %all-to-all-start.6 = ((f32[16,1,1024]{2,1,0:T(1,128)}), f32[16,1,1024]{2,1,0:T(1,128)S(1)}, u32[]{:S(2)}, u32[]{:S(2)}) async-start(f32[16,1,1024]{2,1,0:T(1,128)} %reshape.160), calls=%async_computation.7 | async-start | bytes 131072 | tf_op jit(solution)/shard_map/all_to_all | solution.py:268
  239.6 6.7 %all-to-all-done.6 = f32[16,1,1024]{2,1,0:T(1,128)S(1)} async-done(((f32[16,1,1024]{2,1,0:T(1,128)}), f32[16,1,1024]{2,1,0:T(1,128)S(1)}, u32[]{:S(2)}, u32[]{:S(2)}) %all-to-all-start.6) | async-done | bytes 65568 | tf_op jit(solution)/shard_map/all_to_all | solution.py:268
  246.4 9.3 %all-to-all-start.7 = ((f32[32,1,512]{2,1,0:T(1,128)}), f32[32,1,512]{2,1,0:T(1,128)S(1)}, u32[]{:S(2)}, u32[]{:S(2)}) async-start(f32[32,1,512]{2,1,0:T(1,128)} %reshape.162), calls=%async_computation.8 | async-start | bytes 131072 | tf_op jit(solution)/shard_map/all_to_all | solution.py:270
  257.8 6.7 %all-to-all-done.7 = f32[32,1,512]{2,1,0:T(1,128)S(1)} async-done(((f32[32,1,512]{2,1,0:T(1,128)}), f32[32,1,512]{2,1,0:T(1,128)S(1)}, u32[]{:S(2)}, u32[]{:S(2)}) %all-to-all-start.7) | async-done | bytes 65568 | tf_op jit(solution)/shard_map/all_to_all | solution.py:270
  (70 shorter events, 13.4 us)
Async XLA Ops:
  8.0 88.8 %copy-start = (bf16[512,512]{1,0:T(8,128)(2,1)S(1)}, bf16[512,512]{1,0:T(8,128)(2,1)}, u32[]{:S(2)}) copy-start(bf16[512,512]{1,0:T(8,128)(2,1)} %param.6) | copy-start | bytes 1572868
  8.0 88.8 %all-gather.3.cloned.1.call-start = ((), (), s32[]{:S(2)}) async-start(), calls=%async_computation.9 | async-start | bytes 1114112 | tf_op jit(solution)/shard_map/all_gather | solution.py:217
  9.0 8.0 %collective-permute-start = (bf16[32,512]{1,0:T(8,128)(2,1)S(1)}, bf16[32,512]{1,0:T(8,128)(2,1)S(1)}, u32[]{:S(2)}, u32[]{:S(2)}) collective-permute-start(bf16[32,512]{1,0:T(8,128)(2,1)S(1)} %get-tuple-element.35), channel_id=1, source_target_pairs={{0,16},{1,48},{2,80},{3,112},{4,144},{5,176},{6,208},{7,240},{8,27... | collective-permute-start | bytes 98312 | tf_op jit(solution)/shard_map/ppermute | solution.py:212
  14.8 6.7 %collective-permute-start.1 = (bf16[32,512]{1,0:T(8,128)(2,1)S(1)}, bf16[32,512]{1,0:T(8,128)(2,1)S(1)}, u32[]{:S(2)}, u32[]{:S(2)}) collective-permute-start(bf16[32,512]{1,0:T(8,128)(2,1)S(1)} %get-tuple-element.36), channel_id=1, source_target_pairs={{0,0},{1,32},{2,64},{3,96},{4,128},{5,160},{6,192},{7,224},{8,256}... | collective-permute-start | bytes 98312 | tf_op jit(solution)/shard_map/ppermute | solution.py:212
  23.9 10.8 %all-to-all-start = ((bf16[4,32,1216]{2,1,0:T(8,128)(2,1)}), bf16[4,32,1216]{2,1,0:T(8,128)(2,1)S(1)}, u32[]{:S(2)}, u32[]{:S(2)}) async-start(bf16[4,32,1216]{2,1,0:T(8,128)(2,1)} %broadcast_in_dim.78), calls=%async_computation | async-start | bytes 655360 | tf_op jit(solution)/shard_map/all_to_all | solution.py:179
  35.5 41.7 %all-to-all-start.1 = ((bf16[8,32,1024]{2,1,0:T(8,128)(2,1)}), bf16[8,32,1024]{2,1,0:T(8,128)(2,1)S(1)}, u32[]{:S(2)}, u32[]{:S(2)}) async-start(bf16[8,32,1024]{2,1,0:T(8,128)(2,1)} %broadcast_in_dim.82), calls=%async_computation.1 | async-start | bytes 1048576 | tf_op jit(solution)/shard_map/all_to_all | solution.py:179
  59.2 24.4 %copy-start.8 = (f32[32,512]{1,0:T(8,128)S(1)}, f32[32,512]{1,0:T(8,128)}, u32[]{:S(2)}) copy-start(f32[32,512]{1,0:T(8,128)} %param.7) | copy-start | bytes 196612
  77.2 9.9 %copy-start.5 = (bf16[8,32,1024]{2,1,0:T(8,128)(2,1)}, bf16[8,32,1024]{2,1,0:T(8,128)(2,1)S(1)}, u32[]{:S(2)}) copy-start(bf16[8,32,1024]{2,1,0:T(8,128)(2,1)S(1)} %all-to-all-done.1) | copy-start | bytes 1572868
  78.2 14.6 %all-to-all-start.2 = ((f32[16,16,128]{2,1,0:T(8,128)}), f32[16,16,128]{2,1,0:T(8,128)S(1)}, u32[]{:S(2)}, u32[]{:S(2)}) async-start(f32[16,16,128]{2,1,0:T(8,128)} %bitcast.6), calls=%async_computation.2 | async-start | bytes 262144 | tf_op jit(solution)/shard_map/all_to_all | solution.py:245
  93.4 11.1 %all-to-all-start.3 = ((f32[8,16,128]{2,1,0:T(8,128)}), f32[8,16,128]{2,1,0:T(8,128)S(1)}, u32[]{:S(2)}, u32[]{:S(2)}) async-start(f32[8,16,128]{2,1,0:T(8,128)} %broadcast_in_dim.83), calls=%async_computation.3 | async-start | bytes 131072 | tf_op jit(solution)/shard_map/all_to_all | solution.py:179
  106.1 57.9 %copy-start.7 = (f32[256,64]{0,1:T(8,128)S(1)}, f32[256,64]{0,1:T(8,128)}, u32[]{:S(2)}) copy-start(f32[256,64]{0,1:T(8,128)} %param.4) | copy-start | bytes 196612
  106.1 52.5 %all-to-all-start.4 = ((f32[32,8,16,128]{3,2,1,0:T(8,128)}), f32[32,8,16,128]{3,2,1,0:T(8,128)S(1)}, u32[]{:S(2)}, u32[]{:S(2)}) async-start(f32[32,8,16,128]{3,2,1,0:T(8,128)} %broadcast_in_dim.86), calls=%async_computation.4 | async-start | bytes 4194304 | tf_op jit(solution)/shard_map/all_to_all | solution.py:179
  110.2 57.4 %all-gather.5.cloned.1.call-start = ((), (), s32[]{:S(2)}) async-start(), calls=%async_computation.10 | async-start | bytes 2621440 | tf_op jit(solution)/shard_map/all_gather | solution.py:251
  110.8 116.5 %reduce-scatter.2.cloned.1.call-start = ((), (), s32[]{:S(2)}) async-start(), calls=%async_computation.11 | async-start | bytes 1114112 | tf_op jit(solution)/shard_map/reduce_scatter | solution.py:257
  158.6 18.2 %collective-permute-start.2 = (f32[32,8,16,128]{3,2,1,0:T(8,128)S(1)}, f32[32,8,16,128]{3,2,1,0:T(8,128)}, u32[]{:S(2)}, u32[]{:S(2)}) collective-permute-start(f32[32,8,16,128]{3,2,1,0:T(8,128)S(1)} %all-to-all-done.4.mine_ref), channel_id=1, source_target_pairs={{0,1},{1,0},{2,3},{3,2},{4,5},{5,4},{6,7},{7,6},{8,9},{9,8},{10,11... | collective-permute-start | bytes 6291464 | tf_op jit(solution)/shard_map/ppermute | solution.py:249
  167.7 1.9 copy-start.4
  167.7 2.0 copy-start.6
  171.5 55.8 %all-to-all-start.5 = ((f32[32,16,1024]{2,1,0:T(8,128)}), f32[32,16,1024]{2,1,0:T(8,128)}, u32[]{:S(2)}, u32[]{:S(2)}) async-start(f32[32,16,1024]{2,1,0:T(8,128)} %bitcast.42), calls=%async_computation.5 | async-start | bytes 4194304 | tf_op jit(solution)/shard_map/all_to_all | solution.py:260
  225.4 1.9 copy-start.1
  227.3 1.7 copy-start.3
  229.1 2.2 copy-start.2
  235.0 11.4 %all-to-all-start.6 = ((f32[16,1,1024]{2,1,0:T(1,128)}), f32[16,1,1024]{2,1,0:T(1,128)S(1)}, u32[]{:S(2)}, u32[]{:S(2)}) async-start(f32[16,1,1024]{2,1,0:T(1,128)} %reshape.160), calls=%async_computation.7 | async-start | bytes 131072 | tf_op jit(solution)/shard_map/all_to_all | solution.py:268
  246.4 18.2 %all-to-all-start.7 = ((f32[32,1,512]{2,1,0:T(1,128)}), f32[32,1,512]{2,1,0:T(1,128)S(1)}, u32[]{:S(2)}, u32[]{:S(2)}) async-start(f32[32,1,512]{2,1,0:T(1,128)} %reshape.162), calls=%async_computation.8 | async-start | bytes 131072 | tf_op jit(solution)/shard_map/all_to_all | solution.py:270
Sparse Core Ops, SparseCore 0:
  22.3 56.2 all-gather.2
  171.6 51.5 reduce-scatter.1
Sparse Core Ops, SparseCore 1:
  112.8 46.8 all-gather.4

commit v4 on v3

--- a/solution.py
+++ b/solution.py
@@ -68,17 +68,31 @@
 
 
 def factor_kernel(core_ref, mine_ref, other_ref, w_ref, s_ref, m_ref):
-    big = w_ref.shape[0]
-    rows, tall, half, lanes = mine_ref.shape
+    big, n, _ = w_ref.shape
+    rows, kept, half, lanes = mine_ref.shape
+    tall = n // lanes
     wide = rows // tall
     core = core_ref[0]
     for y in range(tall):
-        for z in range(y + 1):
+        for d in range(kept):
+            z = y - d
+            if z < 0 and d * 2 >= tall:
+                continue
             for x in range(wide):
-                at = (wide * z + x) * 2 * half
-                cols = slice((y % 2) * lanes, (y % 2) * lanes + lanes)
-                w_ref[y // 2, pl.ds(pl.multiple_of(at + core * half, half), half), cols] = mine_ref[wide * y + x, z]
-                w_ref[y // 2, pl.ds(pl.multiple_of(at + (1 - core) * half, half), half), cols] = other_ref[wide * y + x, z]
+                at = (wide * max(z, 0) + x) * 2 * half
+                first = pl.ds(pl.multiple_of(at + core * half, half), half)
+                second = pl.ds(pl.multiple_of(at + (1 - core) * half, half), half)
+                if z >= 0:
+                    cols = slice((y % 2) * lanes, (y % 2) * lanes + lanes)
+                    w_ref[y // 2, first, cols] = mine_ref[wide * y + x, d]
+                    w_ref[y // 2, second, cols] = other_ref[wide * y + x, d]
+                else:
+                    s_ref[first, :] = mine_ref[wide * y + x, d]
+                    s_ref[second, :] = other_ref[wide * y + x, d]
+            if z < 0:
+                z += tall
+                cols = slice((z % 2) * lanes, (z % 2) * lanes + lanes)
+                w_ref[z // 2, y * lanes:(y + 1) * lanes, cols] = s_ref[...].T
 
     def step(b, carry):
         top = pl.multiple_of(b * 256, 256)
@@ -233,8 +247,11 @@
     partial = placed.reshape(tall * block_rows, wide * block_rows) - lax.dot_general(
         rows_y, rows_x, (((1,), (1,)), ((), ())), preferred_element_type=jnp.float32
     )
+    kept = tall // 2 + 1
+    turned = partial.reshape(tall, block_rows, wide * block_rows)[::-1]
+    turned = lax.dynamic_slice_in_dim(jnp.concatenate([turned, turned], axis=0), tall - 1 - row_place // wide, tall, 0)
     thin = tall * block_rows // col_count
-    partial = partial.reshape(col_count, thin, wide * block_rows)
+    partial = turned.reshape(col_count, thin, wide * block_rows)
     lane = lax.broadcasted_iota(jnp.int32, (1, panel), 1)
     right_placed = jnp.where(lane // block_rows == row_place, jnp.tile(right_block.T, (1, row_count)), 0.0)
     product = right_placed - lax.dot_general(
@@ -242,18 +259,18 @@
     )
     product = product.reshape(row_count, product.shape[0] // row_count, panel)
 
-    own_diag = jnp.sum(lax.all_to_all(partial, "col", 0, 0), axis=0)
-    diag_z = collect(own_diag, "col", chips, along_z)
-    diag_z, product = lax.optimization_barrier((diag_z, product))
-    diag_row = collect(diag_z, "row", row_count)
-    other = lax.ppermute(diag_row, "col", [(i, i ^ 1) for i in range(col_count)])
-
-    chosen = lax.all_gather(rows_y, "row", axis=0, tiled=False, axis_index_groups=along_x)
-    chosen = chosen.reshape(wide, tall, block_rows, depth).transpose(1, 0, 2, 3).reshape(panel, depth)
+    chosen = lax.all_gather(own, "row", axis=0, tiled=True)
     gram_placed = jnp.where(lane // col_width == col_place, jnp.tile(gram_panel, (1, col_count)), 0.0)
     update_part = gram_placed - lax.dot_general(
         left_factor, chosen, (((1,), (1,)), ((), ())), preferred_element_type=jnp.float32
     )
+
+    own_diag = jnp.sum(lax.all_to_all(partial, "col", 0, 0), axis=0)
+    diag_z = collect(own_diag, "col", chips, along_z)
+    diag_z, product, update_part = lax.optimization_barrier((diag_z[:kept], product, update_part))
+    diag_row = collect(diag_z, "row", row_count)
+    other = lax.ppermute(diag_row, "col", [(i, i ^ 1) for i in range(col_count)])
+
     update = lax.psum_scatter(update_part, "col", scatter_dimension=0, tiled=True)
 
     product, _ = lax.optimization_barrier((product, diag_row))

time: 275 us -> 311 us (1.13)
  blocking collectives: 0 us -> 48.8 us
  local copies, waits for them, and re-layouts: 24.1 us -> 20.1 us
    all_gather x1, waiting for transfers between devices: 0.01 us -> 50.1 us  [body(): chosen = lax.all_gather(own, 'row', axis=0, tiled=True)]
    all_to_all x4 -> x3, waiting for transfers between devices: 76.2 us -> 26.7 us  [collect(): return lax.all_to_all(many, axis, 0, 0, axis_index_groups=groups)]
    all_to_all x0 -> x2, blocking collectives: none -> 48.8 us  [the longest x1 34.5 us: collect(): return lax.all_to_all(many, axis, 0, 0, axis_index_groups=groups)]
    all_to_all x1 -> x0, waiting for transfers between devices: 5.61 us -> none  [body(): own_diag = jnp.sum(lax.all_to_all(partial, 'col', 0, 0), axis=0)]
    all_to_all x1 -> x0, starting transfers between devices: 5.39 us -> none  [body(): own_diag = jnp.sum(lax.all_to_all(partial, 'col', 0, 0), axis=0)]
    all_to_all x1, starting transfers between devices: 3.61 us -> 8.59 us  [body(): panel_factor = lax.all_to_all(rows_out, 'col', 0, 0).reshape(-1, col_width)]
    all_to_all x4 -> x3, starting transfers between devices: 34.6 us -> 30.4 us  [collect(): return lax.all_to_all(many, axis, 0, 0, axis_index_groups=groups)]
    ppermute x1, starting transfers between devices: 5.34 us -> 8.49 us  [body(): lax.ppermute(diag_row, 'col', [(i, i ^ 1) for i in range(col_count)])]
  transfers between devices with their start and end apart: 14 -> 12, of which waited for: 8 -> 8; matrix products, arithmetic and copies ran while one was open for 8% -> 6% of each run, Pallas kernels for 18% -> 15%
where the time goes in v4:
time: 311 us; the launch traced here: 310 us
  waiting for transfers between devices  96.9 us (31%)
  starting transfers between devices  68.7 us (22%)
  Pallas kernels  49.9 us (16%)
  blocking collectives  48.8 us (16%)
  local copies, waits for them, and re-layouts  20.1 us (6%)
  between operations  14.2 us (5%)
  matrix products  7.39 us (2%)
  other arithmetic  4.2 us (1%)
    all_gather x1, waiting for transfers between devices, body(): chosen = lax.all_gather(own, 'row', axis=0, tiled=True)  50.1 us
    pallas_call x1, Pallas kernels, factor(): pl.pallas_call(factor_kernel, out_shape=jax.ShapeDtypeStruct((panel // 25...  47.1 us
    all_to_all x1, blocking collectives, collect(): return lax.all_to_all(many, axis, 0, 0, axis_index_groups=groups)  34.5 us
    all_to_all x3, starting transfers between devices, collect(): return lax.all_to_all(many, axis, 0, 0, axis_index_groups=groups)  30.4 us
    all_to_all x3, waiting for transfers between devices, collect(): return lax.all_to_all(many, axis, 0, 0, axis_index_groups=groups)  26.7 us
    all_to_all x1, blocking collectives, body(): own_diag = jnp.sum(lax.all_to_all(partial, 'col', 0, 0), axis=0)  14.3 us
    all_to_all x1, starting transfers between devices, body(): panel_factor = lax.all_to_all(rows_out, 'col', 0, 0).reshape(-1, col_width)  8.59 us
    ppermute x1, starting transfers between devices, body(): lax.ppermute(diag_row, 'col', [(i, i ^ 1) for i in range(col_count)])  8.49 us
  transfers between devices with their start and end apart: 12, of which 8 were waited for; matrix products, arithmetic and copies ran while one was open for 6% of the time, Pallas kernels for 15%

profile of v4, /device:TPU:1, one launch (start us, length us, event | category | flops | bytes accessed | tf_op | source)
XLA Modules:
  0.0 310.1 jit_solution(5746130114270967947)
XLA Ops:
  7.3 0.9 slice.24
  8.2 5.8 %collective-permute-start = (bf16[32,512]{1,0:T(8,128)(2,1)S(1)}, bf16[32,512]{1,0:T(8,128)(2,1)S(1)}, u32[]{:S(2)}, u32[]{:S(2)}) collective-permute-start(bf16[32,512]{1,0:T(8,128)(2,1)S(1)} %get-tuple-element.33), channel_id=1, source_target_pairs={{0,16},{1,48},{2,80},{3,112},{4,144},{5,176},{6,208},{7,240},{8,27... | collective-permute-start | bytes 98312 | tf_op jit(solution)/shard_map/ppermute | solution.py:226
  13.9 2.2 collective-permute-start.1
  16.1 4.5 %collective-permute-done.1 = bf16[32,512]{1,0:T(8,128)(2,1)S(1)} collective-permute-done((bf16[32,512]{1,0:T(8,128)(2,1)S(1)}, bf16[32,512]{1,0:T(8,128)(2,1)S(1)}, u32[]{:S(2)}, u32[]{:S(2)}) %collective-permute-start.1) | collective-permute-done | bytes 32800 | tf_op jit(solution)/shard_map/ppermute | solution.py:226
  22.9 0.9 concatenate.9
  24.6 3.5 %all-to-all-start = ((bf16[4,32,1216]{2,1,0:T(8,128)(2,1)}), bf16[4,32,1216]{2,1,0:T(8,128)(2,1)S(1)}, u32[]{:S(2)}, u32[]{:S(2)}) async-start(bf16[4,32,1216]{2,1,0:T(8,128)(2,1)} %broadcast_in_dim.78), calls=%async_computation | async-start | bytes 655360 | tf_op jit(solution)/shard_map/all_to_all | solution.py:193
  28.3 7.1 %all-to-all-done = bf16[4,32,1216]{2,1,0:T(8,128)(2,1)S(1)} async-done(((bf16[4,32,1216]{2,1,0:T(8,128)(2,1)}), bf16[4,32,1216]{2,1,0:T(8,128)(2,1)S(1)}, u32[]{:S(2)}, u32[]{:S(2)}) %all-to-all-start) | async-done | bytes 311328 | tf_op jit(solution)/shard_map/all_to_all | solution.py:193
  35.4 1.7 broadcast_in_dim.82
  37.1 23.6 %all-to-all-start.1 = ((bf16[8,32,1024]{2,1,0:T(8,128)(2,1)}), bf16[8,32,1024]{2,1,0:T(8,128)(2,1)S(1)}, u32[]{:S(2)}, u32[]{:S(2)}) async-start(bf16[8,32,1024]{2,1,0:T(8,128)(2,1)} %broadcast_in_dim.82), calls=%async_computation.1 | async-start | bytes 1048576 | tf_op jit(solution)/shard_map/all_to_all | solution.py:193
  61.8 17.0 %all-to-all-done.1 = bf16[8,32,1024]{2,1,0:T(8,128)(2,1)S(1)} async-done(((bf16[8,32,1024]{2,1,0:T(8,128)(2,1)}), bf16[8,32,1024]{2,1,0:T(8,128)(2,1)S(1)}, u32[]{:S(2)}, u32[]{:S(2)}) %all-to-all-start.1) | async-done | bytes 524320 | tf_op jit(solution)/shard_map/all_to_all | solution.py:193
  79.2 14.3 %all_to_all.40 = f32[16,16,128]{2,1,0:T(8,128)S(1)} all-to-all(f32[16,16,128]{2,1,0:T(8,128)S(1)} %bitcast.41), channel_id=1, replica_groups=mesh['row'=32,'col'=16] {'col'}, dimensions={0} | all-to-all | bytes 262144 | tf_op jit(solution)/shard_map/all_to_all | solution.py:268
  94.2 3.4 %all-to-all-start.3 = ((f32[8,16,128]{2,1,0:T(8,128)}), f32[8,16,128]{2,1,0:T(8,128)S(1)}, u32[]{:S(2)}, u32[]{:S(2)}) async-start(f32[8,16,128]{2,1,0:T(8,128)} %broadcast_in_dim.83), calls=%async_computation.3 | async-start | bytes 131072 | tf_op jit(solution)/shard_map/all_to_all | solution.py:193
  97.7 1.4 copy.15
  99.1 1.6 tile.8
  100.7 1.9 copy.14
  102.6 2.6 all-to-all-done.3
  105.3 3.4 %bitcast_subtract_fusion = f32[512,1024]{1,0:T(8,128)} fusion(f32[512,1024]{1,0:T(8,128)S(1)} %copy.14, bf16[1024,512]{1,0:T(8,128)(2,1)} %all-gather.3.cloned.1.call-done, bf16[512,512]{1,0:T(8,128)(2,1)S(1)} %copy-done, pred[1024]{0:T(1024)(128)(4,1)S(1)} %fusion.2), kind=kOutput, calls=%fused_computation | convolution fusion | flops 537919488 | bytes 5768192 | tf_op jit(solution)/shard_map/dot_general | solution.py:257
  108.7 50.1 %all-gather.5.cloned.1.call-done = bf16[1024,1024]{1,0:T(8,128)(2,1)} async-done(((bf16[32,1024]{1,0:T(8,128)(2,1)}), bf16[1024,1024]{1,0:T(8,128)(2,1)}) %all-gather.5.cloned.1.call-update) | async-done | bytes 2097168 | tf_op jit(solution)/shard_map/all_gather | solution.py:262
  158.8 3.7 %convolution_subtract_fusion = f32[256,1024]{1,0:T(8,128)} fusion(bf16[256,1024]{1,0:T(8,128)(2,1)S(1)} %copy-done.5, bf16[1024,1024]{1,0:T(8,128)(2,1)} %all-gather.5.cloned.1.call-done, f32[256,1024]{1,0:T(8,128)} %copy.15, pred[1024]{0:T(1024)(128)(4,1)S(1)} %fusion.4), kind=kOutput, calls=%fused_computation.1 | convolution fusion | flops 537395200 | bytes 4719616 | tf_op jit(solution)/shard_map/dot_general | solution.py:264
  162.5 34.5 %all_to_all.41.mine_ref = f32[32,5,16,128]{3,2,1,0:T(8,128)S(1)} all-to-all(f32[32,5,16,128]{3,2,1,0:T(8,128)S(1)} %broadcast_in_dim.88), channel_id=1, replica_groups=mesh['row'=32,'col'=16] {'row'}, dimensions={0} | all-to-all | bytes 2621440 | tf_op jit(solution)/shard_map/all_to_all | solution.py:193
  197.1 8.5 %collective-permute-start.2 = (f32[32,5,16,128]{3,2,1,0:T(8,128)S(1)}, f32[32,5,16,128]{3,2,1,0:T(8,128)S(1)}, u32[]{:S(2)}, u32[]{:S(2)}) collective-permute-start(f32[32,5,16,128]{3,2,1,0:T(8,128)S(1)} %all_to_all.41.mine_ref), channel_id=1, source_target_pairs={{0,1},{1,0},{2,3},{3,2},{4,5},{5,4},{6,7},{7,6},{8,9},{9,8},{10,11... | collective-permute-start | bytes 3932168 | tf_op jit(solution)/shard_map/ppermute | solution.py:272
  205.6 5.0 %all-to-all-start.5 = ((f32[32,16,1024]{2,1,0:T(8,128)}), f32[32,16,1024]{2,1,0:T(8,128)}, u32[]{:S(2)}, u32[]{:S(2)}) async-start(f32[32,16,1024]{2,1,0:T(8,128)} %bitcast.33), calls=%async_computation.5 | async-start | bytes 4194304 | tf_op jit(solution)/shard_map/all_to_all | solution.py:277
  210.6 47.1 %shard_map.59.w_ref = f32[4,1024,256]{2,1,0:T(8,128)S(1)} custom-call(s32[1]{0:T(128)} %bitcast.core_ref, f32[32,5,16,128]{3,2,1,0:T(8,128)S(1)} %all_to_all.41.mine_ref, f32[32,5,16,128]{3,2,1,0:T(8,128)S(1)} %collective-permute-done.2.other_ref), custom_call_target="tpu_custom_call" | custom-call | flops 49999998976 | bytes 8000000 | tf_op jit(solution)/shard_map/pallas_call | solution.py:161
  257.7 1.9 copy-done.1
  259.6 1.3 reduce-scatter.2.cloned.1.call-done.u_ref
  260.9 1.7 reduce_sum.19.v_ref
  262.7 2.2 copy-done.2
  264.9 2.8 shard_map.60
  268.6 8.6 %all-to-all-start.6 = ((f32[16,1,1024]{2,1,0:T(1,128)}), f32[16,1,1024]{2,1,0:T(1,128)S(1)}, u32[]{:S(2)}, u32[]{:S(2)}) async-start(f32[16,1,1024]{2,1,0:T(1,128)} %reshape.156), calls=%async_computation.7 | async-start | bytes 131072 | tf_op jit(solution)/shard_map/all_to_all | solution.py:285
  278.2 6.7 %all-to-all-done.6 = f32[16,1,1024]{2,1,0:T(1,128)S(1)} async-done(((f32[16,1,1024]{2,1,0:T(1,128)}), f32[16,1,1024]{2,1,0:T(1,128)S(1)}, u32[]{:S(2)}, u32[]{:S(2)}) %all-to-all-start.6) | async-done | bytes 65568 | tf_op jit(solution)/shard_map/all_to_all | solution.py:285
  285.0 8.1 %all-to-all-start.7 = ((f32[32,1,512]{2,1,0:T(1,128)}), f32[32,1,512]{2,1,0:T(1,128)S(1)}, u32[]{:S(2)}, u32[]{:S(2)}) async-start(f32[32,1,512]{2,1,0:T(1,128)} %reshape.158), calls=%async_computation.8 | async-start | bytes 131072 | tf_op jit(solution)/shard_map/all_to_all | solution.py:287
  295.2 6.7 %all-to-all-done.7 = f32[32,1,512]{2,1,0:T(1,128)S(1)} async-done(((f32[32,1,512]{2,1,0:T(1,128)}), f32[32,1,512]{2,1,0:T(1,128)S(1)}, u32[]{:S(2)}, u32[]{:S(2)}) %all-to-all-start.7) | async-done | bytes 65568 | tf_op jit(solution)/shard_map/all_to_all | solution.py:287
  (71 shorter events, 11.2 us)
Async XLA Ops:
  7.2 98.1 %copy-start = (bf16[512,512]{1,0:T(8,128)(2,1)S(1)}, bf16[512,512]{1,0:T(8,128)(2,1)}, u32[]{:S(2)}) copy-start(bf16[512,512]{1,0:T(8,128)(2,1)} %param.6) | copy-start | bytes 1572868
  7.2 98.1 %all-gather.3.cloned.1.call-start = ((), (), s32[]{:S(2)}) async-start(), calls=%async_computation.9 | async-start | bytes 1114112 | tf_op jit(solution)/shard_map/all_gather | solution.py:231
  8.1 13.2 %copy-start.4 = (bf16[32,1024]{1,0:T(8,128)(2,1)}, bf16[32,1024]{1,0:T(8,128)(2,1)S(1)}, u32[]{:S(2)}) copy-start(bf16[32,1024]{1,0:T(8,128)(2,1)S(1)} %slice.24) | copy-start | bytes 196612
  8.2 8.0 %collective-permute-start = (bf16[32,512]{1,0:T(8,128)(2,1)S(1)}, bf16[32,512]{1,0:T(8,128)(2,1)S(1)}, u32[]{:S(2)}, u32[]{:S(2)}) collective-permute-start(bf16[32,512]{1,0:T(8,128)(2,1)S(1)} %get-tuple-element.33), channel_id=1, source_target_pairs={{0,16},{1,48},{2,80},{3,112},{4,144},{5,176},{6,208},{7,240},{8,27... | collective-permute-start | bytes 98312 | tf_op jit(solution)/shard_map/ppermute | solution.py:226
  13.9 6.7 %collective-permute-start.1 = (bf16[32,512]{1,0:T(8,128)(2,1)S(1)}, bf16[32,512]{1,0:T(8,128)(2,1)S(1)}, u32[]{:S(2)}, u32[]{:S(2)}) collective-permute-start(bf16[32,512]{1,0:T(8,128)(2,1)S(1)} %get-tuple-element.34), channel_id=1, source_target_pairs={{0,0},{1,32},{2,64},{3,96},{4,128},{5,160},{6,192},{7,224},{8,256}... | collective-permute-start | bytes 98312 | tf_op jit(solution)/shard_map/ppermute | solution.py:226
  21.3 137.4 %all-gather.5.cloned.1.call-start = ((), (), s32[]{:S(2)}) async-start(), calls=%async_computation.10 | async-start | bytes 2162688 | tf_op jit(solution)/shard_map/all_gather | solution.py:262
  24.6 10.8 %all-to-all-start = ((bf16[4,32,1216]{2,1,0:T(8,128)(2,1)}), bf16[4,32,1216]{2,1,0:T(8,128)(2,1)S(1)}, u32[]{:S(2)}, u32[]{:S(2)}) async-start(bf16[4,32,1216]{2,1,0:T(8,128)(2,1)} %broadcast_in_dim.78), calls=%async_computation | async-start | bytes 655360 | tf_op jit(solution)/shard_map/all_to_all | solution.py:193
  37.1 41.7 %all-to-all-start.1 = ((bf16[8,32,1024]{2,1,0:T(8,128)(2,1)}), bf16[8,32,1024]{2,1,0:T(8,128)(2,1)S(1)}, u32[]{:S(2)}, u32[]{:S(2)}) async-start(bf16[8,32,1024]{2,1,0:T(8,128)(2,1)} %broadcast_in_dim.82), calls=%async_computation.1 | async-start | bytes 1048576 | tf_op jit(solution)/shard_map/all_to_all | solution.py:193
  61.0 36.5 %copy-start.7 = (f32[256,64]{0,1:T(8,128)S(1)}, f32[256,64]{0,1:T(8,128)}, u32[]{:S(2)}) copy-start(f32[256,64]{0,1:T(8,128)} %param.4) | copy-start | bytes 196612
  79.1 20.0 %copy-start.8 = (f32[32,512]{1,0:T(8,128)S(1)}, f32[32,512]{1,0:T(8,128)}, u32[]{:S(2)}) copy-start(f32[32,512]{1,0:T(8,128)} %param.7) | copy-start | bytes 196612
  94.2 11.1 %all-to-all-start.3 = ((f32[8,16,128]{2,1,0:T(8,128)}), f32[8,16,128]{2,1,0:T(8,128)S(1)}, u32[]{:S(2)}, u32[]{:S(2)}) async-start(f32[8,16,128]{2,1,0:T(8,128)} %broadcast_in_dim.83), calls=%async_computation.3 | async-start | bytes 131072 | tf_op jit(solution)/shard_map/all_to_all | solution.py:193
  97.5 163.4 %reduce-scatter.2.cloned.1.call-start = ((), (), s32[]{:S(2)}) async-start(), calls=%async_computation.11 | async-start | bytes 1114112 | tf_op jit(solution)/shard_map/reduce_scatter | solution.py:274
  105.3 3.4 %copy-start.6 = (f32[8,16,128]{2,1,0:T(8,128)}, f32[8,16,128]{2,1,0:T(8,128)S(1)}, u32[]{:S(2)}) copy-start(f32[8,16,128]{2,1,0:T(8,128)S(1)} %all-to-all-done.3) | copy-start | bytes 196612
  105.3 53.5 %copy-start.5 = (bf16[256,1024]{1,0:T(8,128)(2,1)S(1)}, bf16[256,1024]{1,0:T(8,128)(2,1)}, u32[]{:S(2)}) copy-start(bf16[256,1024]{1,0:T(8,128)(2,1)} %param.5) | copy-start | bytes 1572868
  158.8 3.7 %slice-start = ((f32[8,16,128]{2,1,0:T(8,128)}), f32[5,16,128]{2,1,0:T(8,128)S(1)}, s32[]{:S(2)}) async-start(f32[8,16,128]{2,1,0:T(8,128)} %copy-done.6), calls=%async_computation.12 | async-start | bytes 81920 | tf_op jit(solution)/shard_map/slice | solution.py:270
  197.1 13.5 %collective-permute-start.2 = (f32[32,5,16,128]{3,2,1,0:T(8,128)S(1)}, f32[32,5,16,128]{3,2,1,0:T(8,128)S(1)}, u32[]{:S(2)}, u32[]{:S(2)}) collective-permute-start(f32[32,5,16,128]{3,2,1,0:T(8,128)S(1)} %all_to_all.41.mine_ref), channel_id=1, source_target_pairs={{0,1},{1,0},{2,3},{3,2},{4,5},{5,4},{6,7},{7,6},{8,9},{9,8},{10,11... | collective-permute-start | bytes 3932168 | tf_op jit(solution)/shard_map/ppermute | solution.py:272
  205.6 55.3 %all-to-all-start.5 = ((f32[32,16,1024]{2,1,0:T(8,128)}), f32[32,16,1024]{2,1,0:T(8,128)}, u32[]{:S(2)}, u32[]{:S(2)}) async-start(f32[32,16,1024]{2,1,0:T(8,128)} %bitcast.33), calls=%async_computation.5 | async-start | bytes 4194304 | tf_op jit(solution)/shard_map/all_to_all | solution.py:277
  257.7 1.9 copy-start.1
  260.9 1.7 copy-start.3
  262.7 2.2 copy-start.2
  268.6 16.4 %all-to-all-start.6 = ((f32[16,1,1024]{2,1,0:T(1,128)}), f32[16,1,1024]{2,1,0:T(1,128)S(1)}, u32[]{:S(2)}, u32[]{:S(2)}) async-start(f32[16,1,1024]{2,1,0:T(1,128)} %reshape.156), calls=%async_computation.7 | async-start | bytes 131072 | tf_op jit(solution)/shard_map/all_to_all | solution.py:285
  285.0 16.9 %all-to-all-start.7 = ((f32[32,1,512]{2,1,0:T(1,128)}), f32[32,1,512]{2,1,0:T(1,128)S(1)}, u32[]{:S(2)}, u32[]{:S(2)}) async-start(f32[32,1,512]{2,1,0:T(1,128)} %reshape.158), calls=%async_computation.8 | async-start | bytes 131072 | tf_op jit(solution)/shard_map/all_to_all | solution.py:287
Sparse Core Ops, SparseCore 0:
  21.5 56.2 all-gather.2
  81.5 77.2 all-gather.4
  205.7 55.1 reduce-scatter.1

commit v5 on v4

--- a/solution.py
+++ b/solution.py
@@ -141,16 +141,13 @@
     lax.fori_loop(0, big, step, 0)
 
 
-def solve_kernel(w_ref, u_ref, v_ref, out_u_ref, out_v_ref, x_ref):
+def solve_kernel(w_ref, u_ref, out_ref, x_ref):
     big = w_ref.shape[0]
-    n = u_ref.shape[0]
-    x_ref[0:n, :] = u_ref[...]
-    x_ref[n:, :] = v_ref[...]
+    x_ref[...] = u_ref[...]
     for b in range(big):
         span = slice(256 * b, 256 * b + 256)
         y = mmt(x_ref[:, span], w_ref[b, span, :])
-        out_u_ref[:, span] = y[0:n, :]
-        out_v_ref[:, span] = y[n:, :]
+        out_ref[:, span] = y
         for j in range(b + 1, big):
             right = slice(256 * j, 256 * j + 256)
             x_ref[:, right] = x_ref[:, right] - mm(y, w_ref[j, span, :])
@@ -169,16 +166,16 @@
     )(core, mine, other)
 
 
-def forward(w, u, v):
+def forward(w, u):
     vmem = pl.BlockSpec(memory_space=pltpu.VMEM)
     return pl.pallas_call(
         solve_kernel,
-        out_shape=[jax.ShapeDtypeStruct(u.shape, jnp.float32), jax.ShapeDtypeStruct(v.shape, jnp.float32)],
-        in_specs=[vmem, vmem, vmem],
-        out_specs=[vmem, vmem],
-        scratch_shapes=[pltpu.VMEM((u.shape[0] + v.shape[0], u.shape[1]), jnp.float32)],
+        out_shape=jax.ShapeDtypeStruct(u.shape, jnp.float32),
+        in_specs=[vmem, vmem],
+        out_specs=vmem,
+        scratch_shapes=[pltpu.VMEM(u.shape, jnp.float32)],
         compiler_params=pltpu.CompilerParams(vmem_limit_bytes=12 * 1024 * 1024),
-    )(w, u, v)
+    )(w, u)
 
 
 def split_three(value):
@@ -212,29 +209,15 @@
     own = left_factor[:block_rows]
     per_col = row_count // col_count
     strip = depth // per_col
-
-    both = ("row", "col")
-    pieces = []
-    for turn in range(per_col):
-        half = (row_place + turn) % per_col
-        sent = lax.dynamic_slice_in_dim(own, half * strip, strip, 1)
-        pairs = []
-        for r in range(row_count):
-            for c in range(col_count):
-                to_row = per_col * c + (r + turn) % per_col
-                pairs.append((r * col_count + c, to_row * col_count + r // per_col))
-        pieces.append(lax.ppermute(sent, both, pairs))
-    flip = (row_place % per_col) == 1
-    mine = jnp.concatenate(
-        [jnp.where(flip, pieces[1], pieces[0]), jnp.where(flip, pieces[0], pieces[1])], axis=0
-    )
-    strip_piece = lax.all_gather(mine, "col", axis=0, tiled=True)
-    own_late, _ = lax.optimization_barrier((own, mine))
-
-    gram_parts = split_three(gram_panel[:block_rows])
-    packed = jnp.concatenate([own] + gram_parts, axis=1)
-    from_x = collect(packed, "row", wide, along_x)
-    from_y = collect(own_late, "row", tall, along_y)
+    lane = lax.broadcasted_iota(jnp.int32, (1, panel), 1)
+
+    packed = jnp.concatenate([own] + split_three(gram_panel[:block_rows]), axis=1)
+    near = [packed]
+    for shift in range(1, wide):
+        pairs = [(y * wide + x, y * wide + (x + shift) % wide) for y in range(tall) for x in range(wide)]
+        near.append(lax.ppermute(packed, "row", pairs))
+    from_x = jnp.stack([lax.select_n((x_place - x) % wide, *near) for x in range(wide)], axis=0)
+    from_y = collect(own, "row", tall, along_y)
     rows_x = from_x[:, :, :depth].reshape(wide * block_rows, depth)
     rows_y = from_y.reshape(tall * block_rows, depth)
     gram_x = from_x[:, :, depth:].astype(jnp.float32).reshape(wide * block_rows, 3, per_col, block_rows)
@@ -252,39 +235,57 @@
     turned = lax.dynamic_slice_in_dim(jnp.concatenate([turned, turned], axis=0), tall - 1 - row_place // wide, tall, 0)
     thin = tall * block_rows // col_count
     partial = turned.reshape(col_count, thin, wide * block_rows)
-    lane = lax.broadcasted_iota(jnp.int32, (1, panel), 1)
-    right_placed = jnp.where(lane // block_rows == row_place, jnp.tile(right_block.T, (1, row_count)), 0.0)
-    product = right_placed - lax.dot_general(
-        solved_prev, strip_piece, (((0,), (1,)), ((), ())), preferred_element_type=jnp.float32
-    )
-    product = product.reshape(row_count, product.shape[0] // row_count, panel)
-
-    chosen = lax.all_gather(own, "row", axis=0, tiled=True)
+    own_diag = jnp.sum(lax.all_to_all(partial, "col", 0, 0), axis=0)
+    diag_z = collect(own_diag, "col", chips, along_z)
+
+    pieces = []
+    for turn in range(per_col):
+        half = (row_place + turn) % per_col
+        sent = lax.dynamic_slice_in_dim(own, half * strip, strip, 1)
+        pairs = []
+        for r in range(row_count):
+            for c in range(col_count):
+                to_row = per_col * c + (r + turn) % per_col
+                pairs.append((r * col_count + c, to_row * col_count + r // per_col))
+        pieces.append(lax.ppermute(sent, ("row", "col"), pairs))
+    flip = (row_place % per_col) == 1
+    mine = jnp.concatenate(
+        [jnp.where(flip, pieces[1], pieces[0]), jnp.where(flip, pieces[0], pieces[1])], axis=0
+    )
+
+    chosen = lax.all_gather(rows_y, "row", axis=0, tiled=False, axis_index_groups=along_x)
+    chosen, mine = lax.optimization_barrier((chosen, mine))
+    chosen = chosen.reshape(wide, tall, block_rows, depth).transpose(1, 0, 2, 3).reshape(panel, depth)
     gram_placed = jnp.where(lane // col_width == col_place, jnp.tile(gram_panel, (1, col_count)), 0.0)
     update_part = gram_placed - lax.dot_general(
         left_factor, chosen, (((1,), (1,)), ((), ())), preferred_element_type=jnp.float32
     )
-
-    own_diag = jnp.sum(lax.all_to_all(partial, "col", 0, 0), axis=0)
-    diag_z = collect(own_diag, "col", chips, along_z)
-    diag_z, product, update_part = lax.optimization_barrier((diag_z[:kept], product, update_part))
+    right_placed = jnp.where(lane // block_rows == row_place, jnp.tile(right_block.T, (1, row_count)), 0.0)
+
+    diag_z, update_part, right_placed = lax.optimization_barrier((diag_z[:kept], update_part, right_placed))
     diag_row = collect(diag_z, "row", row_count)
     other = lax.ppermute(diag_row, "col", [(i, i ^ 1) for i in range(col_count)])
-
     update = lax.psum_scatter(update_part, "col", scatter_dimension=0, tiled=True)
 
+    strip_piece = lax.all_gather(mine, "col", axis=0, tiled=True)
+    product = right_placed - lax.dot_general(
+        solved_prev, strip_piece, (((0,), (1,)), ((), ())), preferred_element_type=jnp.float32
+    )
+    product = product.reshape(row_count, product.shape[0] // row_count, panel)
     product, _ = lax.optimization_barrier((product, diag_row))
     spread_out = lax.all_to_all(product, "row", 0, 0)
 
     diag_row, other, _, _ = lax.optimization_barrier((diag_row, other, update_part, product))
     factored = factor((col_place % 2).reshape(1), diag_row, other, panel)
-    factored, spread_out, update = lax.optimization_barrier((factored, spread_out, update))
-    reduced = jnp.sum(spread_out, axis=0)
-    rows_out, vox_out = forward(factored, update, reduced)
+    factored, spread_out = lax.optimization_barrier((factored, spread_out))
+    vox_out = forward(factored, jnp.sum(spread_out, axis=0))
+    update, vox_out = lax.optimization_barrier((update, vox_out))
+    rows_out = forward(factored, update)
+    vox_out = vox_out.reshape(-1, row_count, block_rows).transpose(1, 0, 2)
+    solved_panel = lax.all_to_all(vox_out, "row", 0, 0).reshape(-1, block_rows).T
+    rows_out, solved_panel = lax.optimization_barrier((rows_out, solved_panel))
     rows_out = rows_out.reshape(-1, col_count, col_width).transpose(1, 0, 2)
     panel_factor = lax.all_to_all(rows_out, "col", 0, 0).reshape(-1, col_width)
-    vox_out = vox_out.reshape(-1, row_count, block_rows).transpose(1, 0, 2)
-    solved_panel = lax.all_to_all(vox_out, "row", 0, 0).reshape(-1, block_rows).T
     return (panel_factor, solved_panel)
 
 

time: 311 us -> 269 us (0.86)
  waiting for transfers between devices: 96.9 us -> 60.8 us
  blocking collectives: 48.8 us -> 22 us
  starting transfers between devices: 68.7 us -> 78.4 us
  local copies, waits for them, and re-layouts: 20.1 us -> 25.2 us
  other arithmetic: 4.2 us -> 8.79 us
    all_gather x1, waiting for transfers between devices: 50.1 us -> 0.01 us  [body(): lax.all_gather(rows_y, 'row', axis=0, tiled=False, axis_index_groups=alon...]
    all_to_all x3 -> x2, starting transfers between devices: 30.4 us -> 7.98 us  [collect(): return lax.all_to_all(many, axis, 0, 0, axis_index_groups=groups)]
    all_to_all x0 -> x1, starting transfers between devices: none -> 20.3 us  [body(): own_diag = jnp.sum(lax.all_to_all(partial, 'col', 0, 0), axis=0)]
    all_to_all x1 -> x0, blocking collectives: 14.3 us -> none  [body(): own_diag = jnp.sum(lax.all_to_all(partial, 'col', 0, 0), axis=0)]
    all_to_all x1, blocking collectives: 34.5 us -> 22 us  [collect(): return lax.all_to_all(many, axis, 0, 0, axis_index_groups=groups)]
    ppermute x2 -> x5, starting transfers between devices: 7.96 us -> 19.9 us  [the longest x3 10.9 us: body(): near.append(lax.ppermute(packed, 'row', pairs))]
    all_to_all x3 -> x2, waiting for transfers between devices: 26.7 us -> 36.8 us  [collect(): return lax.all_to_all(many, axis, 0, 0, axis_index_groups=groups)]
    all_to_all x0 -> x1, waiting for transfers between devices: none -> 7.15 us  [body(): own_diag = jnp.sum(lax.all_to_all(partial, 'col', 0, 0), axis=0)]
  transfers between devices with their start and end apart: 12 -> 15, of which waited for: 8 -> 6; matrix products, arithmetic and copies ran while one was open for 6% -> 8% of each run, Pallas kernels for 15% -> 20%
where the time goes in v5:
time: 269 us; the launch traced here: 268 us
  starting transfers between devices  78.4 us (29%)
  waiting for transfers between devices  60.8 us (23%)
  Pallas kernels  52.5 us (20%)
  local copies, waits for them, and re-layouts  25.2 us (9%)
  blocking collectives  22 us (8%)
  between operations  14.4 us (5%)
  other arithmetic  8.79 us (3%)
  matrix products  6.14 us (2%)
    pallas_call x1, Pallas kernels, factor(): pl.pallas_call(factor_kernel, out_shape=jax.ShapeDtypeStruct((panel // 25...  47.1 us
    all_to_all x2, waiting for transfers between devices, collect(): return lax.all_to_all(many, axis, 0, 0, axis_index_groups=groups)  36.8 us
    all_to_all x1, blocking collectives, collect(): return lax.all_to_all(many, axis, 0, 0, axis_index_groups=groups)  22 us
    all_to_all x1, starting transfers between devices, body(): own_diag = jnp.sum(lax.all_to_all(partial, 'col', 0, 0), axis=0)  20.3 us
    unnamed x38, local copies, waits for them, and re-layouts  11.3 us
    ppermute x3, starting transfers between devices, body(): near.append(lax.ppermute(packed, 'row', pairs))  10.9 us
    all_to_all x1, starting transfers between devices, body(): spread_out = lax.all_to_all(product, 'row', 0, 0)  9.57 us
    ppermute x2, starting transfers between devices, body(): pieces.append(lax.ppermute(sent, ('row', 'col'), pairs))  9.07 us
  transfers between devices with their start and end apart: 15, of which 6 were waited for; matrix products, arithmetic and copies ran while one was open for 8% of the time, Pallas kernels for 20%

profile of v5, /device:TPU:1, one launch (start us, length us, event | category | flops | bytes accessed | tf_op | source)
XLA Modules:
  0.0 268.2 jit_solution(6410898204614585256)
XLA Ops:
  8.2 22.0 %all_to_all.35 = bf16[8,32,1024]{2,1,0:T(8,128)(2,1)} all-to-all(bf16[8,32,1024]{2,1,0:T(8,128)(2,1)S(1)} %broadcast_in_dim.75), channel_id=1, replica_groups={{0,64,128,192,256,320,384,448},{16,80,144,208,272,336,400,464},{32,96,1..., dimensions={0} | all-to-all | bytes 1048576 | tf_op jit(solution)/shard_map/all_to_all | solution.py:190
  30.4 5.9 %collective-permute-start.2 = (bf16[32,1216]{1,0:T(8,128)(2,1)S(1)}, bf16[32,1216]{1,0:T(8,128)(2,1)S(1)}, u32[]{:S(2)}, u32[]{:S(2)}) collective-permute-start(bf16[32,1216]{1,0:T(8,128)(2,1)S(1)} %concatenate.9), channel_id=1, source_target_pairs={{0,48},{16,0},{32,16},{48,32},{64,112},{80,64},{96,80},{112,96},{1... | collective-permute-start | bytes 233480 | tf_op jit(solution)/shard_map/ppermute | solution.py:218
  36.3 2.4 collective-permute-start.1
  38.8 2.5 collective-permute-start
  42.0 7.2 %collective-permute-start.3 = (bf16[32,512]{1,0:T(8,128)(2,1)}, bf16[32,512]{1,0:T(8,128)(2,1)}, u32[]{:S(2)}, u32[]{:S(2)}) collective-permute-start(bf16[32,512]{1,0:T(8,128)(2,1)} %get-tuple-element.45), channel_id=1, source_target_pairs={{0,16},{1,48},{2,80},{3,112},{4,144},{5,176},{6,208},{7,240},{8,27... | collective-permute-start | bytes 98312 | tf_op jit(solution)/shard_map/ppermute | solution.py:250
  49.1 1.9 collective-permute-start.4
  51.4 1.6 tile.20
  53.0 1.9 copy.42
  62.1 20.3 %all-to-all-start.1 = ((f32[16,16,128]{2,1,0:T(8,128)}), f32[16,16,128]{2,1,0:T(8,128)S(1)}, u32[]{:S(2)}, u32[]{:S(2)}) async-start(f32[16,16,128]{2,1,0:T(8,128)} %bitcast.12), calls=%async_computation.1 | async-start | bytes 262144 | tf_op jit(solution)/shard_map/all_to_all | solution.py:238
  82.4 1.6 broadcast_select_fusion
  84.4 7.1 %all-to-all-done.1 = f32[16,16,128]{2,1,0:T(8,128)S(1)} async-done(((f32[16,16,128]{2,1,0:T(8,128)}), f32[16,16,128]{2,1,0:T(8,128)S(1)}, u32[]{:S(2)}, u32[]{:S(2)}) %all-to-all-start.1) | async-done | bytes 131104 | tf_op jit(solution)/shard_map/all_to_all | solution.py:238
  92.2 3.4 %all-to-all-start.2 = ((f32[8,16,128]{2,1,0:T(8,128)}), f32[8,16,128]{2,1,0:T(8,128)S(1)}, u32[]{:S(2)}, u32[]{:S(2)}) async-start(f32[8,16,128]{2,1,0:T(8,128)} %broadcast_in_dim.76), calls=%async_computation.2 | async-start | bytes 131072 | tf_op jit(solution)/shard_map/all_to_all | solution.py:190
  97.0 6.3 %all-to-all-done.2 = f32[8,16,128]{2,1,0:T(8,128)S(1)} async-done(((f32[8,16,128]{2,1,0:T(8,128)}), f32[8,16,128]{2,1,0:T(8,128)S(1)}, u32[]{:S(2)}, u32[]{:S(2)}) %all-to-all-start.2) | async-done | bytes 65568 | tf_op jit(solution)/shard_map/all_to_all | solution.py:190
  103.3 1.8 copy.40
  105.2 1.8 fusion
  108.1 4.6 %all-to-all-start.3 = ((f32[32,5,16,128]{3,2,1,0:T(8,128)}), f32[32,5,16,128]{3,2,1,0:T(8,128)S(1)}, u32[]{:S(2)}, u32[]{:S(2)}) async-start(f32[32,5,16,128]{3,2,1,0:T(8,128)} %broadcast_in_dim.81), calls=%async_computation.3 | async-start | bytes 2621440 | tf_op jit(solution)/shard_map/all_to_all | solution.py:190
  113.6 30.5 %all-to-all-done.3.mine_ref = f32[32,5,16,128]{3,2,1,0:T(8,128)S(1)} async-done(((f32[32,5,16,128]{3,2,1,0:T(8,128)}), f32[32,5,16,128]{3,2,1,0:T(8,128)S(1)}, u32[]{:S(2)}, u32[]{:S(2)}) %all-to-all-start.3) | async-done | bytes 1310752 | tf_op jit(solution)/shard_map/all_to_all | solution.py:190
  144.1 5.1 %collective-permute-start.5 = (f32[32,5,16,128]{3,2,1,0:T(8,128)S(1)}, f32[32,5,16,128]{3,2,1,0:T(8,128)S(1)}, u32[]{:S(2)}, u32[]{:S(2)}) collective-permute-start(f32[32,5,16,128]{3,2,1,0:T(8,128)S(1)} %all-to-all-done.3.mine_ref), channel_id=1, source_target_pairs={{0,1},{1,0},{2,3},{3,2},{4,5},{5,4},{6,7},{7,6},{8,9},{9,8},{10,11... | collective-permute-start | bytes 3932168 | tf_op jit(solution)/shard_map/ppermute | solution.py:267
  149.2 6.0 %all-gather.5.cloned.1.call-done = bf16[1024,512]{1,0:T(8,128)(2,1)} async-done(((bf16[64,512]{1,0:T(8,128)(2,1)}), bf16[1024,512]{1,0:T(8,128)(2,1)}) %all-gather.5.cloned.1.call-update) | async-done | bytes 1048592 | tf_op jit(solution)/shard_map/all_gather | solution.py:270
  155.2 4.1 %bitcast_subtract_fusion = f32[512,1024]{1,0:T(8,128)} fusion(f32[512,1024]{1,0:T(8,128)} %broadcast_select_fusion, bf16[1024,512]{1,0:T(8,128)(2,1)} %all-gather.5.cloned.1.call-done, bf16[512,512]{1,0:T(8,128)(2,1)S(1)} %copy-done), kind=kOutput, calls=%fused_computation | convolution fusion | flops 537395200 | bytes 5767168 | tf_op jit(solution)/shard_map/dot_general | solution.py:271
  159.2 9.6 %all-to-all-start.4 = ((f32[32,16,1024]{2,1,0:T(8,128)}), f32[32,16,1024]{2,1,0:T(8,128)}, u32[]{:S(2)}, u32[]{:S(2)}) async-start(f32[32,16,1024]{2,1,0:T(8,128)} %bitcast.55), calls=%async_computation.4 | async-start | bytes 4194304 | tf_op jit(solution)/shard_map/all_to_all | solution.py:276
  168.8 47.1 %shard_map.59.w_ref = f32[4,1024,256]{2,1,0:T(8,128)S(1)} custom-call(s32[1]{0:T(128)} %bitcast.core_ref, f32[32,5,16,128]{3,2,1,0:T(8,128)S(1)} %all-to-all-done.3.mine_ref, f32[32,5,16,128]{3,2,1,0:T(8,128)S(1)} %collective-permute-done.5.other_ref), custom_call_target="tpu_custom_call" | custom-call | flops 49999998976 | bytes 8000000 | tf_op jit(solution)/shard_map/pallas_call | solution.py:158
  215.9 2.0 copy-done.1
  217.9 1.7 reduce_sum.19.u_ref
  219.6 2.2 copy-done.2
  221.8 2.7 %shard_map.60 = f32[16,1024]{1,0:T(8,128)S(1)} custom-call(f32[4,1024,256]{2,1,0:T(8,128)S(1)} %copy-done.2, f32[16,1024]{1,0:T(8,128)S(1)} %reduce_sum.19.u_ref), custom_call_target="tpu_custom_call" | custom-call | tf_op jit(solution)/shard_map/pallas_call | solution.py:171
  225.6 9.0 %all-to-all-start.5 = ((f32[32,1,512]{2,1,0:T(1,128)}), f32[32,1,512]{2,1,0:T(1,128)S(1)}, u32[]{:S(2)}, u32[]{:S(2)}) async-start(f32[32,1,512]{2,1,0:T(1,128)} %reshape.163), calls=%async_computation.6 | async-start | bytes 131072 | tf_op jit(solution)/shard_map/all_to_all | solution.py:285
  234.6 2.2 copy-done.3
  237.6 2.7 %shard_map.61 = f32[16,1024]{1,0:T(8,128)S(1)} custom-call(f32[4,1024,256]{2,1,0:T(8,128)S(1)} %copy-done.3, f32[16,1024]{1,0:T(8,128)S(1)} %copy-done.4), custom_call_target="tpu_custom_call" | custom-call | tf_op jit(solution)/shard_map/pallas_call | solution.py:171
  240.3 3.1 %all-to-all-done.5 = f32[32,1,512]{2,1,0:T(1,128)S(1)} async-done(((f32[32,1,512]{2,1,0:T(1,128)}), f32[32,1,512]{2,1,0:T(1,128)S(1)}, u32[]{:S(2)}, u32[]{:S(2)}) %all-to-all-start.5) | async-done | bytes 65568 | tf_op jit(solution)/shard_map/all_to_all | solution.py:285
  245.8 6.4 %all-to-all-start.6 = ((f32[16,1,1024]{2,1,0:T(1,128)}), f32[16,1,1024]{2,1,0:T(1,128)S(1)}, u32[]{:S(2)}, u32[]{:S(2)}) async-start(f32[16,1,1024]{2,1,0:T(1,128)} %reshape.165), calls=%async_computation.7 | async-start | bytes 131072 | tf_op jit(solution)/shard_map/all_to_all | solution.py:288
  252.9 7.1 %all-to-all-done.6 = f32[16,1,1024]{2,1,0:T(1,128)S(1)} async-done(((f32[16,1,1024]{2,1,0:T(1,128)}), f32[16,1,1024]{2,1,0:T(1,128)S(1)}, u32[]{:S(2)}, u32[]{:S(2)}) %all-to-all-start.6) | async-done | bytes 65568 | tf_op jit(solution)/shard_map/all_to_all | solution.py:288
  (92 shorter events, 20.2 us)
Async XLA Ops:
  7.2 148.0 %copy-start = (bf16[512,512]{1,0:T(8,128)(2,1)S(1)}, bf16[512,512]{1,0:T(8,128)(2,1)}, u32[]{:S(2)}) copy-start(bf16[512,512]{1,0:T(8,128)(2,1)} %param.6) | copy-start | bytes 1572868
  7.2 23.0 %slice-start.1 = ((f32[256,64]{0,1:T(8,128)}), f32[32,64]{0,1:T(8,128)S(1)}, s32[]{:S(2)}) async-start(f32[256,64]{0,1:T(8,128)} %param.4), calls=%async_computation.12 | async-start | bytes 65536 | tf_op jit(solution)/shard_map/slice | solution.py:214
  7.2 44.2 %copy-start.13 = (f32[32,512]{1,0:T(8,128)S(1)}, f32[32,512]{1,0:T(8,128)}, u32[]{:S(2)}) copy-start(f32[32,512]{1,0:T(8,128)} %param.7) | copy-start | bytes 196612
  7.2 96.1 %all-gather.3.cloned.1.call-start = ((), (), s32[]{:S(2)}) async-start(), calls=%async_computation.8 | async-start | bytes 2621440 | tf_op jit(solution)/shard_map/all_gather | solution.py:256
  30.4 24.5 %collective-permute-start.2 = (bf16[32,1216]{1,0:T(8,128)(2,1)S(1)}, bf16[32,1216]{1,0:T(8,128)(2,1)S(1)}, u32[]{:S(2)}, u32[]{:S(2)}) collective-permute-start(bf16[32,1216]{1,0:T(8,128)(2,1)S(1)} %concatenate.9), channel_id=1, source_target_pairs={{0,48},{16,0},{32,16},{48,32},{64,112},{80,64},{96,80},{112,96},{1... | collective-permute-start | bytes 233480 | tf_op jit(solution)/shard_map/ppermute | solution.py:218
  36.3 18.6 %collective-permute-start.1 = (bf16[32,1216]{1,0:T(8,128)(2,1)S(1)}, bf16[32,1216]{1,0:T(8,128)(2,1)S(1)}, u32[]{:S(2)}, u32[]{:S(2)}) collective-permute-start(bf16[32,1216]{1,0:T(8,128)(2,1)S(1)} %concatenate.9), channel_id=1, source_target_pairs={{0,32},{16,48},{32,0},{48,16},{64,96},{80,112},{96,64},{112,80},{1... | collective-permute-start | bytes 233480 | tf_op jit(solution)/shard_map/ppermute | solution.py:218
  38.8 16.2 %collective-permute-start = (bf16[32,1216]{1,0:T(8,128)(2,1)S(1)}, bf16[32,1216]{1,0:T(8,128)(2,1)S(1)}, u32[]{:S(2)}, u32[]{:S(2)}) collective-permute-start(bf16[32,1216]{1,0:T(8,128)(2,1)S(1)} %concatenate.9), channel_id=1, source_target_pairs={{0,16},{16,32},{32,48},{48,0},{64,80},{80,96},{96,112},{112,64},{1... | collective-permute-start | bytes 233480 | tf_op jit(solution)/shard_map/ppermute | solution.py:218
  42.0 53.6 %collective-permute-start.3 = (bf16[32,512]{1,0:T(8,128)(2,1)}, bf16[32,512]{1,0:T(8,128)(2,1)}, u32[]{:S(2)}, u32[]{:S(2)}) collective-permute-start(bf16[32,512]{1,0:T(8,128)(2,1)} %get-tuple-element.45), channel_id=1, source_target_pairs={{0,16},{1,48},{2,80},{3,112},{4,144},{5,176},{6,208},{7,240},{8,27... | collective-permute-start | bytes 98312 | tf_op jit(solution)/shard_map/ppermute | solution.py:250
  49.1 46.5 %collective-permute-start.4 = (bf16[32,512]{1,0:T(8,128)(2,1)}, bf16[32,512]{1,0:T(8,128)(2,1)}, u32[]{:S(2)}, u32[]{:S(2)}) collective-permute-start(bf16[32,512]{1,0:T(8,128)(2,1)} %get-tuple-element.46), channel_id=1, source_target_pairs={{0,0},{1,32},{2,64},{3,96},{4,128},{5,160},{6,192},{7,224},{8,256}... | collective-permute-start | bytes 98312 | tf_op jit(solution)/shard_map/ppermute | solution.py:250
  54.9 6.1 %copy-start.5 = (bf16[8,32,1024]{2,1,0:T(8,128)(2,1)S(1)}, bf16[8,32,1024]{2,1,0:T(8,128)(2,1)}, u32[]{:S(2)}) copy-start(bf16[8,32,1024]{2,1,0:T(8,128)(2,1)} %all_to_all.35) | copy-start | bytes 1572868
  55.0 0.6 copy-start.6
  55.0 0.7 copy-start.7
  55.1 0.7 copy-start.8
  55.1 0.7 copy-start.9
  62.1 29.5 %all-to-all-start.1 = ((f32[16,16,128]{2,1,0:T(8,128)}), f32[16,16,128]{2,1,0:T(8,128)S(1)}, u32[]{:S(2)}, u32[]{:S(2)}) async-start(f32[16,16,128]{2,1,0:T(8,128)} %bitcast.12), calls=%async_computation.1 | async-start | bytes 262144 | tf_op jit(solution)/shard_map/all_to_all | solution.py:238
  82.4 1.6 copy-start.12
  92.2 11.1 %all-to-all-start.2 = ((f32[8,16,128]{2,1,0:T(8,128)}), f32[8,16,128]{2,1,0:T(8,128)S(1)}, u32[]{:S(2)}, u32[]{:S(2)}) async-start(f32[8,16,128]{2,1,0:T(8,128)} %broadcast_in_dim.76), calls=%async_computation.2 | async-start | bytes 131072 | tf_op jit(solution)/shard_map/all_to_all | solution.py:190
  103.3 1.8 copy-start.11
  103.3 1.8 copy-start.10
  105.2 1.8 slice-start
  108.1 35.9 %all-to-all-start.3 = ((f32[32,5,16,128]{3,2,1,0:T(8,128)}), f32[32,5,16,128]{3,2,1,0:T(8,128)S(1)}, u32[]{:S(2)}, u32[]{:S(2)}) async-start(f32[32,5,16,128]{3,2,1,0:T(8,128)} %broadcast_in_dim.81), calls=%async_computation.3 | async-start | bytes 2621440 | tf_op jit(solution)/shard_map/all_to_all | solution.py:190
  112.8 42.4 %all-gather.5.cloned.1.call-start = ((), (), s32[]{:S(2)}) async-start(), calls=%async_computation.9 | async-start | bytes 1114112 | tf_op jit(solution)/shard_map/all_gather | solution.py:270
  113.5 111.0 %reduce-scatter.2.cloned.1.call-start = ((), (), s32[]{:S(2)}) async-start(), calls=%async_computation.10 | async-start | bytes 1114112 | tf_op jit(solution)/shard_map/reduce_scatter | solution.py:268
  144.1 24.8 %collective-permute-start.5 = (f32[32,5,16,128]{3,2,1,0:T(8,128)S(1)}, f32[32,5,16,128]{3,2,1,0:T(8,128)S(1)}, u32[]{:S(2)}, u32[]{:S(2)}) collective-permute-start(f32[32,5,16,128]{3,2,1,0:T(8,128)S(1)} %all-to-all-done.3.mine_ref), channel_id=1, source_target_pairs={{0,1},{1,0},{2,3},{3,2},{4,5},{5,4},{6,7},{7,6},{8,9},{9,8},{10,11... | collective-permute-start | bytes 3932168 | tf_op jit(solution)/shard_map/ppermute | solution.py:267
  159.2 58.6 %all-to-all-start.4 = ((f32[32,16,1024]{2,1,0:T(8,128)}), f32[32,16,1024]{2,1,0:T(8,128)}, u32[]{:S(2)}, u32[]{:S(2)}) async-start(f32[32,16,1024]{2,1,0:T(8,128)} %bitcast.55), calls=%async_computation.4 | async-start | bytes 4194304 | tf_op jit(solution)/shard_map/all_to_all | solution.py:276
  215.9 2.0 copy-start.1
  219.6 2.2 copy-start.2
  225.6 17.8 %all-to-all-start.5 = ((f32[32,1,512]{2,1,0:T(1,128)}), f32[32,1,512]{2,1,0:T(1,128)S(1)}, u32[]{:S(2)}, u32[]{:S(2)}) async-start(f32[32,1,512]{2,1,0:T(1,128)} %reshape.163), calls=%async_computation.6 | async-start | bytes 131072 | tf_op jit(solution)/shard_map/all_to_all | solution.py:285
  234.6 2.2 copy-start.3
  236.8 0.8 copy-start.4
  245.8 14.2 %all-to-all-start.6 = ((f32[16,1,1024]{2,1,0:T(1,128)}), f32[16,1,1024]{2,1,0:T(1,128)S(1)}, u32[]{:S(2)}, u32[]{:S(2)}) async-start(f32[16,1,1024]{2,1,0:T(1,128)} %reshape.165), calls=%async_computation.7 | async-start | bytes 131072 | tf_op jit(solution)/shard_map/all_to_all | solution.py:288
Sparse Core Ops, SparseCore 0:
  30.3 39.2 all-gather.2
  116.3 38.8 all-gather.4
  158.0 57.7 reduce-scatter.1

commit v6 on v5

--- a/solution.py
+++ b/solution.py
@@ -8,48 +8,75 @@
 HI = lax.Precision.HIGHEST
 
 
-def factor_block(s_ref):
+def factor_block(s_ref, c_ref):
     lane = lax.broadcasted_iota(jnp.int32, (8, 128), 1)
     sub = lax.broadcasted_iota(jnp.int32, (8, 128), 0)
+
+    def wide(value, at):
+        return jnp.broadcast_to(value[:, at:at + 1], (8, 128))
+
+    def apply(v, base, q):
+        rows = s_ref[8 * v:8 * v + 8, :]
+        part = [wide(rows, base + j) * q[j] for j in range(8)]
+        total = ((part[0] + part[1]) + (part[2] + part[3])) + ((part[4] + part[5]) + (part[6] + part[7]))
+        rows = jnp.where((lane >= base) & (lane < base + 8), 0.0, rows) - total
+        s_ref[8 * v:8 * v + 8, :] = rows
+        return rows
+
+    w = s_ref[0:8, :]
+    follow = s_ref[8:16, :]
+    waiting = []
     for g in range(16):
         base = 8 * g
         inside = (lane >= base) & (lane < base + 8)
-        w = s_ref[base:base + 8, :]
         x = [[None] * 8 for _ in range(8)]
         for j in range(8):
-            c = jnp.broadcast_to(w[:, base + j:base + j + 1], (8, 128))
+            c = wide(w, base + j)
+            at = 72 * (g % 2) + 8 * j
+            c_ref[at:at + 8, :] = c
             for i in range(j, 8):
-                x[i][j] = jnp.broadcast_to(c[i:i + 1, :], (8, 128))
+                x[i][j] = c_ref[pl.ds(at + i, 8, stride=0), :]
         start = jnp.where(lane == sub + base, 1.0, jnp.where(inside, 0.0, w))
-        r = [jnp.broadcast_to(start[j:j + 1, :], (8, 128)) for j in range(8)]
-        m = [[None] * 8 for _ in range(8)]
-        q = [None] * 8
+        at = 72 * (g % 2) + 64
+        c_ref[at:at + 8, :] = start
+        r = [c_ref[pl.ds(at + j, 8, stride=0), :] for j in range(8)]
+        if g < 15:
+            if waiting:
+                follow = waiting.pop(0)()
+            b = [wide(follow, base + k) for k in range(8)]
+            follow = jnp.where(inside, 0.0, follow)
+        ahead = [[None] * 8 for _ in range(8)]
         top = None
+        share = -(-len(waiting) // 8)
         for j in range(8):
+            d = 1.0 / x[j][j]
             s = lax.rsqrt(x[j][j])
             t = r[j] * s
             top = t if top is None else jnp.where(sub == j, t, top)
-            m[j][j] = s
-            for k in range(j):
-                m[j][k] = m[j][k] * s
-            for k in range(j + 1):
-                part = m[j][k] * t
-                q[k] = part if q[k] is None else q[k] + part
-            col = {i: x[i][j] * s for i in range(j + 1, 8)}
+            f = {i: x[i][j] * d for i in range(j + 1, 8)}
             for i in range(j + 1, 8):
                 for k in range(j + 1, i + 1):
-                    x[i][k] = x[i][k] - col[i] * col[k]
-                r[i] = r[i] - col[i] * t
-                for k in range(j + 1):
-                    part = col[i] * m[j][k]
-                    m[i][k] = -part if m[i][k] is None else m[i][k] - part
+                    x[i][k] = x[i][k] - (x[i][j] * x[k][j]) * d if i == j + 1 else x[i][k] - f[i] * x[k][j]
+            p = r[j] * d
+            for i in range(j + 1, 8):
+                r[i] = r[i] - x[i][j] * p
+            if g < 15:
+                follow = follow - b[j] * p
+                for k in range(j + 1, 8):
+                    b[k] = b[k] - b[j] * f[k]
+            for i in range(j):
+                r[i] = r[i] - ahead[i][j] * p
+                for k in range(j + 1, 8):
+                    ahead[i][k] = ahead[i][k] - ahead[i][j] * f[k]
+            r[j] = p
+            for k in range(j + 1, 8):
+                ahead[j][k] = f[k]
+            for _ in range(share):
+                if waiting:
+                    waiting.pop(0)()
         s_ref[base:base + 8, :] = top
-        for v in range(g + 1, 16):
-            wv = s_ref[8 * v:8 * v + 8, :]
-            acc = jnp.where(inside, 0.0, wv)
-            for j in range(8):
-                acc = acc - jnp.broadcast_to(wv[:, base + j:base + j + 1], (8, 128)) * q[j]
-            s_ref[8 * v:8 * v + 8, :] = acc
+        w = follow
+        waiting = [lambda v=v, base=base, q=r: apply(v, base, q) for v in range(g + 2, 16)]
     rows = lax.broadcasted_iota(jnp.int32, (128, 128), 0)
     cols = lax.broadcasted_iota(jnp.int32, (128, 128), 1)
     s_ref[...] = jnp.where(cols <= rows, s_ref[...], 0.0)
@@ -67,7 +94,7 @@
     return lax.dot_general(a, b, (((1,), (1,)), ((), ())), precision=HI, preferred_element_type=jnp.float32)
 
 
-def factor_kernel(core_ref, mine_ref, other_ref, w_ref, s_ref, m_ref):
+def factor_kernel(core_ref, mine_ref, other_ref, out_ref, w_ref, s_ref, m_ref, c_ref, sems):
     big, n, _ = w_ref.shape
     rows, kept, half, lanes = mine_ref.shape
     tall = n // lanes
@@ -110,7 +137,7 @@
                 m_ref[0:128, 128:256] = upper
                 s_ref[...] = w_ref[b, pl.ds(mid, 128), 128:256] - mtm(upper, upper)
 
-            factor_block(s_ref)
+            factor_block(s_ref, c_ref)
             return carry
 
         lax.fori_loop(0, 2, half_step, 0)
@@ -124,6 +151,13 @@
             @pl.when(j > b)
             def _():
                 w_ref[j, pl.ds(top, 256), :] = mm(m_ref[...], w_ref[j, pl.ds(top, 256), :])
+
+        for j in range(big):
+            @pl.when(j >= b)
+            def _():
+                pltpu.make_async_copy(
+                    w_ref.at[j, pl.ds(top, 256), :], out_ref.at[j, pl.ds(top, 256), :], sems.at[b, j]
+                ).start()
 
         def below(i, carry):
             at = pl.multiple_of(i * 256, 256)
@@ -139,30 +173,49 @@
         return carry
 
     lax.fori_loop(0, big, step, 0)
-
-
-def solve_kernel(w_ref, u_ref, out_ref, x_ref):
+    for b in range(big):
+        span = pl.ds(256 * b, 256)
+        for j in range(b, big):
+            pltpu.make_async_copy(w_ref.at[j, span, :], out_ref.at[j, span, :], sems.at[b, j]).wait()
+
+
+def solve_kernel(from_ref, u_ref, out_ref, w_ref, x_ref, sems):
     big = w_ref.shape[0]
+    copies = {}
+    for b in range(big):
+        span = pl.ds(256 * b, 256)
+        for j in range(b, big):
+            copies[b, j] = pltpu.make_async_copy(from_ref.at[j, span, :], w_ref.at[j, span, :], sems.at[b, j])
+            copies[b, j].start()
     x_ref[...] = u_ref[...]
     for b in range(big):
         span = slice(256 * b, 256 * b + 256)
+        copies[b, b].wait()
         y = mmt(x_ref[:, span], w_ref[b, span, :])
         out_ref[:, span] = y
         for j in range(b + 1, big):
             right = slice(256 * j, 256 * j + 256)
+            copies[b, j].wait()
             x_ref[:, right] = x_ref[:, right] - mm(y, w_ref[j, span, :])
 
 
 def factor(core, mine, other, panel):
     vmem = pl.BlockSpec(memory_space=pltpu.VMEM)
+    big = panel // 256
     return pl.pallas_call(
         factor_kernel,
-        out_shape=jax.ShapeDtypeStruct((panel // 256, panel, 256), jnp.float32),
+        out_shape=pltpu.HBM((big, panel, 256), jnp.float32),
         in_specs=[pl.BlockSpec(memory_space=pltpu.SMEM), vmem, vmem],
-        out_specs=vmem,
-        scratch_shapes=[pltpu.VMEM((128, 128), jnp.float32), pltpu.VMEM((256, 256), jnp.float32)],
-        compiler_params=pltpu.CompilerParams(vmem_limit_bytes=12 * 1024 * 1024),
-        cost_estimate=pl.CostEstimate(flops=50_000_000_000, transcendentals=0, bytes_accessed=8_000_000),
+        out_specs=pl.BlockSpec(memory_space=pltpu.HBM),
+        scratch_shapes=[
+            pltpu.VMEM((big, panel, 256), jnp.float32),
+            pltpu.VMEM((128, 128), jnp.float32),
+            pltpu.VMEM((256, 256), jnp.float32),
+            pltpu.VMEM((144, 128), jnp.float32),
+            pltpu.SemaphoreType.DMA((big, big)),
+        ],
+        compiler_params=pltpu.CompilerParams(vmem_limit_bytes=16 * 1024 * 1024),
+        cost_estimate=pl.CostEstimate(flops=40_000_000_000, transcendentals=0, bytes_accessed=8_000_000),
     )(core, mine, other)
 
 
@@ -171,11 +224,15 @@
     return pl.pallas_call(
         solve_kernel,
         out_shape=jax.ShapeDtypeStruct(u.shape, jnp.float32),
-        in_specs=[vmem, vmem],
+        in_specs=[pl.BlockSpec(memory_space=pltpu.HBM), vmem],
         out_specs=vmem,
-        scratch_shapes=[pltpu.VMEM(u.shape, jnp.float32)],
+        scratch_shapes=[
+            pltpu.VMEM(w.shape, jnp.float32),
+            pltpu.VMEM(u.shape, jnp.float32),
+            pltpu.SemaphoreType.DMA((w.shape[0], w.shape[0])),
+        ],
         compiler_params=pltpu.CompilerParams(vmem_limit_bytes=12 * 1024 * 1024),
-    )(w, u)
+    )(pltpu.with_memory_space_constraint(w, pltpu.HBM), u)
 
 
 def split_three(value):
@@ -212,12 +269,9 @@
     lane = lax.broadcasted_iota(jnp.int32, (1, panel), 1)
 
     packed = jnp.concatenate([own] + split_three(gram_panel[:block_rows]), axis=1)
-    near = [packed]
-    for shift in range(1, wide):
-        pairs = [(y * wide + x, y * wide + (x + shift) % wide) for y in range(tall) for x in range(wide)]
-        near.append(lax.ppermute(packed, "row", pairs))
-    from_x = jnp.stack([lax.select_n((x_place - x) % wide, *near) for x in range(wide)], axis=0)
     from_y = collect(own, "row", tall, along_y)
+    packed, from_y = lax.optimization_barrier((packed, from_y))
+    from_x = collect(packed, "row", wide, along_x)
     rows_x = from_x[:, :, :depth].reshape(wide * block_rows, depth)
     rows_y = from_y.reshape(tall * block_rows, depth)
     gram_x = from_x[:, :, depth:].astype(jnp.float32).reshape(wide * block_rows, 3, per_col, block_rows)
@@ -235,13 +289,14 @@
     turned = lax.dynamic_slice_in_dim(jnp.concatenate([turned, turned], axis=0), tall - 1 - row_place // wide, tall, 0)
     thin = tall * block_rows // col_count
     partial = turned.reshape(col_count, thin, wide * block_rows)
-    own_diag = jnp.sum(lax.all_to_all(partial, "col", 0, 0), axis=0)
+
+    own_late, partial_now = lax.optimization_barrier((own, partial))
+    own_diag = jnp.sum(lax.all_to_all(partial_now, "col", 0, 0), axis=0)
     diag_z = collect(own_diag, "col", chips, along_z)
-
     pieces = []
     for turn in range(per_col):
         half = (row_place + turn) % per_col
-        sent = lax.dynamic_slice_in_dim(own, half * strip, strip, 1)
+        sent = lax.dynamic_slice_in_dim(own_late, half * strip, strip, 1)
         pairs = []
         for r in range(row_count):
             for c in range(col_count):
@@ -254,7 +309,6 @@
     )
 
     chosen = lax.all_gather(rows_y, "row", axis=0, tiled=False, axis_index_groups=along_x)
-    chosen, mine = lax.optimization_barrier((chosen, mine))
     chosen = chosen.reshape(wide, tall, block_rows, depth).transpose(1, 0, 2, 3).reshape(panel, depth)
     gram_placed = jnp.where(lane // col_width == col_place, jnp.tile(gram_panel, (1, col_count)), 0.0)
     update_part = gram_placed - lax.dot_general(
@@ -262,7 +316,7 @@
     )
     right_placed = jnp.where(lane // block_rows == row_place, jnp.tile(right_block.T, (1, row_count)), 0.0)
 
-    diag_z, update_part, right_placed = lax.optimization_barrier((diag_z[:kept], update_part, right_placed))
+    diag_z, update_part, right_placed, _ = lax.optimization_barrier((diag_z[:kept], update_part, right_placed, mine))
     diag_row = collect(diag_z, "row", row_count)
     other = lax.ppermute(diag_row, "col", [(i, i ^ 1) for i in range(col_count)])
     update = lax.psum_scatter(update_part, "col", scatter_dimension=0, tiled=True)

time: 269 us -> 273 us (1.015)
  waiting for transfers between devices: 60.8 us -> 88.2 us
  blocking collectives: 22 us -> 0 us
  starting transfers between devices: 78.4 us -> 84.6 us
  Pallas kernels: 52.5 us -> 48 us
  local copies, waits for them, and re-layouts: 25.2 us -> 22.2 us
    all_to_all x2 -> x4, starting transfers between devices: 7.98 us -> 34.1 us  [collect(): return lax.all_to_all(many, axis, 0, 0, axis_index_groups=groups)]
    all_to_all x1 -> x0, blocking collectives: 22 us -> none  [collect(): return lax.all_to_all(many, axis, 0, 0, axis_index_groups=groups)]
    all_to_all x2 -> x4, waiting for transfers between devices: 36.8 us -> 55.4 us  [collect(): return lax.all_to_all(many, axis, 0, 0, axis_index_groups=groups)]
    ppermute x3 -> x0, starting transfers between devices: 10.9 us -> none  [body(): near.append(lax.ppermute(packed, 'row', pairs))]
    all_to_all x1, waiting for transfers between devices: 0.01 us -> 9.59 us  [body(): spread_out = lax.all_to_all(product, 'row', 0, 0)]
    pallas_call x1, Pallas kernels: 47.1 us -> 38.1 us  [factor(): pl.pallas_call(factor_kernel, out_shape=pltpu.HBM((big, panel, 256), jnp....]
    all_to_all x1, starting transfers between devices: 20.3 us -> 12.3 us  [body(): own_diag = jnp.sum(lax.all_to_all(partial_now, 'col', 0, 0), axis=0)]
    reduce_scatter x1, waiting for transfers between devices: 0.01 us -> 6.27 us  [body(): lax.psum_scatter(update_part, 'col', scatter_dimension=0, tiled=True)]
  transfers between devices with their start and end apart: 15 -> 14, of which waited for: 6 -> 10; matrix products, arithmetic and copies ran while one was open for 8% -> 8% of each run, Pallas kernels for 20% -> 18%
where the time goes in v6:
time: 273 us; the launch traced here: 272 us
  waiting for transfers between devices  88.2 us (32%)
  starting transfers between devices  84.6 us (31%)
  Pallas kernels  48 us (18%)
  local copies, waits for them, and re-layouts  22.2 us (8%)
  between operations  15.8 us (6%)
  other arithmetic  7.12 us (3%)
  matrix products  6.15 us (2%)
    all_to_all x4, waiting for transfers between devices, collect(): return lax.all_to_all(many, axis, 0, 0, axis_index_groups=groups)  55.4 us
    pallas_call x1, Pallas kernels, factor(): pl.pallas_call(factor_kernel, out_shape=pltpu.HBM((big, panel, 256), jnp....  38.1 us
    all_to_all x4, starting transfers between devices, collect(): return lax.all_to_all(many, axis, 0, 0, axis_index_groups=groups)  34.1 us
    all_to_all x1, starting transfers between devices, body(): own_diag = jnp.sum(lax.all_to_all(partial_now, 'col', 0, 0), axis=0)  12.3 us
    pallas_call x2, Pallas kernels, forward(): pl.pallas_call(solve_kernel, out_shape=jax.ShapeDtypeStruct(u.shape, jnp....  9.84 us
    all_to_all x1, waiting for transfers between devices, body(): spread_out = lax.all_to_all(product, 'row', 0, 0)  9.59 us
    all_to_all x1, starting transfers between devices, body(): spread_out = lax.all_to_all(product, 'row', 0, 0)  9.39 us
    all_to_all x1, starting transfers between devices, body(): panel_factor = lax.all_to_all(rows_out, 'col', 0, 0).reshape(-1, col_width)  9.01 us
  transfers between devices with their start and end apart: 14, of which 10 were waited for; matrix products, arithmetic and copies ran while one was open for 8% of the time, Pallas kernels for 18%

profile of v6, /device:TPU:1, one launch (start us, length us, event | category | flops | bytes accessed | tf_op | source)
XLA Modules:
  0.0 272.0 jit_solution(16400586025706718806)
XLA Ops:
  9.8 7.7 %all-to-all-start = ((bf16[8,32,1024]{2,1,0:T(8,128)(2,1)}), bf16[8,32,1024]{2,1,0:T(8,128)(2,1)S(1)}, u32[]{:S(2)}, u32[]{:S(2)}) async-start(bf16[8,32,1024]{2,1,0:T(8,128)(2,1)} %broadcast_in_dim.78), calls=%async_computation | async-start | bytes 1048576 | tf_op jit(solution)/shard_map/all_to_all | solution.py:247
  18.5 13.8 %all-to-all-done = bf16[8,32,1024]{2,1,0:T(8,128)(2,1)S(1)} async-done(((bf16[8,32,1024]{2,1,0:T(8,128)(2,1)}), bf16[8,32,1024]{2,1,0:T(8,128)(2,1)S(1)}, u32[]{:S(2)}, u32[]{:S(2)}) %all-to-all-start) | async-done | bytes 524320 | tf_op jit(solution)/shard_map/all_to_all | solution.py:247
  33.8 7.2 %all-to-all-start.1 = ((bf16[4,32,1216]{2,1,0:T(8,128)(2,1)}), bf16[4,32,1216]{2,1,0:T(8,128)(2,1)S(1)}, u32[]{:S(2)}, u32[]{:S(2)}) async-start(bf16[4,32,1216]{2,1,0:T(8,128)(2,1)} %broadcast_in_dim.79), calls=%async_computation.1 | async-start | bytes 655360 | tf_op jit(solution)/shard_map/all_to_all | solution.py:247
  41.2 1.6 tile.20
  42.8 1.9 copy.37
  44.7 2.7 all-to-all-done.1
  48.8 1.2 reshape.162
  54.4 12.3 %all-to-all-start.2 = ((f32[16,16,128]{2,1,0:T(8,128)}), f32[16,16,128]{2,1,0:T(8,128)S(1)}, u32[]{:S(2)}, u32[]{:S(2)}) async-start(f32[16,16,128]{2,1,0:T(8,128)} %bitcast.7), calls=%async_computation.2 | async-start | bytes 262144 | tf_op jit(solution)/shard_map/all_to_all | solution.py:294
  66.7 1.5 broadcast_select_fusion
  68.2 2.8 %collective-permute-start = (bf16[32,512]{1,0:T(8,128)(2,1)S(1)}, bf16[32,512]{1,0:T(8,128)(2,1)S(1)}, u32[]{:S(2)}, u32[]{:S(2)}) collective-permute-start(bf16[32,512]{1,0:T(8,128)(2,1)S(1)} %get-tuple-element.45), channel_id=1, source_target_pairs={{0,16},{1,48},{2,80},{3,112},{4,144},{5,176},{6,208},{7,240},{8,27... | collective-permute-start | bytes 98312 | tf_op jit(solution)/shard_map/ppermute | solution.py:305
  71.0 3.4 %collective-permute-start.1 = (bf16[32,512]{1,0:T(8,128)(2,1)S(1)}, bf16[32,512]{1,0:T(8,128)(2,1)S(1)}, u32[]{:S(2)}, u32[]{:S(2)}) collective-permute-start(bf16[32,512]{1,0:T(8,128)(2,1)S(1)} %get-tuple-element.46), channel_id=1, source_target_pairs={{0,0},{1,32},{2,64},{3,96},{4,128},{5,160},{6,192},{7,224},{8,256}... | collective-permute-start | bytes 98312 | tf_op jit(solution)/shard_map/ppermute | solution.py:305
  76.5 15.3 %all-to-all-start.3 = ((f32[8,16,128]{2,1,0:T(8,128)}), f32[8,16,128]{2,1,0:T(8,128)S(1)}, u32[]{:S(2)}, u32[]{:S(2)}) async-start(f32[8,16,128]{2,1,0:T(8,128)} %broadcast_in_dim.83), calls=%async_computation.3 | async-start | bytes 131072 | tf_op jit(solution)/shard_map/all_to_all | solution.py:247
  92.4 7.4 %all-to-all-done.3 = f32[8,16,128]{2,1,0:T(8,128)S(1)} async-done(((f32[8,16,128]{2,1,0:T(8,128)}), f32[8,16,128]{2,1,0:T(8,128)S(1)}, u32[]{:S(2)}, u32[]{:S(2)}) %all-to-all-start.3) | async-done | bytes 65568 | tf_op jit(solution)/shard_map/all_to_all | solution.py:247
  99.8 1.8 copy.35
  101.7 1.8 fusion
  103.5 1.2 broadcast_in_dim.88
  104.6 4.0 %all-to-all-start.4 = ((f32[32,5,16,128]{3,2,1,0:T(8,128)}), f32[32,5,16,128]{3,2,1,0:T(8,128)S(1)}, u32[]{:S(2)}, u32[]{:S(2)}) async-start(f32[32,5,16,128]{3,2,1,0:T(8,128)} %broadcast_in_dim.88), calls=%async_computation.4 | async-start | bytes 2621440 | tf_op jit(solution)/shard_map/all_to_all | solution.py:247
  109.2 31.6 %all-to-all-done.4.mine_ref = f32[32,5,16,128]{3,2,1,0:T(8,128)S(1)} async-done(((f32[32,5,16,128]{3,2,1,0:T(8,128)}), f32[32,5,16,128]{3,2,1,0:T(8,128)S(1)}, u32[]{:S(2)}, u32[]{:S(2)}) %all-to-all-start.4) | async-done | bytes 1310752 | tf_op jit(solution)/shard_map/all_to_all | solution.py:247
  140.8 4.6 %collective-permute-start.2 = (f32[32,5,16,128]{3,2,1,0:T(8,128)S(1)}, f32[32,5,16,128]{3,2,1,0:T(8,128)S(1)}, u32[]{:S(2)}, u32[]{:S(2)}) collective-permute-start(f32[32,5,16,128]{3,2,1,0:T(8,128)S(1)} %all-to-all-done.4.mine_ref), channel_id=1, source_target_pairs={{0,1},{1,0},{2,3},{3,2},{4,5},{5,4},{6,7},{7,6},{8,9},{9,8},{10,11... | collective-permute-start | bytes 3932168 | tf_op jit(solution)/shard_map/ppermute | solution.py:321
  145.4 4.9 %all-gather.5.cloned.1.call-done = bf16[1024,512]{1,0:T(8,128)(2,1)} async-done(((bf16[64,512]{1,0:T(8,128)(2,1)}), bf16[1024,512]{1,0:T(8,128)(2,1)}) %all-gather.5.cloned.1.call-update) | async-done | bytes 1048592 | tf_op jit(solution)/shard_map/all_gather | solution.py:324
  150.4 4.0 %bitcast_subtract_fusion = f32[512,1024]{1,0:T(8,128)} fusion(f32[512,1024]{1,0:T(8,128)} %broadcast_select_fusion, bf16[1024,512]{1,0:T(8,128)(2,1)} %all-gather.5.cloned.1.call-done, bf16[512,512]{1,0:T(8,128)(2,1)S(1)} %copy-done), kind=kOutput, calls=%fused_computation | convolution fusion | flops 537395200 | bytes 5767168 | tf_op jit(solution)/shard_map/dot_general | solution.py:325
  154.4 9.4 %all-to-all-start.5 = ((f32[32,16,1024]{2,1,0:T(8,128)}), f32[32,16,1024]{2,1,0:T(8,128)}, u32[]{:S(2)}, u32[]{:S(2)}) async-start(f32[32,16,1024]{2,1,0:T(8,128)} %bitcast.44), calls=%async_computation.5 | async-start | bytes 4194304 | tf_op jit(solution)/shard_map/all_to_all | solution.py:330
  164.4 38.1 %shard_map.59.from_ref = f32[4,1024,256]{2,1,0:T(8,128)} custom-call(s32[1]{0:T(128)} %bitcast.core_ref, f32[32,5,16,128]{3,2,1,0:T(8,128)S(1)} %all-to-all-done.4.mine_ref, f32[32,5,16,128]{3,2,1,0:T(8,128)S(1)} %collective-permute-done.2.other_ref), custom_call_target="tpu_custom_call" | custom-call | flops 40000000000 | bytes 8000000 | tf_op jit(solution)/shard_map/pallas_call | solution.py:205
  202.5 9.6 %all-to-all-done.5 = f32[32,16,1024]{2,1,0:T(8,128)} async-done(((f32[32,16,1024]{2,1,0:T(8,128)}), f32[32,16,1024]{2,1,0:T(8,128)}, u32[]{:S(2)}, u32[]{:S(2)}) %all-to-all-start.5) | async-done | bytes 2097184 | tf_op jit(solution)/shard_map/all_to_all | solution.py:330
  212.1 1.7 reduce_sum.19.u_ref
  213.9 4.9 %shard_map.60 = f32[16,1024]{1,0:T(8,128)S(1)} custom-call(f32[4,1024,256]{2,1,0:T(8,128)} %shard_map.59.from_ref, f32[16,1024]{1,0:T(8,128)S(1)} %reduce_sum.19.u_ref), custom_call_target="tpu_custom_call" | custom-call | tf_op jit(solution)/shard_map/pallas_call | solution.py:224
  218.8 6.3 %reduce-scatter.2.cloned.1.call-done.u_ref = f32[16,1024]{1,0:T(8,128)} async-done(((f32[256,1024]{1,0:T(8,128)}), f32[16,1024]{1,0:T(8,128)}) %reduce-scatter.2.cloned.1.call-update) | async-done | bytes 65552 | tf_op jit(solution)/shard_map/reduce_scatter | solution.py:322
  226.1 8.7 %all-to-all-start.6 = ((f32[32,1,512]{2,1,0:T(1,128)}), f32[32,1,512]{2,1,0:T(1,128)S(1)}, u32[]{:S(2)}, u32[]{:S(2)}) async-start(f32[32,1,512]{2,1,0:T(1,128)} %reshape.164), calls=%async_computation.7 | async-start | bytes 131072 | tf_op jit(solution)/shard_map/all_to_all | solution.py:339
  235.7 4.9 %shard_map.61 = f32[16,1024]{1,0:T(8,128)S(1)} custom-call(f32[4,1024,256]{2,1,0:T(8,128)} %shard_map.59.from_ref, f32[16,1024]{1,0:T(8,128)S(1)} %copy-done.1), custom_call_target="tpu_custom_call" | custom-call | tf_op jit(solution)/shard_map/pallas_call | solution.py:224
  240.6 3.1 %all-to-all-done.6 = f32[32,1,512]{2,1,0:T(1,128)S(1)} async-done(((f32[32,1,512]{2,1,0:T(1,128)}), f32[32,1,512]{2,1,0:T(1,128)S(1)}, u32[]{:S(2)}, u32[]{:S(2)}) %all-to-all-start.6) | async-done | bytes 65568 | tf_op jit(solution)/shard_map/all_to_all | solution.py:339
  246.1 9.0 %all-to-all-start.7 = ((f32[16,1,1024]{2,1,0:T(1,128)}), f32[16,1,1024]{2,1,0:T(1,128)S(1)}, u32[]{:S(2)}, u32[]{:S(2)}) async-start(f32[16,1,1024]{2,1,0:T(1,128)} %reshape.166), calls=%async_computation.8 | async-start | bytes 131072 | tf_op jit(solution)/shard_map/all_to_all | solution.py:342
  255.9 7.1 %all-to-all-done.7 = f32[16,1,1024]{2,1,0:T(1,128)S(1)} async-done(((f32[16,1,1024]{2,1,0:T(1,128)}), f32[16,1,1024]{2,1,0:T(1,128)S(1)}, u32[]{:S(2)}, u32[]{:S(2)}) %all-to-all-start.7) | async-done | bytes 65568 | tf_op jit(solution)/shard_map/all_to_all | solution.py:342
  (80 shorter events, 20.8 us)
Async XLA Ops:
  8.0 142.4 %copy-start = (bf16[512,512]{1,0:T(8,128)(2,1)S(1)}, bf16[512,512]{1,0:T(8,128)(2,1)}, u32[]{:S(2)}) copy-start(bf16[512,512]{1,0:T(8,128)(2,1)} %param.6) | copy-start | bytes 1572868
  8.0 33.2 %copy-start.10 = (f32[32,512]{1,0:T(8,128)S(1)}, f32[32,512]{1,0:T(8,128)}, u32[]{:S(2)}) copy-start(f32[32,512]{1,0:T(8,128)} %param.7) | copy-start | bytes 196612
  8.9 33.8 %copy-start.5 = (bf16[32,1024]{1,0:T(8,128)(2,1)}, bf16[32,1024]{1,0:T(8,128)(2,1)S(1)}, u32[]{:S(2)}) copy-start(bf16[32,1024]{1,0:T(8,128)(2,1)S(1)} %slice.24) | copy-start | bytes 196612
  9.8 22.4 %all-to-all-start = ((bf16[8,32,1024]{2,1,0:T(8,128)(2,1)}), bf16[8,32,1024]{2,1,0:T(8,128)(2,1)S(1)}, u32[]{:S(2)}, u32[]{:S(2)}) async-start(bf16[8,32,1024]{2,1,0:T(8,128)(2,1)} %broadcast_in_dim.78), calls=%async_computation | async-start | bytes 1048576 | tf_op jit(solution)/shard_map/all_to_all | solution.py:247
  17.5 82.3 %all-gather.3.cloned.1.call-start = ((), (), s32[]{:S(2)}) async-start(), calls=%async_computation.9 | async-start | bytes 2621440 | tf_op jit(solution)/shard_map/all_gather | solution.py:311
  32.2 0.8 copy-start.2
  33.8 13.6 %all-to-all-start.1 = ((bf16[4,32,1216]{2,1,0:T(8,128)(2,1)}), bf16[4,32,1216]{2,1,0:T(8,128)(2,1)S(1)}, u32[]{:S(2)}, u32[]{:S(2)}) async-start(bf16[4,32,1216]{2,1,0:T(8,128)(2,1)} %broadcast_in_dim.79), calls=%async_computation.1 | async-start | bytes 655360 | tf_op jit(solution)/shard_map/all_to_all | solution.py:247
  44.7 8.6 %copy-start.3 = (bf16[8,32,1024]{2,1,0:T(8,128)(2,1)S(1)}, bf16[8,32,1024]{2,1,0:T(8,128)(2,1)}, u32[]{:S(2)}) copy-start(bf16[8,32,1024]{2,1,0:T(8,128)(2,1)} %copy-done.2) | copy-start | bytes 1572868
  47.4 0.7 copy-start.4
  54.4 21.4 %all-to-all-start.2 = ((f32[16,16,128]{2,1,0:T(8,128)}), f32[16,16,128]{2,1,0:T(8,128)S(1)}, u32[]{:S(2)}, u32[]{:S(2)}) async-start(f32[16,16,128]{2,1,0:T(8,128)} %bitcast.7), calls=%async_computation.2 | async-start | bytes 262144 | tf_op jit(solution)/shard_map/all_to_all | solution.py:294
  66.6 1.6 copy-start.6
  66.6 7.8 %copy-start.9 = (f32[256,64]{0,1:T(8,128)S(1)}, f32[256,64]{0,1:T(8,128)}, u32[]{:S(2)}) copy-start(f32[256,64]{0,1:T(8,128)} %param.4) | copy-start | bytes 196612
  68.2 23.5 %collective-permute-start = (bf16[32,512]{1,0:T(8,128)(2,1)S(1)}, bf16[32,512]{1,0:T(8,128)(2,1)S(1)}, u32[]{:S(2)}, u32[]{:S(2)}) collective-permute-start(bf16[32,512]{1,0:T(8,128)(2,1)S(1)} %get-tuple-element.45), channel_id=1, source_target_pairs={{0,16},{1,48},{2,80},{3,112},{4,144},{5,176},{6,208},{7,240},{8,27... | collective-permute-start | bytes 98312 | tf_op jit(solution)/shard_map/ppermute | solution.py:305
  71.0 20.7 %collective-permute-start.1 = (bf16[32,512]{1,0:T(8,128)(2,1)S(1)}, bf16[32,512]{1,0:T(8,128)(2,1)S(1)}, u32[]{:S(2)}, u32[]{:S(2)}) collective-permute-start(bf16[32,512]{1,0:T(8,128)(2,1)S(1)} %get-tuple-element.46), channel_id=1, source_target_pairs={{0,0},{1,32},{2,64},{3,96},{4,128},{5,160},{6,192},{7,224},{8,256}... | collective-permute-start | bytes 98312 | tf_op jit(solution)/shard_map/ppermute | solution.py:305
  76.5 23.3 %all-to-all-start.3 = ((f32[8,16,128]{2,1,0:T(8,128)}), f32[8,16,128]{2,1,0:T(8,128)S(1)}, u32[]{:S(2)}, u32[]{:S(2)}) async-start(f32[8,16,128]{2,1,0:T(8,128)} %broadcast_in_dim.83), calls=%async_computation.3 | async-start | bytes 131072 | tf_op jit(solution)/shard_map/all_to_all | solution.py:247
  99.8 1.8 copy-start.8
  99.8 1.8 copy-start.7
  101.7 1.8 slice-start
  104.6 36.2 %all-to-all-start.4 = ((f32[32,5,16,128]{3,2,1,0:T(8,128)}), f32[32,5,16,128]{3,2,1,0:T(8,128)S(1)}, u32[]{:S(2)}, u32[]{:S(2)}) async-start(f32[32,5,16,128]{3,2,1,0:T(8,128)} %broadcast_in_dim.88), calls=%async_computation.4 | async-start | bytes 2621440 | tf_op jit(solution)/shard_map/all_to_all | solution.py:247
  108.6 41.8 %all-gather.5.cloned.1.call-start = ((), (), s32[]{:S(2)}) async-start(), calls=%async_computation.10 | async-start | bytes 1114112 | tf_op jit(solution)/shard_map/all_gather | solution.py:324
  140.8 23.6 %collective-permute-start.2 = (f32[32,5,16,128]{3,2,1,0:T(8,128)S(1)}, f32[32,5,16,128]{3,2,1,0:T(8,128)S(1)}, u32[]{:S(2)}, u32[]{:S(2)}) collective-permute-start(f32[32,5,16,128]{3,2,1,0:T(8,128)S(1)} %all-to-all-done.4.mine_ref), channel_id=1, source_target_pairs={{0,1},{1,0},{2,3},{3,2},{4,5},{5,4},{6,7},{7,6},{8,9},{9,8},{10,11... | collective-permute-start | bytes 3932168 | tf_op jit(solution)/shard_map/ppermute | solution.py:321
  154.4 57.7 %all-to-all-start.5 = ((f32[32,16,1024]{2,1,0:T(8,128)}), f32[32,16,1024]{2,1,0:T(8,128)}, u32[]{:S(2)}, u32[]{:S(2)}) async-start(f32[32,16,1024]{2,1,0:T(8,128)} %bitcast.44), calls=%async_computation.5 | async-start | bytes 4194304 | tf_op jit(solution)/shard_map/all_to_all | solution.py:330
  163.8 61.2 %reduce-scatter.2.cloned.1.call-start = ((), (), s32[]{:S(2)}) async-start(), calls=%async_computation.11 | async-start | bytes 1114112 | tf_op jit(solution)/shard_map/reduce_scatter | solution.py:322
  226.1 17.5 %all-to-all-start.6 = ((f32[32,1,512]{2,1,0:T(1,128)}), f32[32,1,512]{2,1,0:T(1,128)S(1)}, u32[]{:S(2)}, u32[]{:S(2)}) async-start(f32[32,1,512]{2,1,0:T(1,128)} %reshape.164), calls=%async_computation.7 | async-start | bytes 131072 | tf_op jit(solution)/shard_map/all_to_all | solution.py:339
  234.8 0.8 copy-start.1
  246.1 16.8 %all-to-all-start.7 = ((f32[16,1,1024]{2,1,0:T(1,128)}), f32[16,1,1024]{2,1,0:T(1,128)S(1)}, u32[]{:S(2)}, u32[]{:S(2)}) async-start(f32[16,1,1024]{2,1,0:T(1,128)} %reshape.166), calls=%async_computation.8 | async-start | bytes 131072 | tf_op jit(solution)/shard_map/all_to_all | solution.py:342
Sparse Core Ops, SparseCore 0:
  33.2 38.5 all-gather.2
Sparse Core Ops, SparseCore 1:
  111.8 38.5 all-gather.4
  167.1 57.9 reduce-scatter.1

commit v7 on v6

--- a/solution.py
+++ b/solution.py
@@ -179,20 +179,23 @@
             pltpu.make_async_copy(w_ref.at[j, span, :], out_ref.at[j, span, :], sems.at[b, j]).wait()
 
 
-def solve_kernel(from_ref, u_ref, out_ref, w_ref, x_ref, sems):
+def solve_kernel(from_ref, u_ref, v_ref, out_u_ref, out_v_ref, w_ref, x_ref, sems):
     big = w_ref.shape[0]
+    n = u_ref.shape[0]
     copies = {}
     for b in range(big):
         span = pl.ds(256 * b, 256)
         for j in range(b, big):
             copies[b, j] = pltpu.make_async_copy(from_ref.at[j, span, :], w_ref.at[j, span, :], sems.at[b, j])
             copies[b, j].start()
-    x_ref[...] = u_ref[...]
+    x_ref[0:n, :] = u_ref[...]
+    x_ref[n:, :] = v_ref[...]
     for b in range(big):
         span = slice(256 * b, 256 * b + 256)
         copies[b, b].wait()
         y = mmt(x_ref[:, span], w_ref[b, span, :])
-        out_ref[:, span] = y
+        out_u_ref[:, span] = y[0:n, :]
+        out_v_ref[:, span] = y[n:, :]
         for j in range(b + 1, big):
             right = slice(256 * j, 256 * j + 256)
             copies[b, j].wait()
@@ -215,24 +218,24 @@
             pltpu.SemaphoreType.DMA((big, big)),
         ],
         compiler_params=pltpu.CompilerParams(vmem_limit_bytes=16 * 1024 * 1024),
-        cost_estimate=pl.CostEstimate(flops=40_000_000_000, transcendentals=0, bytes_accessed=8_000_000),
+        cost_estimate=pl.CostEstimate(flops=panel**3, transcendentals=0, bytes_accessed=8 * panel * panel),
     )(core, mine, other)
 
 
-def forward(w, u):
+def forward(w, u, v):
     vmem = pl.BlockSpec(memory_space=pltpu.VMEM)
     return pl.pallas_call(
         solve_kernel,
-        out_shape=jax.ShapeDtypeStruct(u.shape, jnp.float32),
-        in_specs=[pl.BlockSpec(memory_space=pltpu.HBM), vmem],
-        out_specs=vmem,
+        out_shape=[jax.ShapeDtypeStruct(u.shape, jnp.float32), jax.ShapeDtypeStruct(v.shape, jnp.float32)],
+        in_specs=[pl.BlockSpec(memory_space=pltpu.HBM), vmem, vmem],
+        out_specs=[vmem, vmem],
         scratch_shapes=[
             pltpu.VMEM(w.shape, jnp.float32),
-            pltpu.VMEM(u.shape, jnp.float32),
+            pltpu.VMEM((u.shape[0] + v.shape[0], u.shape[1]), jnp.float32),
             pltpu.SemaphoreType.DMA((w.shape[0], w.shape[0])),
         ],
         compiler_params=pltpu.CompilerParams(vmem_limit_bytes=12 * 1024 * 1024),
-    )(pltpu.with_memory_space_constraint(w, pltpu.HBM), u)
+    )(pltpu.with_memory_space_constraint(w, pltpu.HBM), u, v)
 
 
 def split_three(value):
@@ -265,11 +268,31 @@
     along_z = [[z * 2 + core for z in range(chips)] for core in range(2)]
     own = left_factor[:block_rows]
     per_col = row_count // col_count
-    strip = depth // per_col
     lane = lax.broadcasted_iota(jnp.int32, (1, panel), 1)
 
+    prev_rows, vox = solved_prev.shape
+    vox_part = vox // per_col
+    packed = jnp.concatenate([solved_prev] + split_three(right_block), axis=0)
+    pieces = []
+    for turn in range(per_col):
+        half = (row_place + turn) % per_col
+        sent = lax.dynamic_slice_in_dim(packed, half * vox_part, vox_part, 1)
+        pairs = []
+        for r in range(row_count):
+            for c in range(col_count):
+                to_row = per_col * c + (r + turn) % per_col
+                pairs.append((r * col_count + c, to_row * col_count + r // per_col))
+        pieces.append(lax.ppermute(sent, ("row", "col"), pairs))
+    flip = (row_place % per_col) == 1
+    first = jnp.where(flip, pieces[1], pieces[0])
+    second = jnp.where(flip, pieces[0], pieces[1])
+    solved_here = jnp.concatenate([first[:prev_rows], second[:prev_rows]], axis=0)
+    right_here = jnp.concatenate([first[prev_rows:], second[prev_rows:]], axis=0).astype(jnp.float32)
+    right_here = right_here.reshape(per_col, 3, block_rows, vox_part)
+    right_here = (right_here[:, 0] + right_here[:, 1] + right_here[:, 2]).reshape(col_width, vox_part)
+
+    from_y = collect(own, "row", tall, along_y)
     packed = jnp.concatenate([own] + split_three(gram_panel[:block_rows]), axis=1)
-    from_y = collect(own, "row", tall, along_y)
     packed, from_y = lax.optimization_barrier((packed, from_y))
     from_x = collect(packed, "row", wide, along_x)
     rows_x = from_x[:, :, :depth].reshape(wide * block_rows, depth)
@@ -289,57 +312,44 @@
     turned = lax.dynamic_slice_in_dim(jnp.concatenate([turned, turned], axis=0), tall - 1 - row_place // wide, tall, 0)
     thin = tall * block_rows // col_count
     partial = turned.reshape(col_count, thin, wide * block_rows)
-
-    own_late, partial_now = lax.optimization_barrier((own, partial))
-    own_diag = jnp.sum(lax.all_to_all(partial_now, "col", 0, 0), axis=0)
+    own_diag = jnp.sum(lax.all_to_all(partial, "col", 0, 0), axis=0)
     diag_z = collect(own_diag, "col", chips, along_z)
-    pieces = []
-    for turn in range(per_col):
-        half = (row_place + turn) % per_col
-        sent = lax.dynamic_slice_in_dim(own_late, half * strip, strip, 1)
-        pairs = []
-        for r in range(row_count):
-            for c in range(col_count):
-                to_row = per_col * c + (r + turn) % per_col
-                pairs.append((r * col_count + c, to_row * col_count + r // per_col))
-        pieces.append(lax.ppermute(sent, ("row", "col"), pairs))
-    flip = (row_place % per_col) == 1
-    mine = jnp.concatenate(
-        [jnp.where(flip, pieces[1], pieces[0]), jnp.where(flip, pieces[0], pieces[1])], axis=0
-    )
 
     chosen = lax.all_gather(rows_y, "row", axis=0, tiled=False, axis_index_groups=along_x)
     chosen = chosen.reshape(wide, tall, block_rows, depth).transpose(1, 0, 2, 3).reshape(panel, depth)
-    gram_placed = jnp.where(lane // col_width == col_place, jnp.tile(gram_panel, (1, col_count)), 0.0)
+    at_col = lane // col_width == col_place
+    gram_placed = jnp.where(at_col, jnp.tile(gram_panel, (1, col_count)), 0.0)
     update_part = gram_placed - lax.dot_general(
         left_factor, chosen, (((1,), (1,)), ((), ())), preferred_element_type=jnp.float32
     )
-    right_placed = jnp.where(lane // block_rows == row_place, jnp.tile(right_block.T, (1, row_count)), 0.0)
-
-    diag_z, update_part, right_placed, _ = lax.optimization_barrier((diag_z[:kept], update_part, right_placed, mine))
+    right_placed = jnp.where(at_col, jnp.tile(right_here.T, (1, col_count)), 0.0)
+    product = right_placed - lax.dot_general(
+        solved_here, chosen, (((0,), (1,)), ((), ())), preferred_element_type=jnp.float32
+    )
+
+    diag_z, update_part, product = lax.optimization_barrier((diag_z[:kept], update_part, product))
     diag_row = collect(diag_z, "row", row_count)
     other = lax.ppermute(diag_row, "col", [(i, i ^ 1) for i in range(col_count)])
     update = lax.psum_scatter(update_part, "col", scatter_dimension=0, tiled=True)
-
-    strip_piece = lax.all_gather(mine, "col", axis=0, tiled=True)
-    product = right_placed - lax.dot_general(
-        solved_prev, strip_piece, (((0,), (1,)), ((), ())), preferred_element_type=jnp.float32
-    )
-    product = product.reshape(row_count, product.shape[0] // row_count, panel)
+    product = product.reshape(col_count, vox_part // col_count, panel)
     product, _ = lax.optimization_barrier((product, diag_row))
-    spread_out = lax.all_to_all(product, "row", 0, 0)
-
-    diag_row, other, _, _ = lax.optimization_barrier((diag_row, other, update_part, product))
+    spread_out = lax.all_to_all(product, "col", 0, 0)
+
     factored = factor((col_place % 2).reshape(1), diag_row, other, panel)
-    factored, spread_out = lax.optimization_barrier((factored, spread_out))
-    vox_out = forward(factored, jnp.sum(spread_out, axis=0))
-    update, vox_out = lax.optimization_barrier((update, vox_out))
-    rows_out = forward(factored, update)
-    vox_out = vox_out.reshape(-1, row_count, block_rows).transpose(1, 0, 2)
-    solved_panel = lax.all_to_all(vox_out, "row", 0, 0).reshape(-1, block_rows).T
-    rows_out, solved_panel = lax.optimization_barrier((rows_out, solved_panel))
+    factored, spread_out, update = lax.optimization_barrier((factored, spread_out, update))
+    rows_out, vox_out = forward(factored, update, jnp.sum(spread_out, axis=0))
+
+    pairs = []
+    for r in range(row_count):
+        for c in range(col_count):
+            pairs.append((r * col_count + c, (per_col * c + r % per_col) * col_count + r // per_col))
+    vox_out = lax.ppermute(vox_out, ("row", "col"), pairs)
     rows_out = rows_out.reshape(-1, col_count, col_width).transpose(1, 0, 2)
     panel_factor = lax.all_to_all(rows_out, "col", 0, 0).reshape(-1, col_width)
+    vox_out, panel_factor = lax.optimization_barrier((vox_out, panel_factor))
+    vox_out = vox_out.reshape(-1, row_count, block_rows).transpose(1, 0, 2)
+    vox_out = lax.all_to_all(vox_out, "row", 0, 0).reshape(col_count, per_col, -1, block_rows)
+    solved_panel = vox_out.transpose(1, 0, 2, 3).reshape(vox, block_rows).T
     return (panel_factor, solved_panel)
 
 

time: 273 us -> 275 us (level)
  starting transfers between devices: 84.6 us -> 97.4 us
  Pallas kernels: 48 us -> 43.1 us
  local copies, waits for them, and re-layouts: 22.2 us -> 17.4 us
  other arithmetic: 7.12 us -> 3.57 us
  waiting for transfers between devices: 88.2 us -> 91.5 us
    all_to_all x3, waiting for transfers between devices: 13.6 us -> 38.8 us  [the longest x1 30.7 us: body(): own_diag = jnp.sum(lax.all_to_all(partial, 'col', 0, 0), axis=0)]
    all_to_all x3, starting transfers between devices: 30.4 us -> 42.7 us  [the longest x1 19.6 us: body(): own_diag = jnp.sum(lax.all_to_all(partial, 'col', 0, 0), axis=0)]
    all_to_all x4, waiting for transfers between devices: 55.4 us -> 46.6 us  [collect(): return lax.all_to_all(many, axis, 0, 0, axis_index_groups=groups)]
    reduce_scatter x1, waiting for transfers between devices: 6.27 us -> 0.02 us  [body(): lax.psum_scatter(update_part, 'col', scatter_dimension=0, tiled=True)]
    ppermute x0 -> x1, starting transfers between devices: none -> 5.01 us  [body(): vox_out = lax.ppermute(vox_out, ('row', 'col'), pairs)]
    all_gather x1 -> x0, waiting for transfers between devices: 4.92 us -> none  [body(): strip_piece = lax.all_gather(mine, 'col', axis=0, tiled=True)]
    pallas_call x2 -> x1, Pallas kernels: 9.84 us -> 4.98 us  [forward(): pl.pallas_call(solve_kernel, out_shape=[jax.ShapeDtypeStruct(u.shape, jnp...]
    all_to_all x1, waiting for transfers between devices: 7.07 us -> 2.79 us  [body(): panel_factor = lax.all_to_all(rows_out, 'col', 0, 0).reshape(-1, col_width)]
  transfers between devices with their start and end apart: 14 -> 14, of which waited for: 10 -> 7; matrix products, arithmetic and copies ran while one was open for 8% -> 4% of each run, Pallas kernels for 18% -> 14%
where the time goes in v7:
time: 275 us; the launch traced here: 273 us
  starting transfers between devices  97.4 us (35%)
  waiting for transfers between devices  91.5 us (33%)
  Pallas kernels  43.1 us (16%)
  local copies, waits for them, and re-layouts  17.4 us (6%)
  between operations  14.6 us (5%)
  matrix products  5.12 us (2%)
  other arithmetic  3.57 us (1%)
    all_to_all x4, waiting for transfers between devices, collect(): return lax.all_to_all(many, axis, 0, 0, axis_index_groups=groups)  46.6 us
    pallas_call x1, Pallas kernels, factor(): pl.pallas_call(factor_kernel, out_shape=pltpu.HBM((big, panel, 256), jnp....  38.1 us
    all_to_all x4, starting transfers between devices, collect(): return lax.all_to_all(many, axis, 0, 0, axis_index_groups=groups)  32.3 us
    all_to_all x1, waiting for transfers between devices, body(): own_diag = jnp.sum(lax.all_to_all(partial, 'col', 0, 0), axis=0)  30.7 us
    all_to_all x1, starting transfers between devices, body(): own_diag = jnp.sum(lax.all_to_all(partial, 'col', 0, 0), axis=0)  19.6 us
    all_to_all x1, starting transfers between devices, body(): lax.all_to_all(vox_out, 'row', 0, 0)  11.7 us
    all_to_all x1, starting transfers between devices, body(): spread_out = lax.all_to_all(product, 'col', 0, 0)  11.3 us
    all_to_all x1, waiting for transfers between devices, body(): lax.all_to_all(vox_out, 'row', 0, 0)  8.11 us
  transfers between devices with their start and end apart: 14, of which 7 were waited for; matrix products, arithmetic and copies ran while one was open for 4% of the time, Pallas kernels for 14%

profile of v7, /device:TPU:1, one launch (start us, length us, event | category | flops | bytes accessed | tf_op | source)
XLA Modules:
  0.0 272.7 jit_solution(11257657871903059138)
XLA Ops:
  7.2 0.9 slice.45
  8.0 0.9 broadcast_in_dim.70
  8.9 7.7 %all-to-all-start = ((bf16[8,32,1024]{2,1,0:T(8,128)(2,1)}), bf16[8,32,1024]{2,1,0:T(8,128)(2,1)S(1)}, u32[]{:S(2)}, u32[]{:S(2)}) async-start(bf16[8,32,1024]{2,1,0:T(8,128)(2,1)} %broadcast_in_dim.70), calls=%async_computation | async-start | bytes 1048576 | tf_op jit(solution)/shard_map/all_to_all | solution.py:250
  16.8 14.5 %all-to-all-done = bf16[8,32,1024]{2,1,0:T(8,128)(2,1)S(1)} async-done(((bf16[8,32,1024]{2,1,0:T(8,128)(2,1)}), bf16[8,32,1024]{2,1,0:T(8,128)(2,1)S(1)}, u32[]{:S(2)}, u32[]{:S(2)}) %all-to-all-start) | async-done | bytes 524320 | tf_op jit(solution)/shard_map/all_to_all | solution.py:250
  31.3 0.8 copy-done.1
  33.1 7.2 %all-to-all-start.1 = ((bf16[4,32,1216]{2,1,0:T(8,128)(2,1)}), bf16[4,32,1216]{2,1,0:T(8,128)(2,1)S(1)}, u32[]{:S(2)}, u32[]{:S(2)}) async-start(bf16[4,32,1216]{2,1,0:T(8,128)(2,1)} %broadcast_in_dim.71), calls=%async_computation.1 | async-start | bytes 655360 | tf_op jit(solution)/shard_map/all_to_all | solution.py:250
  40.3 5.5 %collective-permute-start = (bf16[608,256]{1,0:T(8,128)(2,1)S(1)}, bf16[608,256]{1,0:T(8,128)(2,1)S(1)}, u32[]{:S(2)}, u32[]{:S(2)}) collective-permute-start(bf16[608,256]{1,0:T(8,128)(2,1)S(1)} %get-tuple-element.36), channel_id=1, source_target_pairs={{0,16},{1,48},{2,80},{3,112},{4,144},{5,176},{6,208},{7,240},{8,27... | collective-permute-start | bytes 933896 | tf_op jit(solution)/shard_map/ppermute | solution.py:285
  45.9 2.2 collective-permute-start.1
  50.0 1.1 constant_dynamic-slice_fusion
  52.5 19.6 %all-to-all-start.2 = ((f32[16,16,128]{2,1,0:T(8,128)}), f32[16,16,128]{2,1,0:T(8,128)S(1)}, u32[]{:S(2)}, u32[]{:S(2)}) async-start(f32[16,16,128]{2,1,0:T(8,128)} %bitcast.7), calls=%async_computation.2 | async-start | bytes 262144 | tf_op jit(solution)/shard_map/all_to_all | solution.py:315
  72.1 1.0 broadcast_select_fusion.1
  73.9 30.7 %all-to-all-done.2 = f32[16,16,128]{2,1,0:T(8,128)S(1)} async-done(((f32[16,16,128]{2,1,0:T(8,128)}), f32[16,16,128]{2,1,0:T(8,128)S(1)}, u32[]{:S(2)}, u32[]{:S(2)}) %all-to-all-start.2) | async-done | bytes 131104 | tf_op jit(solution)/shard_map/all_to_all | solution.py:315
  105.3 11.9 %all-to-all-start.3 = ((f32[8,16,128]{2,1,0:T(8,128)}), f32[8,16,128]{2,1,0:T(8,128)S(1)}, u32[]{:S(2)}, u32[]{:S(2)}) async-start(f32[8,16,128]{2,1,0:T(8,128)} %broadcast_in_dim.75), calls=%async_computation.3 | async-start | bytes 131072 | tf_op jit(solution)/shard_map/all_to_all | solution.py:250
  117.3 1.3 copy.37
  118.6 6.1 %all-to-all-done.3 = f32[8,16,128]{2,1,0:T(8,128)S(1)} async-done(((f32[8,16,128]{2,1,0:T(8,128)}), f32[8,16,128]{2,1,0:T(8,128)S(1)}, u32[]{:S(2)}, u32[]{:S(2)}) %all-to-all-start.3) | async-done | bytes 65568 | tf_op jit(solution)/shard_map/all_to_all | solution.py:250
  124.8 1.9 copy.35
  126.7 1.8 fusion
  128.4 3.1 %convolution_subtract_fusion = f32[256,1024]{1,0:T(8,128)} fusion(bf16[1024,1024]{1,0:T(8,128)(2,1)S(1)} %bitcast.47, f32[256,1024]{1,0:T(8,128)} %copy.37, bf16[512,256]{1,0:T(8,128)(2,1)} %slice.72, bf16[512,256]{1,0:T(8,128)(2,1)S(1)} %slice.71, pred[1024]{0:T(1024)(128)(4,1)S(1)} %fusion.7), kind=kOutput, calls=%fused_computation.2 | convolution fusion | flops 538443776 | bytes 4719616 | tf_op jit(solution)/shard_map/dot_general | solution.py:326
  131.5 1.2 broadcast_in_dim.78
  132.6 5.6 %all-to-all-start.4 = ((f32[32,5,16,128]{3,2,1,0:T(8,128)}), f32[32,5,16,128]{3,2,1,0:T(8,128)S(1)}, u32[]{:S(2)}, u32[]{:S(2)}) async-start(f32[32,5,16,128]{3,2,1,0:T(8,128)} %broadcast_in_dim.78), calls=%async_computation.4 | async-start | bytes 2621440 | tf_op jit(solution)/shard_map/all_to_all | solution.py:250
  139.0 25.9 %all-to-all-done.4.mine_ref = f32[32,5,16,128]{3,2,1,0:T(8,128)S(1)} async-done(((f32[32,5,16,128]{3,2,1,0:T(8,128)}), f32[32,5,16,128]{3,2,1,0:T(8,128)S(1)}, u32[]{:S(2)}, u32[]{:S(2)}) %all-to-all-start.4) | async-done | bytes 1310752 | tf_op jit(solution)/shard_map/all_to_all | solution.py:250
  164.9 11.3 %all-to-all-start.5 = ((f32[16,16,1024]{2,1,0:T(8,128)}), f32[16,16,1024]{2,1,0:T(8,128)S(1)}, u32[]{:S(2)}, u32[]{:S(2)}) async-start(f32[16,16,1024]{2,1,0:T(8,128)} %bitcast.19), calls=%async_computation.5 | async-start | bytes 2097152 | tf_op jit(solution)/shard_map/all_to_all | solution.py:336
  176.2 2.3 collective-permute-start.2
  178.5 2.6 collective-permute-done.2.other_ref
  181.1 38.1 %shard_map.59.from_ref = f32[4,1024,256]{2,1,0:T(8,128)} custom-call(s32[1]{0:T(128)} %bitcast.core_ref, f32[32,5,16,128]{3,2,1,0:T(8,128)S(1)} %all-to-all-done.4.mine_ref, f32[32,5,16,128]{3,2,1,0:T(8,128)S(1)} %collective-permute-done.2.other_ref), custom_call_target="tpu_custom_call" | custom-call | flops 1073741824 | bytes 8388608 | tf_op jit(solution)/shard_map/pallas_call | solution.py:208
  219.3 0.8 copy-done
  220.2 5.0 %shard_map.60 = (f32[16,1024]{1,0:T(8,128)S(1)}, f32[16,1024]{1,0:T(8,128)S(1)}) custom-call(f32[4,1024,256]{2,1,0:T(8,128)} %shard_map.59.from_ref, f32[16,1024]{1,0:T(8,128)S(1)} %copy-done, f32[16,1024]{1,0:T(8,128)S(1)} %reduce_sum.19.v_ref), custom_call_target="tpu_custom_call" | custom-call | tf_op jit(solution)/shard_map/pallas_call | solution.py:227
  226.1 7.3 %all-to-all-start.6 = ((f32[16,1,1024]{2,1,0:T(1,128)}), f32[16,1,1024]{2,1,0:T(1,128)S(1)}, u32[]{:S(2)}, u32[]{:S(2)}) async-start(f32[16,1,1024]{2,1,0:T(1,128)} %reshape.145), calls=%async_computation.7 | async-start | bytes 131072 | tf_op jit(solution)/shard_map/all_to_all | solution.py:348
  233.3 5.0 %collective-permute-start.3 = (f32[16,1024]{1,0:T(8,128)S(1)}, f32[16,1024]{1,0:T(8,128)S(1)}, u32[]{:S(2)}, u32[]{:S(2)}) collective-permute-start(f32[16,1024]{1,0:T(8,128)S(1)} %get-tuple-element.24), channel_id=1, source_target_pairs={{0,0},{1,32},{2,64},{3,96},{4,128},{5,160},{6,192},{7,224},{8,256}... | collective-permute-start | bytes 196616 | tf_op jit(solution)/shard_map/ppermute | solution.py:346
  238.4 2.8 %all-to-all-done.6 = f32[16,1,1024]{2,1,0:T(1,128)S(1)} async-done(((f32[16,1,1024]{2,1,0:T(1,128)}), f32[16,1,1024]{2,1,0:T(1,128)S(1)}, u32[]{:S(2)}, u32[]{:S(2)}) %all-to-all-start.6) | async-done | bytes 65568 | tf_op jit(solution)/shard_map/all_to_all | solution.py:348
  243.6 11.7 %all-to-all-start.7 = ((f32[32,1,512]{2,1,0:T(1,128)}), f32[32,1,512]{2,1,0:T(1,128)S(1)}, u32[]{:S(2)}, u32[]{:S(2)}) async-start(f32[32,1,512]{2,1,0:T(1,128)} %reshape.147), calls=%async_computation.8 | async-start | bytes 131072 | tf_op jit(solution)/shard_map/all_to_all | solution.py:351
  256.1 8.1 %all-to-all-done.7 = f32[32,1,512]{2,1,0:T(1,128)S(1)} async-done(((f32[32,1,512]{2,1,0:T(1,128)}), f32[32,1,512]{2,1,0:T(1,128)S(1)}, u32[]{:S(2)}, u32[]{:S(2)}) %all-to-all-start.7) | async-done | bytes 65568 | tf_op jit(solution)/shard_map/all_to_all | solution.py:351
  (80 shorter events, 12.3 us)
Async XLA Ops:
  7.2 9.5 %slice-start.1 = ((f32[256,64]{0,1:T(8,128)}), f32[32,64]{0,1:T(8,128)S(1)}, s32[]{:S(2)}) async-start(f32[256,64]{0,1:T(8,128)} %param.4), calls=%async_computation.12 | async-start | bytes 65536 | tf_op jit(solution)/shard_map/slice | solution.py:295
  8.0 24.2 %copy-start.7 = (f32[32,512]{1,0:T(8,128)S(1)}, f32[32,512]{1,0:T(8,128)}, u32[]{:S(2)}) copy-start(f32[32,512]{1,0:T(8,128)} %param.7) | copy-start | bytes 196612
  8.0 24.2 %copy-start.4 = (bf16[512,512]{1,0:T(8,128)(2,1)S(1)}, bf16[512,512]{1,0:T(8,128)(2,1)}, u32[]{:S(2)}) copy-start(bf16[512,512]{1,0:T(8,128)(2,1)} %param.6) | copy-start | bytes 1572868
  8.9 22.4 %all-to-all-start = ((bf16[8,32,1024]{2,1,0:T(8,128)(2,1)}), bf16[8,32,1024]{2,1,0:T(8,128)(2,1)S(1)}, u32[]{:S(2)}, u32[]{:S(2)}) async-start(bf16[8,32,1024]{2,1,0:T(8,128)(2,1)} %broadcast_in_dim.70), calls=%async_computation | async-start | bytes 1048576 | tf_op jit(solution)/shard_map/all_to_all | solution.py:250
  16.6 108.2 %all-gather.2.cloned.1.call-start = ((), (), s32[]{:S(2)}) async-start(), calls=%async_computation.9 | async-start | bytes 2621440 | tf_op jit(solution)/shard_map/all_gather | solution.py:318
  31.3 0.8 copy-start.1
  32.3 16.0 %copy-start.6 = (f32[256,64]{0,1:T(8,128)S(1)}, f32[256,64]{0,1:T(8,128)}, u32[]{:S(2)}) copy-start(f32[256,64]{0,1:T(8,128)} %param.4) | copy-start | bytes 196612
  33.1 15.7 %all-to-all-start.1 = ((bf16[4,32,1216]{2,1,0:T(8,128)(2,1)}), bf16[4,32,1216]{2,1,0:T(8,128)(2,1)S(1)}, u32[]{:S(2)}, u32[]{:S(2)}) async-start(bf16[4,32,1216]{2,1,0:T(8,128)(2,1)} %broadcast_in_dim.71), calls=%async_computation.1 | async-start | bytes 655360 | tf_op jit(solution)/shard_map/all_to_all | solution.py:250
  40.3 31.8 %collective-permute-start = (bf16[608,256]{1,0:T(8,128)(2,1)S(1)}, bf16[608,256]{1,0:T(8,128)(2,1)S(1)}, u32[]{:S(2)}, u32[]{:S(2)}) collective-permute-start(bf16[608,256]{1,0:T(8,128)(2,1)S(1)} %get-tuple-element.36), channel_id=1, source_target_pairs={{0,16},{1,48},{2,80},{3,112},{4,144},{5,176},{6,208},{7,240},{8,27... | collective-permute-start | bytes 933896 | tf_op jit(solution)/shard_map/ppermute | solution.py:285
  45.9 26.2 %collective-permute-start.1 = (bf16[608,256]{1,0:T(8,128)(2,1)S(1)}, bf16[608,256]{1,0:T(8,128)(2,1)}, u32[]{:S(2)}, u32[]{:S(2)}) collective-permute-start(bf16[608,256]{1,0:T(8,128)(2,1)S(1)} %get-tuple-element.37), channel_id=1, source_target_pairs={{0,0},{1,32},{2,64},{3,96},{4,128},{5,160},{6,192},{7,224},{8,256}... | collective-permute-start | bytes 933896 | tf_op jit(solution)/shard_map/ppermute | solution.py:285
  48.8 2.6 copy-start.2
  52.5 52.2 %all-to-all-start.2 = ((f32[16,16,128]{2,1,0:T(8,128)}), f32[16,16,128]{2,1,0:T(8,128)S(1)}, u32[]{:S(2)}, u32[]{:S(2)}) async-start(f32[16,16,128]{2,1,0:T(8,128)} %bitcast.7), calls=%async_computation.2 | async-start | bytes 262144 | tf_op jit(solution)/shard_map/all_to_all | solution.py:315
  105.3 19.5 %all-to-all-start.3 = ((f32[8,16,128]{2,1,0:T(8,128)}), f32[8,16,128]{2,1,0:T(8,128)S(1)}, u32[]{:S(2)}, u32[]{:S(2)}) async-start(f32[8,16,128]{2,1,0:T(8,128)} %broadcast_in_dim.75), calls=%async_computation.3 | async-start | bytes 131072 | tf_op jit(solution)/shard_map/all_to_all | solution.py:250
  124.8 1.9 copy-start.5
  124.8 1.9 copy-start.3
  128.4 3.1 %slice-start = ((f32[8,16,128]{2,1,0:T(8,128)}), f32[5,16,128]{2,1,0:T(8,128)S(1)}, s32[]{:S(2)}) async-start(f32[8,16,128]{2,1,0:T(8,128)} %copy-done.5), calls=%async_computation.11 | async-start | bytes 81920 | tf_op jit(solution)/shard_map/slice | solution.py:330
  132.6 32.2 %all-to-all-start.4 = ((f32[32,5,16,128]{3,2,1,0:T(8,128)}), f32[32,5,16,128]{3,2,1,0:T(8,128)S(1)}, u32[]{:S(2)}, u32[]{:S(2)}) async-start(f32[32,5,16,128]{3,2,1,0:T(8,128)} %broadcast_in_dim.78), calls=%async_computation.4 | async-start | bytes 2621440 | tf_op jit(solution)/shard_map/all_to_all | solution.py:250
  138.2 81.0 %reduce-scatter.2.cloned.1.call-start = ((), (), s32[]{:S(2)}) async-start(), calls=%async_computation.10 | async-start | bytes 1114112 | tf_op jit(solution)/shard_map/reduce_scatter | solution.py:333
  164.9 54.4 %all-to-all-start.5 = ((f32[16,16,1024]{2,1,0:T(8,128)}), f32[16,16,1024]{2,1,0:T(8,128)S(1)}, u32[]{:S(2)}, u32[]{:S(2)}) async-start(f32[16,16,1024]{2,1,0:T(8,128)} %bitcast.19), calls=%async_computation.5 | async-start | bytes 2097152 | tf_op jit(solution)/shard_map/all_to_all | solution.py:336
  176.2 4.9 %collective-permute-start.2 = (f32[32,5,16,128]{3,2,1,0:T(8,128)S(1)}, f32[32,5,16,128]{3,2,1,0:T(8,128)S(1)}, u32[]{:S(2)}, u32[]{:S(2)}) collective-permute-start(f32[32,5,16,128]{3,2,1,0:T(8,128)S(1)} %all-to-all-done.4.mine_ref), channel_id=1, source_target_pairs={{0,1},{1,0},{2,3},{3,2},{4,5},{5,4},{6,7},{7,6},{8,9},{9,8},{10,11... | collective-permute-start | bytes 3932168 | tf_op jit(solution)/shard_map/ppermute | solution.py:332
  219.3 0.8 copy-start
  226.1 15.1 %all-to-all-start.6 = ((f32[16,1,1024]{2,1,0:T(1,128)}), f32[16,1,1024]{2,1,0:T(1,128)S(1)}, u32[]{:S(2)}, u32[]{:S(2)}) async-start(f32[16,1,1024]{2,1,0:T(1,128)} %reshape.145), calls=%async_computation.7 | async-start | bytes 131072 | tf_op jit(solution)/shard_map/all_to_all | solution.py:348
  233.3 9.2 %collective-permute-start.3 = (f32[16,1024]{1,0:T(8,128)S(1)}, f32[16,1024]{1,0:T(8,128)S(1)}, u32[]{:S(2)}, u32[]{:S(2)}) collective-permute-start(f32[16,1024]{1,0:T(8,128)S(1)} %get-tuple-element.24), channel_id=1, source_target_pairs={{0,0},{1,32},{2,64},{3,96},{4,128},{5,160},{6,192},{7,224},{8,256}... | collective-permute-start | bytes 196616 | tf_op jit(solution)/shard_map/ppermute | solution.py:346
  243.6 20.6 %all-to-all-start.7 = ((f32[32,1,512]{2,1,0:T(1,128)}), f32[32,1,512]{2,1,0:T(1,128)S(1)}, u32[]{:S(2)}, u32[]{:S(2)}) async-start(f32[32,1,512]{2,1,0:T(1,128)} %reshape.147), calls=%async_computation.8 | async-start | bytes 131072 | tf_op jit(solution)/shard_map/all_to_all | solution.py:351
Sparse Core Ops, SparseCore 0:
  32.3 40.7 all-gather.1
  141.9 67.0 reduce-scatter.1

commit v8 on v7

--- a/solution.py
+++ b/solution.py
@@ -273,16 +273,24 @@
     prev_rows, vox = solved_prev.shape
     vox_part = vox // per_col
     packed = jnp.concatenate([solved_prev] + split_three(right_block), axis=0)
-    pieces = []
+    spread = 2
+    piece_vox = vox_part // spread
+    sends = []
+    routes = []
     for turn in range(per_col):
         half = (row_place + turn) % per_col
-        sent = lax.dynamic_slice_in_dim(packed, half * vox_part, vox_part, 1)
-        pairs = []
-        for r in range(row_count):
-            for c in range(col_count):
-                to_row = per_col * c + (r + turn) % per_col
-                pairs.append((r * col_count + c, to_row * col_count + r // per_col))
-        pieces.append(lax.ppermute(sent, ("row", "col"), pairs))
+        for q in range(spread):
+            sends.append(lax.dynamic_slice_in_dim(packed, half * vox_part + q * piece_vox, piece_vox, 1))
+            pairs = []
+            for r in range(row_count):
+                for c in range(col_count):
+                    to_row = per_col * c + (r + turn) % per_col + q * (row_count // spread)
+                    pairs.append((r * col_count + c, to_row % row_count * col_count + r // per_col))
+            routes.append(pairs)
+    own, *sends = lax.optimization_barrier((own, *sends))
+    parts = [lax.ppermute(sent, ("row", "col"), pairs) for sent, pairs in zip(sends, routes)]
+    from_y, *parts = lax.optimization_barrier((collect(own, "row", tall, along_y), *parts))
+    pieces = [jnp.concatenate(parts[turn * spread:(turn + 1) * spread], axis=1) for turn in range(per_col)]
     flip = (row_place % per_col) == 1
     first = jnp.where(flip, pieces[1], pieces[0])
     second = jnp.where(flip, pieces[0], pieces[1])
@@ -291,7 +299,6 @@
     right_here = right_here.reshape(per_col, 3, block_rows, vox_part)
     right_here = (right_here[:, 0] + right_here[:, 1] + right_here[:, 2]).reshape(col_width, vox_part)
 
-    from_y = collect(own, "row", tall, along_y)
     packed = jnp.concatenate([own] + split_three(gram_panel[:block_rows]), axis=1)
     packed, from_y = lax.optimization_barrier((packed, from_y))
     from_x = collect(packed, "row", wide, along_x)
@@ -342,14 +349,14 @@
     pairs = []
     for r in range(row_count):
         for c in range(col_count):
-            pairs.append((r * col_count + c, (per_col * c + r % per_col) * col_count + r // per_col))
+            from_row = (r - c * spread // col_count * (row_count // spread)) % row_count
+            pairs.append((r * col_count + c, (r % per_col * col_count + c) * col_count + from_row // per_col))
     vox_out = lax.ppermute(vox_out, ("row", "col"), pairs)
     rows_out = rows_out.reshape(-1, col_count, col_width).transpose(1, 0, 2)
     panel_factor = lax.all_to_all(rows_out, "col", 0, 0).reshape(-1, col_width)
     vox_out, panel_factor = lax.optimization_barrier((vox_out, panel_factor))
     vox_out = vox_out.reshape(-1, row_count, block_rows).transpose(1, 0, 2)
-    vox_out = lax.all_to_all(vox_out, "row", 0, 0).reshape(col_count, per_col, -1, block_rows)
-    solved_panel = vox_out.transpose(1, 0, 2, 3).reshape(vox, block_rows).T
+    solved_panel = lax.all_to_all(vox_out, "row", 0, 0).reshape(vox, block_rows).T
     return (panel_factor, solved_panel)
 
 

time: 275 us -> 264 us (0.960)
  waiting for transfers between devices: 91.5 us -> 81.7 us
    all_to_all x1, waiting for transfers between devices: 30.7 us -> 8.3 us  [body(): own_diag = jnp.sum(lax.all_to_all(partial, 'col', 0, 0), axis=0)]
    ppermute x2 -> x4, starting transfers between devices: 7.74 us -> 29.1 us  [body(): lax.ppermute(sent, ('row', 'col'), pairs)]
    ppermute x2 -> x4, waiting for transfers between devices: 0.01 us -> 14.1 us  [body(): lax.ppermute(sent, ('row', 'col'), pairs)]
    all_to_all x4, starting transfers between devices: 32.3 us -> 21.9 us  [collect(): return lax.all_to_all(many, axis, 0, 0, axis_index_groups=groups)]
    all_to_all x1, starting transfers between devices: 19.6 us -> 13 us  [body(): own_diag = jnp.sum(lax.all_to_all(partial, 'col', 0, 0), axis=0)]
    all_to_all x1, starting transfers between devices: 11.3 us -> 6.67 us  [body(): spread_out = lax.all_to_all(product, 'col', 0, 0)]
    all_to_all x4, waiting for transfers between devices: 46.6 us -> 43 us  [collect(): return lax.all_to_all(many, axis, 0, 0, axis_index_groups=groups)]
  transfers between devices with their start and end apart: 14 -> 16, of which waited for: 7 -> 8; matrix products, arithmetic and copies ran while one was open for 4% -> 3% of each run, Pallas kernels for 14% -> 15%
where the time goes in v8:
time: 264 us; the launch traced here: 261 us
  starting transfers between devices  95.7 us (36%)
  waiting for transfers between devices  81.7 us (31%)
  Pallas kernels  43.1 us (16%)
  local copies, waits for them, and re-layouts  16 us (6%)
  between operations  14.6 us (6%)
  matrix products  5.14 us (2%)
  other arithmetic  4.64 us (2%)
    all_to_all x4, waiting for transfers between devices, collect(): return lax.all_to_all(many, axis, 0, 0, axis_index_groups=groups)  43 us
    pallas_call x1, Pallas kernels, factor(): pl.pallas_call(factor_kernel, out_shape=pltpu.HBM((big, panel, 256), jnp....  38.1 us
    ppermute x4, starting transfers between devices, body(): lax.ppermute(sent, ('row', 'col'), pairs)  29.1 us
    all_to_all x4, starting transfers between devices, collect(): return lax.all_to_all(many, axis, 0, 0, axis_index_groups=groups)  21.9 us
    ppermute x4, waiting for transfers between devices, body(): lax.ppermute(sent, ('row', 'col'), pairs)  14.1 us
    all_to_all x1, starting transfers between devices, body(): own_diag = jnp.sum(lax.all_to_all(partial, 'col', 0, 0), axis=0)  13 us
    all_to_all x1, starting transfers between devices, body(): lax.all_to_all(vox_out, 'row', 0, 0).reshape(vox, block_rows)  11.9 us
    all_to_all x1, waiting for transfers between devices, body(): lax.all_to_all(vox_out, 'row', 0, 0).reshape(vox, block_rows)  8.62 us
  transfers between devices with their start and end apart: 16, of which 8 were waited for; matrix products, arithmetic and copies ran while one was open for 3% of the time, Pallas kernels for 15%

profile of v8, /device:TPU:1, one launch (start us, length us, event | category | flops | bytes accessed | tf_op | source)
XLA Modules:
  0.0 261.0 jit_solution(2504288479181136764)
XLA Ops:
  8.0 0.9 reduce-precision_convert_fusion.1
  8.9 1.1 pad_maximum_fusion
  10.2 0.9 broadcast_in_dim.70
  11.0 7.7 %all-to-all-start = ((bf16[8,32,1024]{2,1,0:T(8,128)(2,1)}), bf16[8,32,1024]{2,1,0:T(8,128)(2,1)S(1)}, u32[]{:S(2)}, u32[]{:S(2)}) async-start(bf16[8,32,1024]{2,1,0:T(8,128)(2,1)} %broadcast_in_dim.70), calls=%async_computation | async-start | bytes 1048576 | tf_op jit(solution)/shard_map/all_to_all | solution.py:250
  18.7 5.5 %collective-permute-start = (bf16[608,128]{1,0:T(8,128)(2,1)S(1)}, bf16[608,128]{1,0:T(8,128)(2,1)S(1)}, u32[]{:S(2)}, u32[]{:S(2)}) collective-permute-start(bf16[608,128]{1,0:T(8,128)(2,1)S(1)} %get-tuple-element.26), channel_id=1, source_target_pairs={{0,0},{1,32},{2,64},{3,96},{4,128},{5,160},{6,192},{7,224},{8,256}... | collective-permute-start | bytes 466952 | tf_op jit(solution)/shard_map/ppermute | solution.py:291
  24.2 14.8 %collective-permute-start.1 = (bf16[608,128]{1,0:T(8,128)(2,1)S(1)}, bf16[608,128]{1,0:T(8,128)(2,1)S(1)}, u32[]{:S(2)}, u32[]{:S(2)}) collective-permute-start(bf16[608,128]{1,0:T(8,128)(2,1)S(1)} %get-tuple-element.27), channel_id=1, source_target_pairs={{0,256},{1,288},{2,320},{3,352},{4,384},{5,416},{6,448},{7,480},{8... | collective-permute-start | bytes 466952 | tf_op jit(solution)/shard_map/ppermute | solution.py:291
  39.1 5.2 %collective-permute-start.2 = (bf16[608,128]{1,0:T(8,128)(2,1)S(1)}, bf16[608,128]{1,0:T(8,128)(2,1)S(1)}, u32[]{:S(2)}, u32[]{:S(2)}) collective-permute-start(bf16[608,128]{1,0:T(8,128)(2,1)S(1)} %get-tuple-element.28), channel_id=1, source_target_pairs={{0,16},{1,48},{2,80},{3,112},{4,144},{5,176},{6,208},{7,240},{8,27... | collective-permute-start | bytes 466952 | tf_op jit(solution)/shard_map/ppermute | solution.py:291
  44.3 3.6 %collective-permute-start.3 = (bf16[608,128]{1,0:T(8,128)(2,1)S(1)}, bf16[608,128]{1,0:T(8,128)(2,1)S(1)}, u32[]{:S(2)}, u32[]{:S(2)}) collective-permute-start(bf16[608,128]{1,0:T(8,128)(2,1)S(1)} %get-tuple-element.29), channel_id=1, source_target_pairs={{0,272},{1,304},{2,336},{3,368},{4,400},{5,432},{6,464},{7,496},{8... | collective-permute-start | bytes 466952 | tf_op jit(solution)/shard_map/ppermute | solution.py:291
  48.1 14.1 %collective-permute-done.3 = bf16[608,128]{1,0:T(8,128)(2,1)S(1)} collective-permute-done((bf16[608,128]{1,0:T(8,128)(2,1)S(1)}, bf16[608,128]{1,0:T(8,128)(2,1)S(1)}, u32[]{:S(2)}, u32[]{:S(2)}) %collective-permute-start.3) | collective-permute-done | bytes 155680 | tf_op jit(solution)/shard_map/ppermute | solution.py:291
  64.5 3.5 %all-to-all-start.1 = ((bf16[4,32,1216]{2,1,0:T(8,128)(2,1)}), bf16[4,32,1216]{2,1,0:T(8,128)(2,1)S(1)}, u32[]{:S(2)}, u32[]{:S(2)}) async-start(bf16[4,32,1216]{2,1,0:T(8,128)(2,1)} %broadcast_in_dim.71), calls=%async_computation.1 | async-start | bytes 655360 | tf_op jit(solution)/shard_map/all_to_all | solution.py:250
  68.1 6.2 %all-to-all-done.1 = bf16[4,32,1216]{2,1,0:T(8,128)(2,1)S(1)} async-done(((bf16[4,32,1216]{2,1,0:T(8,128)(2,1)}), bf16[4,32,1216]{2,1,0:T(8,128)(2,1)S(1)}, u32[]{:S(2)}, u32[]{:S(2)}) %all-to-all-start.1) | async-done | bytes 311328 | tf_op jit(solution)/shard_map/all_to_all | solution.py:250
  76.4 13.0 %all-to-all-start.2 = ((f32[16,16,128]{2,1,0:T(8,128)}), f32[16,16,128]{2,1,0:T(8,128)S(1)}, u32[]{:S(2)}, u32[]{:S(2)}) async-start(f32[16,16,128]{2,1,0:T(8,128)} %bitcast.7), calls=%async_computation.2 | async-start | bytes 262144 | tf_op jit(solution)/shard_map/all_to_all | solution.py:322
  90.3 8.3 %all-to-all-done.2 = f32[16,16,128]{2,1,0:T(8,128)S(1)} async-done(((f32[16,16,128]{2,1,0:T(8,128)}), f32[16,16,128]{2,1,0:T(8,128)S(1)}, u32[]{:S(2)}, u32[]{:S(2)}) %all-to-all-start.2) | async-done | bytes 131104 | tf_op jit(solution)/shard_map/all_to_all | solution.py:322
  99.2 3.4 %all-to-all-start.3 = ((f32[8,16,128]{2,1,0:T(8,128)}), f32[8,16,128]{2,1,0:T(8,128)S(1)}, u32[]{:S(2)}, u32[]{:S(2)}) async-start(f32[8,16,128]{2,1,0:T(8,128)} %broadcast_in_dim.75), calls=%async_computation.3 | async-start | bytes 131072 | tf_op jit(solution)/shard_map/all_to_all | solution.py:250
  102.7 1.3 copy.37
  104.1 6.3 %all-to-all-done.3 = f32[8,16,128]{2,1,0:T(8,128)S(1)} async-done(((f32[8,16,128]{2,1,0:T(8,128)}), f32[8,16,128]{2,1,0:T(8,128)S(1)}, u32[]{:S(2)}, u32[]{:S(2)}) %all-to-all-start.3) | async-done | bytes 65568 | tf_op jit(solution)/shard_map/all_to_all | solution.py:250
  110.3 1.9 copy.35
  112.2 1.8 fusion
  114.0 3.1 %convolution_subtract_fusion = f32[256,1024]{1,0:T(8,128)} fusion(bf16[1024,1024]{1,0:T(8,128)(2,1)S(1)} %bitcast.44, f32[256,1024]{1,0:T(8,128)} %copy.37, bf16[512,256]{1,0:T(8,128)(2,1)} %slice.72, bf16[512,256]{1,0:T(8,128)(2,1)S(1)} %slice.71, pred[1024]{0:T(1024)(128)(4,1)S(1)} %fusion.7), kind=kOutput, calls=%fused_computation.2 | convolution fusion | flops 538443776 | bytes 4719616 | tf_op jit(solution)/shard_map/dot_general | solution.py:333
  117.1 1.2 broadcast_in_dim.78
  118.2 7.4 %all-to-all-start.4 = ((f32[32,5,16,128]{3,2,1,0:T(8,128)}), f32[32,5,16,128]{3,2,1,0:T(8,128)S(1)}, u32[]{:S(2)}, u32[]{:S(2)}) async-start(f32[32,5,16,128]{3,2,1,0:T(8,128)} %broadcast_in_dim.78), calls=%async_computation.4 | async-start | bytes 2621440 | tf_op jit(solution)/shard_map/all_to_all | solution.py:250
  126.4 30.5 %all-to-all-done.4.mine_ref = f32[32,5,16,128]{3,2,1,0:T(8,128)S(1)} async-done(((f32[32,5,16,128]{3,2,1,0:T(8,128)}), f32[32,5,16,128]{3,2,1,0:T(8,128)S(1)}, u32[]{:S(2)}, u32[]{:S(2)}) %all-to-all-start.4) | async-done | bytes 1310752 | tf_op jit(solution)/shard_map/all_to_all | solution.py:250
  157.0 6.7 %all-to-all-start.5 = ((f32[16,16,1024]{2,1,0:T(8,128)}), f32[16,16,1024]{2,1,0:T(8,128)S(1)}, u32[]{:S(2)}, u32[]{:S(2)}) async-start(f32[16,16,1024]{2,1,0:T(8,128)} %bitcast.19), calls=%async_computation.5 | async-start | bytes 2097152 | tf_op jit(solution)/shard_map/all_to_all | solution.py:343
  163.7 2.3 collective-permute-start.4
  166.0 2.6 collective-permute-done.4.other_ref
  168.6 38.1 %shard_map.59.from_ref = f32[4,1024,256]{2,1,0:T(8,128)} custom-call(s32[1]{0:T(128)} %bitcast.core_ref, f32[32,5,16,128]{3,2,1,0:T(8,128)S(1)} %all-to-all-done.4.mine_ref, f32[32,5,16,128]{3,2,1,0:T(8,128)S(1)} %collective-permute-done.4.other_ref), custom_call_target="tpu_custom_call" | custom-call | flops 1073741824 | bytes 8388608 | tf_op jit(solution)/shard_map/pallas_call | solution.py:208
  207.6 5.0 %shard_map.60 = (f32[16,1024]{1,0:T(8,128)S(1)}, f32[16,1024]{1,0:T(8,128)S(1)}) custom-call(f32[4,1024,256]{2,1,0:T(8,128)} %shard_map.59.from_ref, f32[16,1024]{1,0:T(8,128)S(1)} %copy-done, f32[16,1024]{1,0:T(8,128)S(1)} %reduce_sum.19.v_ref), custom_call_target="tpu_custom_call" | custom-call | tf_op jit(solution)/shard_map/pallas_call | solution.py:227
  213.5 7.3 %all-to-all-start.6 = ((f32[16,1,1024]{2,1,0:T(1,128)}), f32[16,1,1024]{2,1,0:T(1,128)S(1)}, u32[]{:S(2)}, u32[]{:S(2)}) async-start(f32[16,1,1024]{2,1,0:T(1,128)} %reshape.141), calls=%async_computation.7 | async-start | bytes 131072 | tf_op jit(solution)/shard_map/all_to_all | solution.py:356
  220.8 3.5 %collective-permute-start.5 = (f32[16,1024]{1,0:T(8,128)S(1)}, f32[16,1024]{1,0:T(8,128)S(1)}, u32[]{:S(2)}, u32[]{:S(2)}) collective-permute-start(f32[16,1024]{1,0:T(8,128)S(1)} %get-tuple-element.44), channel_id=1, source_target_pairs={{0,0},{1,16},{2,32},{3,48},{4,64},{5,80},{6,96},{7,112},{8,136},{9... | collective-permute-start | bytes 196616 | tf_op jit(solution)/shard_map/ppermute | solution.py:354
  224.3 4.3 %all-to-all-done.6 = f32[16,1,1024]{2,1,0:T(1,128)S(1)} async-done(((f32[16,1,1024]{2,1,0:T(1,128)}), f32[16,1,1024]{2,1,0:T(1,128)S(1)}, u32[]{:S(2)}, u32[]{:S(2)}) %all-to-all-start.6) | async-done | bytes 65568 | tf_op jit(solution)/shard_map/all_to_all | solution.py:356
  231.2 11.9 %all-to-all-start.7 = ((f32[32,1,512]{2,1,0:T(1,128)}), f32[32,1,512]{2,1,0:T(1,128)S(1)}, u32[]{:S(2)}, u32[]{:S(2)}) async-start(f32[32,1,512]{2,1,0:T(1,128)} %reshape.143), calls=%async_computation.8 | async-start | bytes 131072 | tf_op jit(solution)/shard_map/all_to_all | solution.py:359
  243.8 8.6 %all-to-all-done.7 = f32[32,1,512]{2,1,0:T(1,128)S(1)} async-done(((f32[32,1,512]{2,1,0:T(1,128)}), f32[32,1,512]{2,1,0:T(1,128)S(1)}, u32[]{:S(2)}, u32[]{:S(2)}) %all-to-all-start.7) | async-done | bytes 65568 | tf_op jit(solution)/shard_map/all_to_all | solution.py:359
  (82 shorter events, 14.6 us)
Async XLA Ops:
  10.0 37.9 %slice-start.1 = ((f32[256,64]{0,1:T(8,128)}), f32[32,64]{0,1:T(8,128)S(1)}, s32[]{:S(2)}) async-start(f32[256,64]{0,1:T(8,128)} %param.4), calls=%async_computation.12 | async-start | bytes 65536 | tf_op jit(solution)/shard_map/slice | solution.py:302
  10.2 53.1 %copy-start.5 = (f32[256,64]{0,1:T(8,128)S(1)}, f32[256,64]{0,1:T(8,128)}, u32[]{:S(2)}) copy-start(f32[256,64]{0,1:T(8,128)} %param.4) | copy-start | bytes 196612
  11.0 51.1 %all-to-all-start = ((bf16[8,32,1024]{2,1,0:T(8,128)(2,1)}), bf16[8,32,1024]{2,1,0:T(8,128)(2,1)S(1)}, u32[]{:S(2)}, u32[]{:S(2)}) async-start(bf16[8,32,1024]{2,1,0:T(8,128)(2,1)} %broadcast_in_dim.70), calls=%async_computation | async-start | bytes 1048576 | tf_op jit(solution)/shard_map/all_to_all | solution.py:250
  18.7 91.6 %all-gather.2.cloned.1.call-start = ((), (), s32[]{:S(2)}) async-start(), calls=%async_computation.9 | async-start | bytes 2621440 | tf_op jit(solution)/shard_map/all_gather | solution.py:325
  18.7 29.3 %collective-permute-start = (bf16[608,128]{1,0:T(8,128)(2,1)S(1)}, bf16[608,128]{1,0:T(8,128)(2,1)S(1)}, u32[]{:S(2)}, u32[]{:S(2)}) collective-permute-start(bf16[608,128]{1,0:T(8,128)(2,1)S(1)} %get-tuple-element.26), channel_id=1, source_target_pairs={{0,0},{1,32},{2,64},{3,96},{4,128},{5,160},{6,192},{7,224},{8,256}... | collective-permute-start | bytes 466952 | tf_op jit(solution)/shard_map/ppermute | solution.py:291
  24.2 23.8 %collective-permute-start.1 = (bf16[608,128]{1,0:T(8,128)(2,1)S(1)}, bf16[608,128]{1,0:T(8,128)(2,1)S(1)}, u32[]{:S(2)}, u32[]{:S(2)}) collective-permute-start(bf16[608,128]{1,0:T(8,128)(2,1)S(1)} %get-tuple-element.27), channel_id=1, source_target_pairs={{0,256},{1,288},{2,320},{3,352},{4,384},{5,416},{6,448},{7,480},{8... | collective-permute-start | bytes 466952 | tf_op jit(solution)/shard_map/ppermute | solution.py:291
  39.1 9.0 %collective-permute-start.2 = (bf16[608,128]{1,0:T(8,128)(2,1)S(1)}, bf16[608,128]{1,0:T(8,128)(2,1)S(1)}, u32[]{:S(2)}, u32[]{:S(2)}) collective-permute-start(bf16[608,128]{1,0:T(8,128)(2,1)S(1)} %get-tuple-element.28), channel_id=1, source_target_pairs={{0,16},{1,48},{2,80},{3,112},{4,144},{5,176},{6,208},{7,240},{8,27... | collective-permute-start | bytes 466952 | tf_op jit(solution)/shard_map/ppermute | solution.py:291
  44.3 17.9 %collective-permute-start.3 = (bf16[608,128]{1,0:T(8,128)(2,1)S(1)}, bf16[608,128]{1,0:T(8,128)(2,1)S(1)}, u32[]{:S(2)}, u32[]{:S(2)}) collective-permute-start(bf16[608,128]{1,0:T(8,128)(2,1)S(1)} %get-tuple-element.29), channel_id=1, source_target_pairs={{0,272},{1,304},{2,336},{3,368},{4,400},{5,432},{6,464},{7,496},{8... | collective-permute-start | bytes 466952 | tf_op jit(solution)/shard_map/ppermute | solution.py:291
  62.2 0.8 copy-start.1
  64.5 9.8 %all-to-all-start.1 = ((bf16[4,32,1216]{2,1,0:T(8,128)(2,1)}), bf16[4,32,1216]{2,1,0:T(8,128)(2,1)S(1)}, u32[]{:S(2)}, u32[]{:S(2)}) async-start(bf16[4,32,1216]{2,1,0:T(8,128)(2,1)} %broadcast_in_dim.71), calls=%async_computation.1 | async-start | bytes 655360 | tf_op jit(solution)/shard_map/all_to_all | solution.py:250
  74.3 1.0 copy-start.2
  76.4 22.2 %all-to-all-start.2 = ((f32[16,16,128]{2,1,0:T(8,128)}), f32[16,16,128]{2,1,0:T(8,128)S(1)}, u32[]{:S(2)}, u32[]{:S(2)}) async-start(f32[16,16,128]{2,1,0:T(8,128)} %bitcast.7), calls=%async_computation.2 | async-start | bytes 262144 | tf_op jit(solution)/shard_map/all_to_all | solution.py:322
  99.2 11.1 %all-to-all-start.3 = ((f32[8,16,128]{2,1,0:T(8,128)}), f32[8,16,128]{2,1,0:T(8,128)S(1)}, u32[]{:S(2)}, u32[]{:S(2)}) async-start(f32[8,16,128]{2,1,0:T(8,128)} %broadcast_in_dim.75), calls=%async_computation.3 | async-start | bytes 131072 | tf_op jit(solution)/shard_map/all_to_all | solution.py:250
  110.3 1.9 copy-start.4
  110.3 1.9 copy-start.3
  114.0 3.1 %slice-start = ((f32[8,16,128]{2,1,0:T(8,128)}), f32[5,16,128]{2,1,0:T(8,128)S(1)}, s32[]{:S(2)}) async-start(f32[8,16,128]{2,1,0:T(8,128)} %copy-done.4), calls=%async_computation.11 | async-start | bytes 81920 | tf_op jit(solution)/shard_map/slice | solution.py:337
  118.2 38.8 %all-to-all-start.4 = ((f32[32,5,16,128]{3,2,1,0:T(8,128)}), f32[32,5,16,128]{3,2,1,0:T(8,128)S(1)}, u32[]{:S(2)}, u32[]{:S(2)}) async-start(f32[32,5,16,128]{3,2,1,0:T(8,128)} %broadcast_in_dim.78), calls=%async_computation.4 | async-start | bytes 2621440 | tf_op jit(solution)/shard_map/all_to_all | solution.py:250
  125.7 81.0 %reduce-scatter.2.cloned.1.call-start = ((), (), s32[]{:S(2)}) async-start(), calls=%async_computation.10 | async-start | bytes 1114112 | tf_op jit(solution)/shard_map/reduce_scatter | solution.py:340
  157.0 49.7 %all-to-all-start.5 = ((f32[16,16,1024]{2,1,0:T(8,128)}), f32[16,16,1024]{2,1,0:T(8,128)S(1)}, u32[]{:S(2)}, u32[]{:S(2)}) async-start(f32[16,16,1024]{2,1,0:T(8,128)} %bitcast.19), calls=%async_computation.5 | async-start | bytes 2097152 | tf_op jit(solution)/shard_map/all_to_all | solution.py:343
  163.7 4.9 %collective-permute-start.4 = (f32[32,5,16,128]{3,2,1,0:T(8,128)S(1)}, f32[32,5,16,128]{3,2,1,0:T(8,128)S(1)}, u32[]{:S(2)}, u32[]{:S(2)}) collective-permute-start(f32[32,5,16,128]{3,2,1,0:T(8,128)S(1)} %all-to-all-done.4.mine_ref), channel_id=1, source_target_pairs={{0,1},{1,0},{2,3},{3,2},{4,5},{5,4},{6,7},{7,6},{8,9},{9,8},{10,11... | collective-permute-start | bytes 3932168 | tf_op jit(solution)/shard_map/ppermute | solution.py:339
  206.8 0.8 copy-start
  213.5 15.1 %all-to-all-start.6 = ((f32[16,1,1024]{2,1,0:T(1,128)}), f32[16,1,1024]{2,1,0:T(1,128)S(1)}, u32[]{:S(2)}, u32[]{:S(2)}) async-start(f32[16,1,1024]{2,1,0:T(1,128)} %reshape.141), calls=%async_computation.7 | async-start | bytes 131072 | tf_op jit(solution)/shard_map/all_to_all | solution.py:356
  220.8 9.3 %collective-permute-start.5 = (f32[16,1024]{1,0:T(8,128)S(1)}, f32[16,1024]{1,0:T(8,128)S(1)}, u32[]{:S(2)}, u32[]{:S(2)}) collective-permute-start(f32[16,1024]{1,0:T(8,128)S(1)} %get-tuple-element.44), channel_id=1, source_target_pairs={{0,0},{1,16},{2,32},{3,48},{4,64},{5,80},{6,96},{7,112},{8,136},{9... | collective-permute-start | bytes 196616 | tf_op jit(solution)/shard_map/ppermute | solution.py:354
  231.2 21.2 %all-to-all-start.7 = ((f32[32,1,512]{2,1,0:T(1,128)}), f32[32,1,512]{2,1,0:T(1,128)S(1)}, u32[]{:S(2)}, u32[]{:S(2)}) async-start(f32[32,1,512]{2,1,0:T(1,128)} %reshape.143), calls=%async_computation.8 | async-start | bytes 131072 | tf_op jit(solution)/shard_map/all_to_all | solution.py:359
Sparse Core Ops, SparseCore 0:
  63.2 39.0 all-gather.1
  129.3 64.5 reduce-scatter.1

commit v9 on v8

--- a/solution.py
+++ b/solution.py
@@ -287,21 +287,19 @@
                     to_row = per_col * c + (r + turn) % per_col + q * (row_count // spread)
                     pairs.append((r * col_count + c, to_row % row_count * col_count + r // per_col))
             routes.append(pairs)
-    own, *sends = lax.optimization_barrier((own, *sends))
-    parts = [lax.ppermute(sent, ("row", "col"), pairs) for sent, pairs in zip(sends, routes)]
-    from_y, *parts = lax.optimization_barrier((collect(own, "row", tall, along_y), *parts))
-    pieces = [jnp.concatenate(parts[turn * spread:(turn + 1) * spread], axis=1) for turn in range(per_col)]
-    flip = (row_place % per_col) == 1
-    first = jnp.where(flip, pieces[1], pieces[0])
-    second = jnp.where(flip, pieces[0], pieces[1])
-    solved_here = jnp.concatenate([first[:prev_rows], second[:prev_rows]], axis=0)
-    right_here = jnp.concatenate([first[prev_rows:], second[prev_rows:]], axis=0).astype(jnp.float32)
-    right_here = right_here.reshape(per_col, 3, block_rows, vox_part)
-    right_here = (right_here[:, 0] + right_here[:, 1] + right_here[:, 2]).reshape(col_width, vox_part)
-
+    parts = []
+
+    def beside(stage, value):
+        start, *sends[:] = lax.optimization_barrier((value, *sends))
+        part = lax.ppermute(sends.pop(0), ("row", "col"), routes.pop(0))
+        out, part, *sends[:] = lax.optimization_barrier((stage(start), part, *sends))
+        parts.append(part)
+        return out
+
+    from_y = beside(lambda value: collect(value, "row", tall, along_y), own)
     packed = jnp.concatenate([own] + split_three(gram_panel[:block_rows]), axis=1)
     packed, from_y = lax.optimization_barrier((packed, from_y))
-    from_x = collect(packed, "row", wide, along_x)
+    from_x = beside(lambda value: collect(value, "row", wide, along_x), packed)
     rows_x = from_x[:, :, :depth].reshape(wide * block_rows, depth)
     rows_y = from_y.reshape(tall * block_rows, depth)
     gram_x = from_x[:, :, depth:].astype(jnp.float32).reshape(wide * block_rows, 3, per_col, block_rows)
@@ -319,8 +317,16 @@
     turned = lax.dynamic_slice_in_dim(jnp.concatenate([turned, turned], axis=0), tall - 1 - row_place // wide, tall, 0)
     thin = tall * block_rows // col_count
     partial = turned.reshape(col_count, thin, wide * block_rows)
-    own_diag = jnp.sum(lax.all_to_all(partial, "col", 0, 0), axis=0)
-    diag_z = collect(own_diag, "col", chips, along_z)
+    own_diag = jnp.sum(beside(lambda value: lax.all_to_all(value, "col", 0, 0), partial), axis=0)
+    diag_z = beside(lambda value: collect(value, "col", chips, along_z), own_diag)
+    pieces = [jnp.concatenate(parts[turn * spread:(turn + 1) * spread], axis=1) for turn in range(per_col)]
+    flip = (row_place % per_col) == 1
+    first = jnp.where(flip, pieces[1], pieces[0])
+    second = jnp.where(flip, pieces[0], pieces[1])
+    solved_here = jnp.concatenate([first[:prev_rows], second[:prev_rows]], axis=0)
+    right_here = jnp.concatenate([first[prev_rows:], second[prev_rows:]], axis=0).astype(jnp.float32)
+    right_here = right_here.reshape(per_col, 3, block_rows, vox_part)
+    right_here = (right_here[:, 0] + right_here[:, 1] + right_here[:, 2]).reshape(col_width, vox_part)
 
     chosen = lax.all_gather(rows_y, "row", axis=0, tiled=False, axis_index_groups=along_x)
     chosen = chosen.reshape(wide, tall, block_rows, depth).transpose(1, 0, 2, 3).reshape(panel, depth)
@@ -334,8 +340,7 @@
         solved_here, chosen, (((0,), (1,)), ((), ())), preferred_element_type=jnp.float32
     )
 
-    diag_z, update_part, product = lax.optimization_barrier((diag_z[:kept], update_part, product))
-    diag_row = collect(diag_z, "row", row_count)
+    diag_row = collect(diag_z[:kept], "row", row_count)
     other = lax.ppermute(diag_row, "col", [(i, i ^ 1) for i in range(col_count)])
     update = lax.psum_scatter(update_part, "col", scatter_dimension=0, tiled=True)
     product = product.reshape(col_count, vox_part // col_count, panel)
@@ -346,17 +351,17 @@
     factored, spread_out, update = lax.optimization_barrier((factored, spread_out, update))
     rows_out, vox_out = forward(factored, update, jnp.sum(spread_out, axis=0))
 
-    pairs = []
-    for r in range(row_count):
-        for c in range(col_count):
-            from_row = (r - c * spread // col_count * (row_count // spread)) % row_count
-            pairs.append((r * col_count + c, (r % per_col * col_count + c) * col_count + from_row // per_col))
-    vox_out = lax.ppermute(vox_out, ("row", "col"), pairs)
+    vox_out = vox_out.reshape(-1, row_count, block_rows).transpose(1, 0, 2)
+    vox_out = lax.all_to_all(vox_out, "row", 0, 0)
+    start = col_place * spread // col_count * (row_count // spread)
+    vox_out = lax.dynamic_slice_in_dim(jnp.concatenate([vox_out, vox_out], axis=0), start, row_count, 0)
     rows_out = rows_out.reshape(-1, col_count, col_width).transpose(1, 0, 2)
-    panel_factor = lax.all_to_all(rows_out, "col", 0, 0).reshape(-1, col_width)
-    vox_out, panel_factor = lax.optimization_barrier((vox_out, panel_factor))
-    vox_out = vox_out.reshape(-1, row_count, block_rows).transpose(1, 0, 2)
-    solved_panel = lax.all_to_all(vox_out, "row", 0, 0).reshape(vox, block_rows).T
+    count = rows_out.shape[1] * col_width
+    both = jnp.concatenate([rows_out.reshape(col_count, count), vox_out.reshape(col_count, -1)], axis=1)
+    both = lax.all_to_all(both.reshape(col_count, -1, 128), "col", 0, 0).reshape(col_count, -1)
+    panel_factor = both[:, :count].reshape(-1, col_width)
+    vox_out = both[:, count:].reshape(col_count, per_col, -1, block_rows).transpose(1, 0, 2, 3)
+    solved_panel = vox_out.reshape(vox, block_rows).T
     return (panel_factor, solved_panel)
 
 

time: 264 us -> 272 us (1.030)
  blocking collectives: 0 us -> 34.8 us
  waiting for transfers between devices: 81.7 us -> 50.6 us
  starting transfers between devices: 95.7 us -> 103 us
    all_to_all x0 -> x2, blocking collectives: none -> 34.8 us  [the longest x1 19.5 us: body(): lax.all_to_all(both.reshape(col_count, -1, 128), 'col', 0, 0)]
    all_to_all x4 -> x3, waiting for transfers between devices: 43 us -> 26 us  [collect(): return lax.all_to_all(many, axis, 0, 0, axis_index_groups=groups)]
    ppermute x5 -> x4, starting transfers between devices: 32.6 us -> 47.5 us  [beside(): part = lax.ppermute(sends.pop(0), ('row', 'col'), routes.pop(0))]
    all_to_all x3 -> x2, waiting for transfers between devices: 21.2 us -> 8.62 us  [the longest x1 8.62 us: body(): vox_out = lax.all_to_all(vox_out, 'row', 0, 0)]
    all_to_all x3 -> x2, starting transfers between devices: 32.2 us -> 23.7 us  [the longest x1 18.3 us: body(): lax.all_to_all(value, 'col', 0, 0)]
    all_to_all x1, starting transfers between devices: 6.67 us -> 9.7 us  [body(): spread_out = lax.all_to_all(product, 'col', 0, 0)]
    all_to_all x4 -> x3, starting transfers between devices: 21.9 us -> 19.8 us  [collect(): return lax.all_to_all(many, axis, 0, 0, axis_index_groups=groups)]
    ppermute x5 -> x4, waiting for transfers between devices: 14.1 us -> 13.2 us  [beside(): part = lax.ppermute(sends.pop(0), ('row', 'col'), routes.pop(0))]
  transfers between devices with their start and end apart: 16 -> 13, of which waited for: 8 -> 7; matrix products, arithmetic and copies ran while one was open for 3% -> 6% of each run, Pallas kernels for 15% -> 14%
where the time goes in v9:
time: 272 us; the launch traced here: 271 us
  starting transfers between devices  103 us (38%)
  waiting for transfers between devices  50.6 us (19%)
  Pallas kernels  43.1 us (16%)
  blocking collectives  34.8 us (13%)
  local copies, waits for them, and re-layouts  15.9 us (6%)
  between operations  14.6 us (5%)
  matrix products  5.18 us (2%)
  other arithmetic  3.84 us (1%)
    ppermute x4, starting transfers between devices, beside(): part = lax.ppermute(sends.pop(0), ('row', 'col'), routes.pop(0))  47.5 us
    pallas_call x1, Pallas kernels, factor(): pl.pallas_call(factor_kernel, out_shape=pltpu.HBM((big, panel, 256), jnp....  38.1 us
    all_to_all x3, waiting for transfers between devices, collect(): return lax.all_to_all(many, axis, 0, 0, axis_index_groups=groups)  26 us
    all_to_all x3, starting transfers between devices, collect(): return lax.all_to_all(many, axis, 0, 0, axis_index_groups=groups)  19.8 us
    all_to_all x1, blocking collectives, body(): lax.all_to_all(both.reshape(col_count, -1, 128), 'col', 0, 0)  19.5 us
    all_to_all x1, starting transfers between devices, body(): lax.all_to_all(value, 'col', 0, 0)  18.3 us
    all_to_all x1, blocking collectives, collect(): return lax.all_to_all(many, axis, 0, 0, axis_index_groups=groups)  15.3 us
    ppermute x4, waiting for transfers between devices, beside(): part = lax.ppermute(sends.pop(0), ('row', 'col'), routes.pop(0))  13.2 us
  transfers between devices with their start and end apart: 13, of which 7 were waited for; matrix products, arithmetic and copies ran while one was open for 6% of the time, Pallas kernels for 14%

profile of v9, /device:TPU:1, one launch (start us, length us, event | category | flops | bytes accessed | tf_op | source)
XLA Modules:
  0.0 271.0 jit_solution(15615102010323002790)
XLA Ops:
  7.2 0.8 slice.51
  8.0 0.9 reduce-precision_convert_fusion.1
  8.9 1.1 pad_maximum_fusion
  10.2 0.9 broadcast_in_dim.70
  11.0 7.7 %all-to-all-start = ((bf16[8,32,1024]{2,1,0:T(8,128)(2,1)}), bf16[8,32,1024]{2,1,0:T(8,128)(2,1)S(1)}, u32[]{:S(2)}, u32[]{:S(2)}) async-start(bf16[8,32,1024]{2,1,0:T(8,128)(2,1)} %broadcast_in_dim.70), calls=%async_computation | async-start | bytes 1048576 | tf_op jit(solution)/shard_map/all_to_all | solution.py:250
  18.7 5.5 %collective-permute-start = (bf16[608,128]{1,0:T(8,128)(2,1)S(1)}, bf16[608,128]{1,0:T(8,128)(2,1)S(1)}, u32[]{:S(2)}, u32[]{:S(2)}) collective-permute-start(bf16[608,128]{1,0:T(8,128)(2,1)S(1)} %get-tuple-element.39), channel_id=1, source_target_pairs={{0,0},{1,32},{2,64},{3,96},{4,128},{5,160},{6,192},{7,224},{8,256}... | collective-permute-start | bytes 466952 | tf_op jit(solution)/shard_map/ppermute | solution.py:294
  24.4 2.7 %collective-permute-done = bf16[608,128]{1,0:T(8,128)(2,1)S(1)} collective-permute-done((bf16[608,128]{1,0:T(8,128)(2,1)S(1)}, bf16[608,128]{1,0:T(8,128)(2,1)S(1)}, u32[]{:S(2)}, u32[]{:S(2)}) %collective-permute-start) | collective-permute-done | bytes 155680 | tf_op jit(solution)/shard_map/ppermute | solution.py:294
  27.1 6.4 %all-to-all-done = bf16[8,32,1024]{2,1,0:T(8,128)(2,1)S(1)} async-done(((bf16[8,32,1024]{2,1,0:T(8,128)(2,1)}), bf16[8,32,1024]{2,1,0:T(8,128)(2,1)S(1)}, u32[]{:S(2)}, u32[]{:S(2)}) %all-to-all-start) | async-done | bytes 524320 | tf_op jit(solution)/shard_map/all_to_all | solution.py:250
  34.2 7.2 %all-to-all-start.1 = ((bf16[4,32,1216]{2,1,0:T(8,128)(2,1)}), bf16[4,32,1216]{2,1,0:T(8,128)(2,1)S(1)}, u32[]{:S(2)}, u32[]{:S(2)}) async-start(bf16[4,32,1216]{2,1,0:T(8,128)(2,1)} %broadcast_in_dim.71), calls=%async_computation.1 | async-start | bytes 655360 | tf_op jit(solution)/shard_map/all_to_all | solution.py:250
  41.4 18.4 %collective-permute-start.1 = (bf16[608,128]{1,0:T(8,128)(2,1)S(1)}, bf16[608,128]{1,0:T(8,128)(2,1)S(1)}, u32[]{:S(2)}, u32[]{:S(2)}) collective-permute-start(bf16[608,128]{1,0:T(8,128)(2,1)S(1)} %get-tuple-element.49), channel_id=1, source_target_pairs={{0,256},{1,288},{2,320},{3,352},{4,384},{5,416},{6,448},{7,480},{8... | collective-permute-start | bytes 466952 | tf_op jit(solution)/shard_map/ppermute | solution.py:294
  60.2 2.9 %collective-permute-done.1 = bf16[608,128]{1,0:T(8,128)(2,1)S(1)} collective-permute-done((bf16[608,128]{1,0:T(8,128)(2,1)S(1)}, bf16[608,128]{1,0:T(8,128)(2,1)S(1)}, u32[]{:S(2)}, u32[]{:S(2)}) %collective-permute-start.1) | collective-permute-done | bytes 155680 | tf_op jit(solution)/shard_map/ppermute | solution.py:294
  65.1 18.3 %all-to-all-start.2 = ((f32[16,16,128]{2,1,0:T(8,128)}), f32[16,16,128]{2,1,0:T(8,128)S(1)}, u32[]{:S(2)}, u32[]{:S(2)}) async-start(f32[16,16,128]{2,1,0:T(8,128)} %bitcast.7), calls=%async_computation.2 | async-start | bytes 262144 | tf_op jit(solution)/shard_map/all_to_all | solution.py:320
  83.4 3.8 %collective-permute-start.2 = (bf16[608,128]{1,0:T(8,128)(2,1)S(1)}, bf16[608,128]{1,0:T(8,128)(2,1)S(1)}, u32[]{:S(2)}, u32[]{:S(2)}) collective-permute-start(bf16[608,128]{1,0:T(8,128)(2,1)S(1)} %get-tuple-element.57), channel_id=1, source_target_pairs={{0,16},{1,48},{2,80},{3,112},{4,144},{5,176},{6,208},{7,240},{8,27... | collective-permute-start | bytes 466952 | tf_op jit(solution)/shard_map/ppermute | solution.py:294
  87.2 7.6 %collective-permute-done.2 = bf16[608,128]{1,0:T(8,128)(2,1)S(1)} collective-permute-done((bf16[608,128]{1,0:T(8,128)(2,1)S(1)}, bf16[608,128]{1,0:T(8,128)(2,1)S(1)}, u32[]{:S(2)}, u32[]{:S(2)}) %collective-permute-start.2) | collective-permute-done | bytes 155680 | tf_op jit(solution)/shard_map/ppermute | solution.py:294
  94.8 19.8 %collective-permute-start.3 = (bf16[608,128]{1,0:T(8,128)(2,1)S(1)}, bf16[608,128]{1,0:T(8,128)(2,1)S(1)}, u32[]{:S(2)}, u32[]{:S(2)}) collective-permute-start(bf16[608,128]{1,0:T(8,128)(2,1)S(1)} %get-tuple-element.62), channel_id=1, source_target_pairs={{0,272},{1,304},{2,336},{3,368},{4,400},{5,432},{6,464},{7,496},{8... | collective-permute-start | bytes 466952 | tf_op jit(solution)/shard_map/ppermute | solution.py:294
  114.7 15.3 %all_to_all.40 = f32[8,16,128]{2,1,0:T(8,128)S(1)} all-to-all(f32[8,16,128]{2,1,0:T(8,128)S(1)} %broadcast_in_dim.75), channel_id=1, replica_groups={{0,2,4,6,8,10,12,14},{1,3,5,7,9,11,13,15},{16,18,20,22,24,26,28,30},{17..., dimensions={0} | all-to-all | bytes 131072 | tf_op jit(solution)/shard_map/all_to_all | solution.py:250
  129.9 1.2 broadcast_in_dim.76
  131.1 4.9 %all-to-all-start.4 = ((f32[32,5,16,128]{3,2,1,0:T(8,128)}), f32[32,5,16,128]{3,2,1,0:T(8,128)S(1)}, u32[]{:S(2)}, u32[]{:S(2)}) async-start(f32[32,5,16,128]{3,2,1,0:T(8,128)} %broadcast_in_dim.76), calls=%async_computation.4 | async-start | bytes 2621440 | tf_op jit(solution)/shard_map/all_to_all | solution.py:250
  136.2 1.3 copy.36
  139.3 1.3 copy.34
  140.7 1.9 copy.35
  142.6 1.8 fusion
  144.4 3.1 %convolution_subtract_fusion = f32[256,1024]{1,0:T(8,128)} fusion(bf16[1024,1024]{1,0:T(8,128)(2,1)S(1)} %bitcast.48, f32[256,1024]{1,0:T(8,128)} %copy.34, bf16[512,256]{1,0:T(8,128)(2,1)} %slice.77, bf16[512,256]{1,0:T(8,128)(2,1)} %slice.76, pred[1024]{0:T(1024)(128)(4,1)S(1)} %fusion.8), kind=kOutput, calls=%fused_computation.2 | convolution fusion | flops 538443776 | bytes 4719616 | tf_op jit(solution)/shard_map/dot_general | solution.py:339
  147.6 19.6 %all-to-all-done.4.mine_ref = f32[32,5,16,128]{3,2,1,0:T(8,128)S(1)} async-done(((f32[32,5,16,128]{3,2,1,0:T(8,128)}), f32[32,5,16,128]{3,2,1,0:T(8,128)S(1)}, u32[]{:S(2)}, u32[]{:S(2)}) %all-to-all-start.4) | async-done | bytes 1310752 | tf_op jit(solution)/shard_map/all_to_all | solution.py:250
  167.1 9.7 %all-to-all-start.5 = ((f32[16,16,1024]{2,1,0:T(8,128)}), f32[16,16,1024]{2,1,0:T(8,128)S(1)}, u32[]{:S(2)}, u32[]{:S(2)}) async-start(f32[16,16,1024]{2,1,0:T(8,128)} %bitcast.51), calls=%async_computation.5 | async-start | bytes 2097152 | tf_op jit(solution)/shard_map/all_to_all | solution.py:348
  176.8 2.2 collective-permute-start.4
  179.0 2.7 %collective-permute-done.4.other_ref = f32[32,5,16,128]{3,2,1,0:T(8,128)S(1)} collective-permute-done((f32[32,5,16,128]{3,2,1,0:T(8,128)S(1)}, f32[32,5,16,128]{3,2,1,0:T(8,128)S(1)}, u32[]{:S(2)}, u32[]{:S(2)}) %collective-permute-start.4) | collective-permute-done | bytes 1310752 | tf_op jit(solution)/shard_map/ppermute | solution.py:344
  181.8 38.1 %shard_map.59.from_ref = f32[4,1024,256]{2,1,0:T(8,128)} custom-call(s32[1]{0:T(128)} %bitcast.core_ref, f32[32,5,16,128]{3,2,1,0:T(8,128)S(1)} %all-to-all-done.4.mine_ref, f32[32,5,16,128]{3,2,1,0:T(8,128)S(1)} %collective-permute-done.4.other_ref), custom_call_target="tpu_custom_call" | custom-call | flops 1073741824 | bytes 8388608 | tf_op jit(solution)/shard_map/pallas_call | solution.py:208
  220.8 5.0 %shard_map.60 = (f32[16,1024]{1,0:T(8,128)S(1)}, f32[16,1024]{1,0:T(8,128)S(1)}) custom-call(f32[4,1024,256]{2,1,0:T(8,128)} %shard_map.59.from_ref, f32[16,1024]{1,0:T(8,128)S(1)} %copy-done, f32[16,1024]{1,0:T(8,128)S(1)} %reduce_sum.19.v_ref), custom_call_target="tpu_custom_call" | custom-call | tf_op jit(solution)/shard_map/pallas_call | solution.py:227
  226.9 5.4 %all-to-all-start.6 = ((f32[32,1,512]{2,1,0:T(1,128)}), f32[32,1,512]{2,1,0:T(1,128)S(1)}, u32[]{:S(2)}, u32[]{:S(2)}) async-start(f32[32,1,512]{2,1,0:T(1,128)} %reshape.156), calls=%async_computation.7 | async-start | bytes 131072 | tf_op jit(solution)/shard_map/all_to_all | solution.py:355
  232.5 8.6 %all-to-all-done.6 = f32[32,1,512]{2,1,0:T(1,128)S(1)} async-done(((f32[32,1,512]{2,1,0:T(1,128)}), f32[32,1,512]{2,1,0:T(1,128)S(1)}, u32[]{:S(2)}, u32[]{:S(2)}) %all-to-all-start.6) | async-done | bytes 65568 | tf_op jit(solution)/shard_map/all_to_all | solution.py:355
  242.8 19.5 %all_to_all.41 = f32[16,16,128]{2,1,0:T(8,128)S(1)} all-to-all(f32[16,16,128]{2,1,0:T(8,128)S(1)} %pad_maximum_fusion.1), channel_id=1, replica_groups=mesh['row'=32,'col'=16] {'col'}, dimensions={0} | all-to-all | bytes 262144 | tf_op jit(solution)/shard_map/all_to_all | solution.py:361
  (84 shorter events, 10.8 us)
Async XLA Ops:
  10.0 14.2 %slice-start = ((f32[256,64]{0,1:T(8,128)}), f32[32,64]{0,1:T(8,128)S(1)}, s32[]{:S(2)}) async-start(f32[256,64]{0,1:T(8,128)} %param.4), calls=%async_computation.11 | async-start | bytes 65536 | tf_op jit(solution)/shard_map/slice | solution.py:300
  11.0 22.4 %all-to-all-start = ((bf16[8,32,1024]{2,1,0:T(8,128)(2,1)}), bf16[8,32,1024]{2,1,0:T(8,128)(2,1)S(1)}, u32[]{:S(2)}, u32[]{:S(2)}) async-start(bf16[8,32,1024]{2,1,0:T(8,128)(2,1)} %broadcast_in_dim.70), calls=%async_computation | async-start | bytes 1048576 | tf_op jit(solution)/shard_map/all_to_all | solution.py:250
  18.7 8.4 %collective-permute-start = (bf16[608,128]{1,0:T(8,128)(2,1)S(1)}, bf16[608,128]{1,0:T(8,128)(2,1)S(1)}, u32[]{:S(2)}, u32[]{:S(2)}) collective-permute-start(bf16[608,128]{1,0:T(8,128)(2,1)S(1)} %get-tuple-element.39), channel_id=1, source_target_pairs={{0,0},{1,32},{2,64},{3,96},{4,128},{5,160},{6,192},{7,224},{8,256}... | collective-permute-start | bytes 466952 | tf_op jit(solution)/shard_map/ppermute | solution.py:294
  33.4 26.7 %copy-start.2 = (bf16[8,32,1024]{2,1,0:T(8,128)(2,1)}, bf16[8,32,1024]{2,1,0:T(8,128)(2,1)S(1)}, u32[]{:S(2)}) copy-start(bf16[8,32,1024]{2,1,0:T(8,128)(2,1)S(1)} %all-to-all-done) | copy-start | bytes 1572868
  34.2 28.8 %all-to-all-start.1 = ((bf16[4,32,1216]{2,1,0:T(8,128)(2,1)}), bf16[4,32,1216]{2,1,0:T(8,128)(2,1)S(1)}, u32[]{:S(2)}, u32[]{:S(2)}) async-start(bf16[4,32,1216]{2,1,0:T(8,128)(2,1)} %broadcast_in_dim.71), calls=%async_computation.1 | async-start | bytes 655360 | tf_op jit(solution)/shard_map/all_to_all | solution.py:250
  41.4 99.2 %all-gather.2.cloned.1.call-start = ((), (), s32[]{:S(2)}) async-start(), calls=%async_computation.9 | async-start | bytes 2621440 | tf_op jit(solution)/shard_map/all_gather | solution.py:331
  41.4 21.6 %collective-permute-start.1 = (bf16[608,128]{1,0:T(8,128)(2,1)S(1)}, bf16[608,128]{1,0:T(8,128)(2,1)S(1)}, u32[]{:S(2)}, u32[]{:S(2)}) collective-permute-start(bf16[608,128]{1,0:T(8,128)(2,1)S(1)} %get-tuple-element.49), channel_id=1, source_target_pairs={{0,256},{1,288},{2,320},{3,352},{4,384},{5,416},{6,448},{7,480},{8... | collective-permute-start | bytes 466952 | tf_op jit(solution)/shard_map/ppermute | solution.py:294
  63.1 1.0 copy-start.3
  65.1 29.7 %all-to-all-start.2 = ((f32[16,16,128]{2,1,0:T(8,128)}), f32[16,16,128]{2,1,0:T(8,128)S(1)}, u32[]{:S(2)}, u32[]{:S(2)}) async-start(f32[16,16,128]{2,1,0:T(8,128)} %bitcast.7), calls=%async_computation.2 | async-start | bytes 262144 | tf_op jit(solution)/shard_map/all_to_all | solution.py:320
  83.4 11.5 %collective-permute-start.2 = (bf16[608,128]{1,0:T(8,128)(2,1)S(1)}, bf16[608,128]{1,0:T(8,128)(2,1)S(1)}, u32[]{:S(2)}, u32[]{:S(2)}) collective-permute-start(bf16[608,128]{1,0:T(8,128)(2,1)S(1)} %get-tuple-element.57), channel_id=1, source_target_pairs={{0,16},{1,48},{2,80},{3,112},{4,144},{5,176},{6,208},{7,240},{8,27... | collective-permute-start | bytes 466952 | tf_op jit(solution)/shard_map/ppermute | solution.py:294
  94.8 35.1 %collective-permute-start.3 = (bf16[608,128]{1,0:T(8,128)(2,1)S(1)}, bf16[608,128]{1,0:T(8,128)(2,1)S(1)}, u32[]{:S(2)}, u32[]{:S(2)}) collective-permute-start(bf16[608,128]{1,0:T(8,128)(2,1)S(1)} %get-tuple-element.62), channel_id=1, source_target_pairs={{0,272},{1,304},{2,336},{3,368},{4,400},{5,432},{6,464},{7,496},{8... | collective-permute-start | bytes 466952 | tf_op jit(solution)/shard_map/ppermute | solution.py:294
  131.1 5.0 %copy-start.5 = (f32[256,64]{0,1:T(8,128)S(1)}, f32[256,64]{0,1:T(8,128)}, u32[]{:S(2)}) copy-start(f32[256,64]{0,1:T(8,128)} %param.4) | copy-start | bytes 196612
  131.1 36.0 %all-to-all-start.4 = ((f32[32,5,16,128]{3,2,1,0:T(8,128)}), f32[32,5,16,128]{3,2,1,0:T(8,128)S(1)}, u32[]{:S(2)}, u32[]{:S(2)}) async-start(f32[32,5,16,128]{3,2,1,0:T(8,128)} %broadcast_in_dim.76), calls=%async_computation.4 | async-start | bytes 2621440 | tf_op jit(solution)/shard_map/all_to_all | solution.py:250
  136.0 83.9 %reduce-scatter.2.cloned.1.call-start = ((), (), s32[]{:S(2)}) async-start(), calls=%async_computation.10 | async-start | bytes 1114112 | tf_op jit(solution)/shard_map/reduce_scatter | solution.py:345
  140.7 1.9 copy-start.1
  140.7 2.0 copy-start.4
  167.1 52.8 %all-to-all-start.5 = ((f32[16,16,1024]{2,1,0:T(8,128)}), f32[16,16,1024]{2,1,0:T(8,128)S(1)}, u32[]{:S(2)}, u32[]{:S(2)}) async-start(f32[16,16,1024]{2,1,0:T(8,128)} %bitcast.51), calls=%async_computation.5 | async-start | bytes 2097152 | tf_op jit(solution)/shard_map/all_to_all | solution.py:348
  176.8 4.9 %collective-permute-start.4 = (f32[32,5,16,128]{3,2,1,0:T(8,128)S(1)}, f32[32,5,16,128]{3,2,1,0:T(8,128)S(1)}, u32[]{:S(2)}, u32[]{:S(2)}) collective-permute-start(f32[32,5,16,128]{3,2,1,0:T(8,128)S(1)} %all-to-all-done.4.mine_ref), channel_id=1, source_target_pairs={{0,1},{1,0},{2,3},{3,2},{4,5},{5,4},{6,7},{7,6},{8,9},{9,8},{10,11... | collective-permute-start | bytes 3932168 | tf_op jit(solution)/shard_map/ppermute | solution.py:344
  220.0 0.8 copy-start
  226.9 14.3 %all-to-all-start.6 = ((f32[32,1,512]{2,1,0:T(1,128)}), f32[32,1,512]{2,1,0:T(1,128)S(1)}, u32[]{:S(2)}, u32[]{:S(2)}) async-start(f32[32,1,512]{2,1,0:T(1,128)} %reshape.156), calls=%async_computation.7 | async-start | bytes 131072 | tf_op jit(solution)/shard_map/all_to_all | solution.py:355
Sparse Core Ops, SparseCore 0:
  60.3 38.3 all-gather.1
  144.5 73.4 reduce-scatter.1

commit v10 on v8

--- a/solution.py
+++ b/solution.py
@@ -290,6 +290,9 @@
     own, *sends = lax.optimization_barrier((own, *sends))
     parts = [lax.ppermute(sent, ("row", "col"), pairs) for sent, pairs in zip(sends, routes)]
     from_y, *parts = lax.optimization_barrier((collect(own, "row", tall, along_y), *parts))
+    packed = jnp.concatenate([own] + split_three(gram_panel[:block_rows]), axis=1)
+    packed, from_y = lax.optimization_barrier((packed, from_y))
+    from_x = collect(packed, "row", wide, along_x)
     pieces = [jnp.concatenate(parts[turn * spread:(turn + 1) * spread], axis=1) for turn in range(per_col)]
     flip = (row_place % per_col) == 1
     first = jnp.where(flip, pieces[1], pieces[0])
@@ -298,10 +301,6 @@
     right_here = jnp.concatenate([first[prev_rows:], second[prev_rows:]], axis=0).astype(jnp.float32)
     right_here = right_here.reshape(per_col, 3, block_rows, vox_part)
     right_here = (right_here[:, 0] + right_here[:, 1] + right_here[:, 2]).reshape(col_width, vox_part)
-
-    packed = jnp.concatenate([own] + split_three(gram_panel[:block_rows]), axis=1)
-    packed, from_y = lax.optimization_barrier((packed, from_y))
-    from_x = collect(packed, "row", wide, along_x)
     rows_x = from_x[:, :, :depth].reshape(wide * block_rows, depth)
     rows_y = from_y.reshape(tall * block_rows, depth)
     gram_x = from_x[:, :, depth:].astype(jnp.float32).reshape(wide * block_rows, 3, per_col, block_rows)
@@ -334,8 +333,7 @@
         solved_here, chosen, (((0,), (1,)), ((), ())), preferred_element_type=jnp.float32
     )
 
-    diag_z, update_part, product = lax.optimization_barrier((diag_z[:kept], update_part, product))
-    diag_row = collect(diag_z, "row", row_count)
+    diag_row = collect(diag_z[:kept], "row", row_count)
     other = lax.ppermute(diag_row, "col", [(i, i ^ 1) for i in range(col_count)])
     update = lax.psum_scatter(update_part, "col", scatter_dimension=0, tiled=True)
     product = product.reshape(col_count, vox_part // col_count, panel)
@@ -346,17 +344,17 @@
     factored, spread_out, update = lax.optimization_barrier((factored, spread_out, update))
     rows_out, vox_out = forward(factored, update, jnp.sum(spread_out, axis=0))
 
-    pairs = []
-    for r in range(row_count):
-        for c in range(col_count):
-            from_row = (r - c * spread // col_count * (row_count // spread)) % row_count
-            pairs.append((r * col_count + c, (r % per_col * col_count + c) * col_count + from_row // per_col))
-    vox_out = lax.ppermute(vox_out, ("row", "col"), pairs)
+    vox_out = vox_out.reshape(-1, row_count, block_rows).transpose(1, 0, 2)
+    vox_out = lax.all_to_all(vox_out, "row", 0, 0)
+    start = col_place * spread // col_count * (row_count // spread)
+    vox_out = lax.dynamic_slice_in_dim(jnp.concatenate([vox_out, vox_out], axis=0), start, row_count, 0)
     rows_out = rows_out.reshape(-1, col_count, col_width).transpose(1, 0, 2)
-    panel_factor = lax.all_to_all(rows_out, "col", 0, 0).reshape(-1, col_width)
-    vox_out, panel_factor = lax.optimization_barrier((vox_out, panel_factor))
-    vox_out = vox_out.reshape(-1, row_count, block_rows).transpose(1, 0, 2)
-    solved_panel = lax.all_to_all(vox_out, "row", 0, 0).reshape(vox, block_rows).T
+    count = rows_out.shape[1] * col_width
+    both = jnp.concatenate([rows_out.reshape(col_count, count), vox_out.reshape(col_count, -1)], axis=1)
+    both = lax.all_to_all(both.reshape(col_count, -1, 128), "col", 0, 0).reshape(col_count, -1)
+    panel_factor = both[:, :count].reshape(-1, col_width)
+    vox_out = both[:, count:].reshape(col_count, per_col, -1, block_rows).transpose(1, 0, 2, 3)
+    solved_panel = vox_out.reshape(vox, block_rows).T
     return (panel_factor, solved_panel)
 
 

time: 264 us -> 246 us (0.932)
  blocking collectives: 0 us -> 49.3 us
  starting transfers between devices: 95.7 us -> 62.8 us
  waiting for transfers between devices: 81.7 us -> 50.6 us
    all_to_all x0 -> x3, blocking collectives: none -> 49.3 us  [the longest x1 22 us: body(): own_diag = jnp.sum(lax.all_to_all(partial, 'col', 0, 0), axis=0)]
    all_to_all x3 -> x1, starting transfers between devices: 32.2 us -> 5.39 us  [body(): vox_out = lax.all_to_all(vox_out, 'row', 0, 0)]
    all_to_all x4 -> x3, waiting for transfers between devices: 43 us -> 24.9 us  [collect(): return lax.all_to_all(many, axis, 0, 0, axis_index_groups=groups)]
    all_to_all x3 -> x1, waiting for transfers between devices: 21.2 us -> 8.58 us  [body(): vox_out = lax.all_to_all(vox_out, 'row', 0, 0)]
    ppermute x1 -> x0, starting transfers between devices: 3.51 us -> none  [body(): vox_out = lax.ppermute(vox_out, ('row', 'col'), pairs)]
    all_to_all x4 -> x3, starting transfers between devices: 21.9 us -> 18.7 us  [collect(): return lax.all_to_all(many, axis, 0, 0, axis_index_groups=groups)]
  transfers between devices with their start and end apart: 16 -> 12, of which waited for: 8 -> 5; matrix products, arithmetic and copies ran while one was open for 3% -> 6% of each run, Pallas kernels for 15% -> 16%
where the time goes in v10:
time: 246 us; the launch traced here: 245 us
  starting transfers between devices  62.8 us (26%)
  waiting for transfers between devices  50.6 us (21%)
  blocking collectives  49.3 us (20%)
  Pallas kernels  43.1 us (18%)
  local copies, waits for them, and re-layouts  16 us (7%)
  between operations  14.7 us (6%)
  matrix products  5.21 us (2%)
  other arithmetic  3.21 us (1%)
    pallas_call x1, Pallas kernels, factor(): pl.pallas_call(factor_kernel, out_shape=pltpu.HBM((big, panel, 256), jnp....  38.1 us
    ppermute x4, starting transfers between devices, body(): lax.ppermute(sent, ('row', 'col'), pairs)  29.2 us
    all_to_all x3, waiting for transfers between devices, collect(): return lax.all_to_all(many, axis, 0, 0, axis_index_groups=groups)  24.9 us
    all_to_all x1, blocking collectives, body(): own_diag = jnp.sum(lax.all_to_all(partial, 'col', 0, 0), axis=0)  22 us
    all_to_all x3, starting transfers between devices, collect(): return lax.all_to_all(many, axis, 0, 0, axis_index_groups=groups)  18.7 us
    all_to_all x1, blocking collectives, body(): lax.all_to_all(both.reshape(col_count, -1, 128), 'col', 0, 0)  17.7 us
    ppermute x4, waiting for transfers between devices, body(): lax.ppermute(sent, ('row', 'col'), pairs)  14.1 us
    all_to_all x1, blocking collectives, collect(): return lax.all_to_all(many, axis, 0, 0, axis_index_groups=groups)  9.7 us
  transfers between devices with their start and end apart: 12, of which 5 were waited for; matrix products, arithmetic and copies ran while one was open for 6% of the time, Pallas kernels for 16%

profile of v10, /device:TPU:1, one launch (start us, length us, event | category | flops | bytes accessed | tf_op | source)
XLA Modules:
  0.0 244.8 jit_solution(1753966129498076448)
XLA Ops:
  7.2 0.8 slice.51
  8.0 0.9 reduce-precision_convert_fusion.1
  8.9 1.1 pad_maximum_fusion
  10.2 0.9 broadcast_in_dim.70
  11.0 7.7 %all-to-all-start = ((bf16[8,32,1024]{2,1,0:T(8,128)(2,1)}), bf16[8,32,1024]{2,1,0:T(8,128)(2,1)S(1)}, u32[]{:S(2)}, u32[]{:S(2)}) async-start(bf16[8,32,1024]{2,1,0:T(8,128)(2,1)} %broadcast_in_dim.70), calls=%async_computation | async-start | bytes 1048576 | tf_op jit(solution)/shard_map/all_to_all | solution.py:250
  18.7 5.5 %collective-permute-start = (bf16[608,128]{1,0:T(8,128)(2,1)S(1)}, bf16[608,128]{1,0:T(8,128)(2,1)S(1)}, u32[]{:S(2)}, u32[]{:S(2)}) collective-permute-start(bf16[608,128]{1,0:T(8,128)(2,1)S(1)} %get-tuple-element.21), channel_id=1, source_target_pairs={{0,0},{1,32},{2,64},{3,96},{4,128},{5,160},{6,192},{7,224},{8,256}... | collective-permute-start | bytes 466952 | tf_op jit(solution)/shard_map/ppermute | solution.py:291
  24.2 14.8 %collective-permute-start.1 = (bf16[608,128]{1,0:T(8,128)(2,1)S(1)}, bf16[608,128]{1,0:T(8,128)(2,1)S(1)}, u32[]{:S(2)}, u32[]{:S(2)}) collective-permute-start(bf16[608,128]{1,0:T(8,128)(2,1)S(1)} %get-tuple-element.22), channel_id=1, source_target_pairs={{0,256},{1,288},{2,320},{3,352},{4,384},{5,416},{6,448},{7,480},{8... | collective-permute-start | bytes 466952 | tf_op jit(solution)/shard_map/ppermute | solution.py:291
  39.0 5.2 %collective-permute-start.2 = (bf16[608,128]{1,0:T(8,128)(2,1)S(1)}, bf16[608,128]{1,0:T(8,128)(2,1)S(1)}, u32[]{:S(2)}, u32[]{:S(2)}) collective-permute-start(bf16[608,128]{1,0:T(8,128)(2,1)S(1)} %get-tuple-element.23), channel_id=1, source_target_pairs={{0,16},{1,48},{2,80},{3,112},{4,144},{5,176},{6,208},{7,240},{8,27... | collective-permute-start | bytes 466952 | tf_op jit(solution)/shard_map/ppermute | solution.py:291
  44.2 3.6 %collective-permute-start.3 = (bf16[608,128]{1,0:T(8,128)(2,1)S(1)}, bf16[608,128]{1,0:T(8,128)(2,1)S(1)}, u32[]{:S(2)}, u32[]{:S(2)}) collective-permute-start(bf16[608,128]{1,0:T(8,128)(2,1)S(1)} %get-tuple-element.24), channel_id=1, source_target_pairs={{0,272},{1,304},{2,336},{3,368},{4,400},{5,432},{6,464},{7,496},{8... | collective-permute-start | bytes 466952 | tf_op jit(solution)/shard_map/ppermute | solution.py:291
  48.1 14.0 %collective-permute-done.3 = bf16[608,128]{1,0:T(8,128)(2,1)S(1)} collective-permute-done((bf16[608,128]{1,0:T(8,128)(2,1)S(1)}, bf16[608,128]{1,0:T(8,128)(2,1)S(1)}, u32[]{:S(2)}, u32[]{:S(2)}) %collective-permute-start.3) | collective-permute-done | bytes 155680 | tf_op jit(solution)/shard_map/ppermute | solution.py:291
  62.9 3.5 %all-to-all-start.1 = ((bf16[4,32,1216]{2,1,0:T(8,128)(2,1)}), bf16[4,32,1216]{2,1,0:T(8,128)(2,1)S(1)}, u32[]{:S(2)}, u32[]{:S(2)}) async-start(bf16[4,32,1216]{2,1,0:T(8,128)(2,1)} %broadcast_in_dim.71), calls=%async_computation.1 | async-start | bytes 655360 | tf_op jit(solution)/shard_map/all_to_all | solution.py:250
  67.1 5.7 %all-to-all-done.1 = bf16[4,32,1216]{2,1,0:T(8,128)(2,1)S(1)} async-done(((bf16[4,32,1216]{2,1,0:T(8,128)(2,1)}), bf16[4,32,1216]{2,1,0:T(8,128)(2,1)S(1)}, u32[]{:S(2)}, u32[]{:S(2)}) %all-to-all-start.1) | async-done | bytes 311328 | tf_op jit(solution)/shard_map/all_to_all | solution.py:250
  74.2 22.0 %all_to_all.40 = f32[16,16,128]{2,1,0:T(8,128)S(1)} all-to-all(f32[16,16,128]{2,1,0:T(8,128)S(1)} %bitcast.60), channel_id=1, replica_groups=mesh['row'=32,'col'=16] {'col'}, dimensions={0} | all-to-all | bytes 262144 | tf_op jit(solution)/shard_map/all_to_all | solution.py:321
  96.2 9.7 %all_to_all.41 = f32[8,16,128]{2,1,0:T(8,128)S(1)} all-to-all(f32[8,16,128]{2,1,0:T(8,128)S(1)} %broadcast_in_dim.75), channel_id=1, replica_groups={{0,2,4,6,8,10,12,14},{1,3,5,7,9,11,13,15},{16,18,20,22,24,26,28,30},{17..., dimensions={0} | all-to-all | bytes 131072 | tf_op jit(solution)/shard_map/all_to_all | solution.py:250
  105.9 1.2 broadcast_in_dim.76
  107.1 7.5 %all-to-all-start.4 = ((f32[32,5,16,128]{3,2,1,0:T(8,128)}), f32[32,5,16,128]{3,2,1,0:T(8,128)S(1)}, u32[]{:S(2)}, u32[]{:S(2)}) async-start(f32[32,5,16,128]{3,2,1,0:T(8,128)} %broadcast_in_dim.76), calls=%async_computation.4 | async-start | bytes 2621440 | tf_op jit(solution)/shard_map/all_to_all | solution.py:250
  114.8 1.3 copy.36
  118.0 1.3 copy.34
  119.3 1.9 copy.35
  121.3 1.8 fusion
  123.1 3.1 %convolution_subtract_fusion = f32[256,1024]{1,0:T(8,128)} fusion(bf16[1024,1024]{1,0:T(8,128)(2,1)S(1)} %bitcast.48, f32[256,1024]{1,0:T(8,128)} %copy.34, bf16[512,256]{1,0:T(8,128)(2,1)} %slice.80, bf16[512,256]{1,0:T(8,128)(2,1)} %slice.79, pred[1024]{0:T(1024)(128)(4,1)S(1)} %fusion.8), kind=kOutput, calls=%fused_computation.2 | convolution fusion | flops 538443776 | bytes 4719616 | tf_op jit(solution)/shard_map/dot_general | solution.py:332
  126.2 19.2 %all-to-all-done.4.mine_ref = f32[32,5,16,128]{3,2,1,0:T(8,128)S(1)} async-done(((f32[32,5,16,128]{3,2,1,0:T(8,128)}), f32[32,5,16,128]{3,2,1,0:T(8,128)S(1)}, u32[]{:S(2)}, u32[]{:S(2)}) %all-to-all-start.4) | async-done | bytes 1310752 | tf_op jit(solution)/shard_map/all_to_all | solution.py:250
  145.4 7.2 %all-to-all-start.5 = ((f32[16,16,1024]{2,1,0:T(8,128)}), f32[16,16,1024]{2,1,0:T(8,128)S(1)}, u32[]{:S(2)}, u32[]{:S(2)}) async-start(f32[16,16,1024]{2,1,0:T(8,128)} %bitcast.51), calls=%async_computation.5 | async-start | bytes 2097152 | tf_op jit(solution)/shard_map/all_to_all | solution.py:341
  152.6 2.3 collective-permute-start.4
  155.0 2.6 %collective-permute-done.4.other_ref = f32[32,5,16,128]{3,2,1,0:T(8,128)S(1)} collective-permute-done((f32[32,5,16,128]{3,2,1,0:T(8,128)S(1)}, f32[32,5,16,128]{3,2,1,0:T(8,128)S(1)}, u32[]{:S(2)}, u32[]{:S(2)}) %collective-permute-start.4) | collective-permute-done | bytes 1310752 | tf_op jit(solution)/shard_map/ppermute | solution.py:337
  157.6 38.1 %shard_map.59.from_ref = f32[4,1024,256]{2,1,0:T(8,128)} custom-call(s32[1]{0:T(128)} %bitcast.core_ref, f32[32,5,16,128]{3,2,1,0:T(8,128)S(1)} %all-to-all-done.4.mine_ref, f32[32,5,16,128]{3,2,1,0:T(8,128)S(1)} %collective-permute-done.4.other_ref), custom_call_target="tpu_custom_call" | custom-call | flops 1073741824 | bytes 8388608 | tf_op jit(solution)/shard_map/pallas_call | solution.py:208
  195.8 0.8 copy-done
  196.6 5.0 %shard_map.60 = (f32[16,1024]{1,0:T(8,128)S(1)}, f32[16,1024]{1,0:T(8,128)S(1)}) custom-call(f32[4,1024,256]{2,1,0:T(8,128)} %shard_map.59.from_ref, f32[16,1024]{1,0:T(8,128)S(1)} %copy-done, f32[16,1024]{1,0:T(8,128)S(1)} %reduce_sum.19.v_ref), custom_call_target="tpu_custom_call" | custom-call | tf_op jit(solution)/shard_map/pallas_call | solution.py:227
  202.7 5.4 %all-to-all-start.6 = ((f32[32,1,512]{2,1,0:T(1,128)}), f32[32,1,512]{2,1,0:T(1,128)S(1)}, u32[]{:S(2)}, u32[]{:S(2)}) async-start(f32[32,1,512]{2,1,0:T(1,128)} %reshape.156), calls=%async_computation.7 | async-start | bytes 131072 | tf_op jit(solution)/shard_map/all_to_all | solution.py:348
  208.3 8.6 %all-to-all-done.6 = f32[32,1,512]{2,1,0:T(1,128)S(1)} async-done(((f32[32,1,512]{2,1,0:T(1,128)}), f32[32,1,512]{2,1,0:T(1,128)S(1)}, u32[]{:S(2)}, u32[]{:S(2)}) %all-to-all-start.6) | async-done | bytes 65568 | tf_op jit(solution)/shard_map/all_to_all | solution.py:348
  217.4 0.8 reduce
  218.6 17.7 %all_to_all.42 = f32[16,16,128]{2,1,0:T(8,128)S(1)} all-to-all(f32[16,16,128]{2,1,0:T(8,128)S(1)} %pad_maximum_fusion.1), channel_id=1, replica_groups=mesh['row'=32,'col'=16] {'col'}, dimensions={0} | all-to-all | bytes 262144 | tf_op jit(solution)/shard_map/all_to_all | solution.py:354
  (82 shorter events, 9.0 us)
Async XLA Ops:
  10.0 37.8 %slice-start = ((f32[256,64]{0,1:T(8,128)}), f32[32,64]{0,1:T(8,128)S(1)}, s32[]{:S(2)}) async-start(f32[256,64]{0,1:T(8,128)} %param.4), calls=%async_computation.11 | async-start | bytes 65536 | tf_op jit(solution)/shard_map/slice | solution.py:293
  11.0 51.1 %all-to-all-start = ((bf16[8,32,1024]{2,1,0:T(8,128)(2,1)}), bf16[8,32,1024]{2,1,0:T(8,128)(2,1)S(1)}, u32[]{:S(2)}, u32[]{:S(2)}) async-start(bf16[8,32,1024]{2,1,0:T(8,128)(2,1)} %broadcast_in_dim.70), calls=%async_computation | async-start | bytes 1048576 | tf_op jit(solution)/shard_map/all_to_all | solution.py:250
  18.7 29.4 %collective-permute-start = (bf16[608,128]{1,0:T(8,128)(2,1)S(1)}, bf16[608,128]{1,0:T(8,128)(2,1)S(1)}, u32[]{:S(2)}, u32[]{:S(2)}) collective-permute-start(bf16[608,128]{1,0:T(8,128)(2,1)S(1)} %get-tuple-element.21), channel_id=1, source_target_pairs={{0,0},{1,32},{2,64},{3,96},{4,128},{5,160},{6,192},{7,224},{8,256}... | collective-permute-start | bytes 466952 | tf_op jit(solution)/shard_map/ppermute | solution.py:291
  24.2 23.9 %collective-permute-start.1 = (bf16[608,128]{1,0:T(8,128)(2,1)S(1)}, bf16[608,128]{1,0:T(8,128)(2,1)S(1)}, u32[]{:S(2)}, u32[]{:S(2)}) collective-permute-start(bf16[608,128]{1,0:T(8,128)(2,1)S(1)} %get-tuple-element.22), channel_id=1, source_target_pairs={{0,256},{1,288},{2,320},{3,352},{4,384},{5,416},{6,448},{7,480},{8... | collective-permute-start | bytes 466952 | tf_op jit(solution)/shard_map/ppermute | solution.py:291
  39.0 9.1 %collective-permute-start.2 = (bf16[608,128]{1,0:T(8,128)(2,1)S(1)}, bf16[608,128]{1,0:T(8,128)(2,1)S(1)}, u32[]{:S(2)}, u32[]{:S(2)}) collective-permute-start(bf16[608,128]{1,0:T(8,128)(2,1)S(1)} %get-tuple-element.23), channel_id=1, source_target_pairs={{0,16},{1,48},{2,80},{3,112},{4,144},{5,176},{6,208},{7,240},{8,27... | collective-permute-start | bytes 466952 | tf_op jit(solution)/shard_map/ppermute | solution.py:291
  44.2 17.9 %collective-permute-start.3 = (bf16[608,128]{1,0:T(8,128)(2,1)S(1)}, bf16[608,128]{1,0:T(8,128)(2,1)S(1)}, u32[]{:S(2)}, u32[]{:S(2)}) collective-permute-start(bf16[608,128]{1,0:T(8,128)(2,1)S(1)} %get-tuple-element.24), channel_id=1, source_target_pairs={{0,272},{1,304},{2,336},{3,368},{4,400},{5,432},{6,464},{7,496},{8... | collective-permute-start | bytes 466952 | tf_op jit(solution)/shard_map/ppermute | solution.py:291
  62.1 4.6 %copy-start.2 = (bf16[8,32,1024]{2,1,0:T(8,128)(2,1)}, bf16[8,32,1024]{2,1,0:T(8,128)(2,1)S(1)}, u32[]{:S(2)}) copy-start(bf16[8,32,1024]{2,1,0:T(8,128)(2,1)S(1)} %all-to-all-done) | copy-start | bytes 1572868
  62.9 9.9 %all-to-all-start.1 = ((bf16[4,32,1216]{2,1,0:T(8,128)(2,1)}), bf16[4,32,1216]{2,1,0:T(8,128)(2,1)S(1)}, u32[]{:S(2)}, u32[]{:S(2)}) async-start(bf16[4,32,1216]{2,1,0:T(8,128)(2,1)} %broadcast_in_dim.71), calls=%async_computation.1 | async-start | bytes 655360 | tf_op jit(solution)/shard_map/all_to_all | solution.py:250
  66.4 52.9 %all-gather.2.cloned.1.call-start = ((), (), s32[]{:S(2)}) async-start(), calls=%async_computation.9 | async-start | bytes 2621440 | tf_op jit(solution)/shard_map/all_gather | solution.py:324
  72.8 1.0 copy-start.3
  107.1 7.6 %copy-start.5 = (f32[256,64]{0,1:T(8,128)S(1)}, f32[256,64]{0,1:T(8,128)}, u32[]{:S(2)}) copy-start(f32[256,64]{0,1:T(8,128)} %param.4) | copy-start | bytes 196612
  107.1 38.3 %all-to-all-start.4 = ((f32[32,5,16,128]{3,2,1,0:T(8,128)}), f32[32,5,16,128]{3,2,1,0:T(8,128)S(1)}, u32[]{:S(2)}, u32[]{:S(2)}) async-start(f32[32,5,16,128]{3,2,1,0:T(8,128)} %broadcast_in_dim.76), calls=%async_computation.4 | async-start | bytes 2621440 | tf_op jit(solution)/shard_map/all_to_all | solution.py:250
  114.7 81.0 %reduce-scatter.2.cloned.1.call-start = ((), (), s32[]{:S(2)}) async-start(), calls=%async_computation.10 | async-start | bytes 1114112 | tf_op jit(solution)/shard_map/reduce_scatter | solution.py:338
  119.3 1.9 copy-start.1
  119.3 2.0 copy-start.4
  145.4 50.2 %all-to-all-start.5 = ((f32[16,16,1024]{2,1,0:T(8,128)}), f32[16,16,1024]{2,1,0:T(8,128)S(1)}, u32[]{:S(2)}, u32[]{:S(2)}) async-start(f32[16,16,1024]{2,1,0:T(8,128)} %bitcast.51), calls=%async_computation.5 | async-start | bytes 2097152 | tf_op jit(solution)/shard_map/all_to_all | solution.py:341
  152.6 4.9 %collective-permute-start.4 = (f32[32,5,16,128]{3,2,1,0:T(8,128)S(1)}, f32[32,5,16,128]{3,2,1,0:T(8,128)S(1)}, u32[]{:S(2)}, u32[]{:S(2)}) collective-permute-start(f32[32,5,16,128]{3,2,1,0:T(8,128)S(1)} %all-to-all-done.4.mine_ref), channel_id=1, source_target_pairs={{0,1},{1,0},{2,3},{3,2},{4,5},{5,4},{6,7},{7,6},{8,9},{9,8},{10,11... | collective-permute-start | bytes 3932168 | tf_op jit(solution)/shard_map/ppermute | solution.py:337
  195.8 0.8 copy-start
  202.7 14.2 %all-to-all-start.6 = ((f32[32,1,512]{2,1,0:T(1,128)}), f32[32,1,512]{2,1,0:T(1,128)S(1)}, u32[]{:S(2)}, u32[]{:S(2)}) async-start(f32[32,1,512]{2,1,0:T(1,128)} %reshape.156), calls=%async_computation.7 | async-start | bytes 131072 | tf_op jit(solution)/shard_map/all_to_all | solution.py:348
Sparse Core Ops, SparseCore 0:
  69.3 41.0 all-gather.1
  123.2 63.3 reduce-scatter.1

commit v11 on v10

--- a/solution.py
+++ b/solution.py
@@ -288,19 +288,11 @@
                     pairs.append((r * col_count + c, to_row % row_count * col_count + r // per_col))
             routes.append(pairs)
     own, *sends = lax.optimization_barrier((own, *sends))
-    parts = [lax.ppermute(sent, ("row", "col"), pairs) for sent, pairs in zip(sends, routes)]
+    parts = [lax.ppermute(sent, ("row", "col"), pairs) for sent, pairs in zip(sends[:spread], routes[:spread])]
     from_y, *parts = lax.optimization_barrier((collect(own, "row", tall, along_y), *parts))
     packed = jnp.concatenate([own] + split_three(gram_panel[:block_rows]), axis=1)
     packed, from_y = lax.optimization_barrier((packed, from_y))
     from_x = collect(packed, "row", wide, along_x)
-    pieces = [jnp.concatenate(parts[turn * spread:(turn + 1) * spread], axis=1) for turn in range(per_col)]
-    flip = (row_place % per_col) == 1
-    first = jnp.where(flip, pieces[1], pieces[0])
-    second = jnp.where(flip, pieces[0], pieces[1])
-    solved_here = jnp.concatenate([first[:prev_rows], second[:prev_rows]], axis=0)
-    right_here = jnp.concatenate([first[prev_rows:], second[prev_rows:]], axis=0).astype(jnp.float32)
-    right_here = right_here.reshape(per_col, 3, block_rows, vox_part)
-    right_here = (right_here[:, 0] + right_here[:, 1] + right_here[:, 2]).reshape(col_width, vox_part)
     rows_x = from_x[:, :, :depth].reshape(wide * block_rows, depth)
     rows_y = from_y.reshape(tall * block_rows, depth)
     gram_x = from_x[:, :, depth:].astype(jnp.float32).reshape(wide * block_rows, 3, per_col, block_rows)
@@ -322,18 +314,29 @@
     diag_z = collect(own_diag, "col", chips, along_z)
 
     chosen = lax.all_gather(rows_y, "row", axis=0, tiled=False, axis_index_groups=along_x)
+    diag_z, chosen, *late = lax.optimization_barrier((diag_z[:kept], chosen, *sends[spread:]))
     chosen = chosen.reshape(wide, tall, block_rows, depth).transpose(1, 0, 2, 3).reshape(panel, depth)
     at_col = lane // col_width == col_place
     gram_placed = jnp.where(at_col, jnp.tile(gram_panel, (1, col_count)), 0.0)
     update_part = gram_placed - lax.dot_general(
         left_factor, chosen, (((1,), (1,)), ((), ())), preferred_element_type=jnp.float32
     )
+    late = [lax.ppermute(sent, ("row", "col"), pairs) for sent, pairs in zip(late, routes[spread:])]
+    diag_row, *late = lax.optimization_barrier((collect(diag_z, "row", row_count), *late))
+    parts += late
+    pieces = [jnp.concatenate(parts[turn * spread:(turn + 1) * spread], axis=1) for turn in range(per_col)]
+    flip = (row_place % per_col) == 1
+    first = jnp.where(flip, pieces[1], pieces[0])
+    second = jnp.where(flip, pieces[0], pieces[1])
+    solved_here = jnp.concatenate([first[:prev_rows], second[:prev_rows]], axis=0)
+    right_here = jnp.concatenate([first[prev_rows:], second[prev_rows:]], axis=0).astype(jnp.float32)
+    right_here = right_here.reshape(per_col, 3, block_rows, vox_part)
+    right_here = (right_here[:, 0] + right_here[:, 1] + right_here[:, 2]).reshape(col_width, vox_part)
     right_placed = jnp.where(at_col, jnp.tile(right_here.T, (1, col_count)), 0.0)
     product = right_placed - lax.dot_general(
         solved_here, chosen, (((0,), (1,)), ((), ())), preferred_element_type=jnp.float32
     )
 
-    diag_row = collect(diag_z[:kept], "row", row_count)
     other = lax.ppermute(diag_row, "col", [(i, i ^ 1) for i in range(col_count)])
     update = lax.psum_scatter(update_part, "col", scatter_dimension=0, tiled=True)
     product = product.reshape(col_count, vox_part // col_count, panel)

time: 246 us -> 259 us (1.053)
  waiting for transfers between devices: 50.6 us -> 31.6 us
  starting transfers between devices: 62.8 us -> 81.2 us
  blocking collectives: 49.3 us -> 56.7 us
  local copies, waits for them, and re-layouts: 16 us -> 21.6 us
    all_to_all x3, waiting for transfers between devices: 24.9 us -> 8.79 us  [collect(): return lax.all_to_all(many, axis, 0, 0, axis_index_groups=groups)]
    all_to_all x1, starting transfers between devices: 7.2 us -> 21.6 us  [body(): spread_out = lax.all_to_all(product, 'col', 0, 0)]
    all_to_all x1, blocking collectives: 22 us -> 29.5 us  [body(): own_diag = jnp.sum(lax.all_to_all(partial, 'col', 0, 0), axis=0)]
    ppermute x4, starting transfers between devices: 29.2 us -> 33.7 us  [body(): lax.ppermute(sent, ('row', 'col'), pairs)]
    ppermute x4, waiting for transfers between devices: 14.1 us -> 11.5 us  [body(): lax.ppermute(sent, ('row', 'col'), pairs)]
    unnamed x23 -> x25, local copies, waits for them, and re-layouts: 3.61 us -> 5.32 us
  transfers between devices with their start and end apart: 12 -> 12, of which waited for: 5 -> 6; matrix products, arithmetic and copies ran while one was open for 6% -> 7% of each run, Pallas kernels for 16% -> 15%
where the time goes in v11:
time: 259 us; the launch traced here: 258 us
  starting transfers between devices  81.2 us (31%)
  blocking collectives  56.7 us (22%)
  Pallas kernels  43.1 us (17%)
  waiting for transfers between devices  31.6 us (12%)
  local copies, waits for them, and re-layouts  21.6 us (8%)
  between operations  14.7 us (6%)
  matrix products  5.2 us (2%)
  other arithmetic  4.18 us (2%)
    pallas_call x1, Pallas kernels, factor(): pl.pallas_call(factor_kernel, out_shape=pltpu.HBM((big, panel, 256), jnp....  38.1 us
    ppermute x4, starting transfers between devices, body(): lax.ppermute(sent, ('row', 'col'), pairs)  33.7 us
    all_to_all x1, blocking collectives, body(): own_diag = jnp.sum(lax.all_to_all(partial, 'col', 0, 0), axis=0)  29.5 us
    all_to_all x1, starting transfers between devices, body(): spread_out = lax.all_to_all(product, 'col', 0, 0)  21.6 us
    all_to_all x3, starting transfers between devices, collect(): return lax.all_to_all(many, axis, 0, 0, axis_index_groups=groups)  18.9 us
    all_to_all x1, blocking collectives, body(): lax.all_to_all(both.reshape(col_count, -1, 128), 'col', 0, 0)  17.6 us
    ppermute x4, waiting for transfers between devices, body(): lax.ppermute(sent, ('row', 'col'), pairs)  11.5 us
    all_to_all x1, blocking collectives, collect(): return lax.all_to_all(many, axis, 0, 0, axis_index_groups=groups)  9.7 us
  transfers between devices with their start and end apart: 12, of which 6 were waited for; matrix products, arithmetic and copies ran while one was open for 7% of the time, Pallas kernels for 15%

profile of v11, /device:TPU:1, one launch (start us, length us, event | category | flops | bytes accessed | tf_op | source)
XLA Modules:
  0.0 258.3 jit_solution(11806149771743942158)
XLA Ops:
  8.9 1.1 pad_maximum_fusion
  11.8 7.7 %all-to-all-start = ((bf16[8,32,1024]{2,1,0:T(8,128)(2,1)}), bf16[8,32,1024]{2,1,0:T(8,128)(2,1)S(1)}, u32[]{:S(2)}, u32[]{:S(2)}) async-start(bf16[8,32,1024]{2,1,0:T(8,128)(2,1)} %broadcast_in_dim.70), calls=%async_computation | async-start | bytes 1048576 | tf_op jit(solution)/shard_map/all_to_all | solution.py:250
  19.4 5.5 %collective-permute-start = (bf16[608,128]{1,0:T(8,128)(2,1)S(1)}, bf16[608,128]{1,0:T(8,128)(2,1)S(1)}, u32[]{:S(2)}, u32[]{:S(2)}) collective-permute-start(bf16[608,128]{1,0:T(8,128)(2,1)S(1)} %get-tuple-element.26), channel_id=1, source_target_pairs={{0,0},{1,32},{2,64},{3,96},{4,128},{5,160},{6,192},{7,224},{8,256}... | collective-permute-start | bytes 466952 | tf_op jit(solution)/shard_map/ppermute | solution.py:291
  24.9 14.8 %collective-permute-start.1 = (bf16[608,128]{1,0:T(8,128)(2,1)S(1)}, bf16[608,128]{1,0:T(8,128)(2,1)S(1)}, u32[]{:S(2)}, u32[]{:S(2)}) collective-permute-start(bf16[608,128]{1,0:T(8,128)(2,1)S(1)} %get-tuple-element.27), channel_id=1, source_target_pairs={{0,256},{1,288},{2,320},{3,352},{4,384},{5,416},{6,448},{7,480},{8... | collective-permute-start | bytes 466952 | tf_op jit(solution)/shard_map/ppermute | solution.py:291
  40.0 2.8 %collective-permute-done.1 = bf16[608,128]{1,0:T(8,128)(2,1)S(1)} collective-permute-done((bf16[608,128]{1,0:T(8,128)(2,1)S(1)}, bf16[608,128]{1,0:T(8,128)(2,1)S(1)}, u32[]{:S(2)}, u32[]{:S(2)}) %collective-permute-start.1) | collective-permute-done | bytes 155680 | tf_op jit(solution)/shard_map/ppermute | solution.py:291
  44.3 3.5 %all-to-all-start.1 = ((bf16[4,32,1216]{2,1,0:T(8,128)(2,1)}), bf16[4,32,1216]{2,1,0:T(8,128)(2,1)S(1)}, u32[]{:S(2)}, u32[]{:S(2)}) async-start(bf16[4,32,1216]{2,1,0:T(8,128)(2,1)} %broadcast_in_dim.71), calls=%async_computation.1 | async-start | bytes 655360 | tf_op jit(solution)/shard_map/all_to_all | solution.py:250
  48.1 5.6 %all-to-all-done.1 = bf16[4,32,1216]{2,1,0:T(8,128)(2,1)S(1)} async-done(((bf16[4,32,1216]{2,1,0:T(8,128)(2,1)}), bf16[4,32,1216]{2,1,0:T(8,128)(2,1)S(1)}, u32[]{:S(2)}, u32[]{:S(2)}) %all-to-all-start.1) | async-done | bytes 311328 | tf_op jit(solution)/shard_map/all_to_all | solution.py:250
  55.1 29.5 %all_to_all.40 = f32[16,16,128]{2,1,0:T(8,128)S(1)} all-to-all(f32[16,16,128]{2,1,0:T(8,128)S(1)} %bitcast.60), channel_id=1, replica_groups=mesh['row'=32,'col'=16] {'col'}, dimensions={0} | all-to-all | bytes 262144 | tf_op jit(solution)/shard_map/all_to_all | solution.py:313
  84.6 9.7 %all_to_all.41 = f32[8,16,128]{2,1,0:T(8,128)S(1)} all-to-all(f32[8,16,128]{2,1,0:T(8,128)S(1)} %broadcast_in_dim.75), channel_id=1, replica_groups={{0,2,4,6,8,10,12,14},{1,3,5,7,9,11,13,15},{16,18,20,22,24,26,28,30},{17..., dimensions={0} | all-to-all | bytes 131072 | tf_op jit(solution)/shard_map/all_to_all | solution.py:250
  94.3 1.2 broadcast_in_dim.76
  95.5 7.8 %all-to-all-start.4 = ((f32[32,5,16,128]{3,2,1,0:T(8,128)}), f32[32,5,16,128]{3,2,1,0:T(8,128)S(1)}, u32[]{:S(2)}, u32[]{:S(2)}) async-start(f32[32,5,16,128]{3,2,1,0:T(8,128)} %broadcast_in_dim.76), calls=%async_computation.4 | async-start | bytes 2621440 | tf_op jit(solution)/shard_map/all_to_all | solution.py:250
  103.5 1.3 copy.36
  104.9 6.1 %collective-permute-start.2 = (bf16[608,128]{1,0:T(8,128)(2,1)}, bf16[608,128]{1,0:T(8,128)(2,1)}, u32[]{:S(2)}, u32[]{:S(2)}) collective-permute-start(bf16[608,128]{1,0:T(8,128)(2,1)} %get-tuple-element.34), channel_id=1, source_target_pairs={{0,16},{1,48},{2,80},{3,112},{4,144},{5,176},{6,208},{7,240},{8,27... | collective-permute-start | bytes 466952 | tf_op jit(solution)/shard_map/ppermute | solution.py:324
  111.0 7.3 %collective-permute-start.3 = (bf16[608,128]{1,0:T(8,128)(2,1)}, bf16[608,128]{1,0:T(8,128)(2,1)}, u32[]{:S(2)}, u32[]{:S(2)}) collective-permute-start(bf16[608,128]{1,0:T(8,128)(2,1)} %get-tuple-element.35), channel_id=1, source_target_pairs={{0,272},{1,304},{2,336},{3,368},{4,400},{5,432},{6,464},{7,496},{8... | collective-permute-start | bytes 466952 | tf_op jit(solution)/shard_map/ppermute | solution.py:324
  118.3 1.9 copy.35
  120.3 1.8 fusion
  122.0 8.7 %collective-permute-done.3 = bf16[608,128]{1,0:T(8,128)(2,1)} collective-permute-done((bf16[608,128]{1,0:T(8,128)(2,1)}, bf16[608,128]{1,0:T(8,128)(2,1)}, u32[]{:S(2)}, u32[]{:S(2)}) %collective-permute-start.3) | collective-permute-done | bytes 155680 | tf_op jit(solution)/shard_map/ppermute | solution.py:324
  130.7 3.2 %all-to-all-done.4.mine_ref = f32[32,5,16,128]{3,2,1,0:T(8,128)S(1)} async-done(((f32[32,5,16,128]{3,2,1,0:T(8,128)}), f32[32,5,16,128]{3,2,1,0:T(8,128)S(1)}, u32[]{:S(2)}, u32[]{:S(2)}) %all-to-all-start.4) | async-done | bytes 1310752 | tf_op jit(solution)/shard_map/all_to_all | solution.py:250
  133.9 0.9 constant_dynamic-update-slice_fusion.1
  134.9 1.0 constant_dynamic-update-slice_fusion
  135.8 1.0 broadcast_select_fusion.1
  138.4 1.1 tile.8
  139.5 2.5 copy.34
  142.0 3.1 %convolution_subtract_fusion = f32[256,1024]{1,0:T(8,128)} fusion(bf16[1024,1024]{1,0:T(8,128)(2,1)S(1)} %bitcast.48, f32[256,1024]{1,0:T(8,128)} %copy.34, bf16[512,256]{1,0:T(8,128)(2,1)} %slice.80, bf16[512,256]{1,0:T(8,128)(2,1)} %slice.79, pred[1024]{0:T(1024)(128)(4,1)S(1)} %fusion.8), kind=kOutput, calls=%fused_computation.2 | convolution fusion | flops 538443776 | bytes 4719616 | tf_op jit(solution)/shard_map/dot_general | solution.py:336
  145.2 21.6 %all-to-all-start.5 = ((f32[16,16,1024]{2,1,0:T(8,128)}), f32[16,16,1024]{2,1,0:T(8,128)S(1)}, u32[]{:S(2)}, u32[]{:S(2)}) async-start(f32[16,16,1024]{2,1,0:T(8,128)} %bitcast.51), calls=%async_computation.5 | async-start | bytes 2097152 | tf_op jit(solution)/shard_map/all_to_all | solution.py:344
  166.8 2.2 collective-permute-start.4
  169.0 2.7 %collective-permute-done.4.other_ref = f32[32,5,16,128]{3,2,1,0:T(8,128)S(1)} collective-permute-done((f32[32,5,16,128]{3,2,1,0:T(8,128)S(1)}, f32[32,5,16,128]{3,2,1,0:T(8,128)S(1)}, u32[]{:S(2)}, u32[]{:S(2)}) %collective-permute-start.4) | collective-permute-done | bytes 1310752 | tf_op jit(solution)/shard_map/ppermute | solution.py:340
  171.7 38.1 %shard_map.59.from_ref = f32[4,1024,256]{2,1,0:T(8,128)} custom-call(s32[1]{0:T(128)} %bitcast.core_ref, f32[32,5,16,128]{3,2,1,0:T(8,128)S(1)} %all-to-all-done.4.mine_ref, f32[32,5,16,128]{3,2,1,0:T(8,128)S(1)} %collective-permute-done.4.other_ref), custom_call_target="tpu_custom_call" | custom-call | flops 1073741824 | bytes 8388608 | tf_op jit(solution)/shard_map/pallas_call | solution.py:208
  210.8 5.0 %shard_map.60 = (f32[16,1024]{1,0:T(8,128)S(1)}, f32[16,1024]{1,0:T(8,128)S(1)}) custom-call(f32[4,1024,256]{2,1,0:T(8,128)} %shard_map.59.from_ref, f32[16,1024]{1,0:T(8,128)S(1)} %copy-done, f32[16,1024]{1,0:T(8,128)S(1)} %reduce_sum.19.v_ref), custom_call_target="tpu_custom_call" | custom-call | tf_op jit(solution)/shard_map/pallas_call | solution.py:227
  216.8 4.7 %all-to-all-start.6 = ((f32[32,1,512]{2,1,0:T(1,128)}), f32[32,1,512]{2,1,0:T(1,128)S(1)}, u32[]{:S(2)}, u32[]{:S(2)}) async-start(f32[32,1,512]{2,1,0:T(1,128)} %reshape.156), calls=%async_computation.7 | async-start | bytes 131072 | tf_op jit(solution)/shard_map/all_to_all | solution.py:351
  221.8 8.6 %all-to-all-done.6 = f32[32,1,512]{2,1,0:T(1,128)S(1)} async-done(((f32[32,1,512]{2,1,0:T(1,128)}), f32[32,1,512]{2,1,0:T(1,128)S(1)}, u32[]{:S(2)}, u32[]{:S(2)}) %all-to-all-start.6) | async-done | bytes 65568 | tf_op jit(solution)/shard_map/all_to_all | solution.py:351
  232.1 17.6 %all_to_all.42 = f32[16,16,128]{2,1,0:T(8,128)S(1)} all-to-all(f32[16,16,128]{2,1,0:T(8,128)S(1)} %pad_maximum_fusion.1), channel_id=1, replica_groups=mesh['row'=32,'col'=16] {'col'}, dimensions={0} | all-to-all | bytes 262144 | tf_op jit(solution)/shard_map/all_to_all | solution.py:357
  (85 shorter events, 14.1 us)
Async XLA Ops:
  10.0 29.8 %slice-start = ((f32[256,64]{0,1:T(8,128)}), f32[32,64]{0,1:T(8,128)S(1)}, s32[]{:S(2)}) async-start(f32[256,64]{0,1:T(8,128)} %param.4), calls=%async_computation.11 | async-start | bytes 65536 | tf_op jit(solution)/shard_map/slice | solution.py:293
  11.8 31.0 %all-to-all-start = ((bf16[8,32,1024]{2,1,0:T(8,128)(2,1)}), bf16[8,32,1024]{2,1,0:T(8,128)(2,1)S(1)}, u32[]{:S(2)}, u32[]{:S(2)}) async-start(bf16[8,32,1024]{2,1,0:T(8,128)(2,1)} %broadcast_in_dim.70), calls=%async_computation | async-start | bytes 1048576 | tf_op jit(solution)/shard_map/all_to_all | solution.py:250
  19.4 74.9 %all-gather.2.cloned.1.call-start = ((), (), s32[]{:S(2)}) async-start(), calls=%async_computation.9 | async-start | bytes 2621440 | tf_op jit(solution)/shard_map/all_gather | solution.py:316
  19.4 20.5 %collective-permute-start = (bf16[608,128]{1,0:T(8,128)(2,1)S(1)}, bf16[608,128]{1,0:T(8,128)(2,1)S(1)}, u32[]{:S(2)}, u32[]{:S(2)}) collective-permute-start(bf16[608,128]{1,0:T(8,128)(2,1)S(1)} %get-tuple-element.26), channel_id=1, source_target_pairs={{0,0},{1,32},{2,64},{3,96},{4,128},{5,160},{6,192},{7,224},{8,256}... | collective-permute-start | bytes 466952 | tf_op jit(solution)/shard_map/ppermute | solution.py:291
  24.9 17.8 %collective-permute-start.1 = (bf16[608,128]{1,0:T(8,128)(2,1)S(1)}, bf16[608,128]{1,0:T(8,128)(2,1)S(1)}, u32[]{:S(2)}, u32[]{:S(2)}) collective-permute-start(bf16[608,128]{1,0:T(8,128)(2,1)S(1)} %get-tuple-element.27), channel_id=1, source_target_pairs={{0,256},{1,288},{2,320},{3,352},{4,384},{5,416},{6,448},{7,480},{8... | collective-permute-start | bytes 466952 | tf_op jit(solution)/shard_map/ppermute | solution.py:291
  42.7 0.8 copy-start.2
  44.3 9.3 %all-to-all-start.1 = ((bf16[4,32,1216]{2,1,0:T(8,128)(2,1)}), bf16[4,32,1216]{2,1,0:T(8,128)(2,1)S(1)}, u32[]{:S(2)}, u32[]{:S(2)}) async-start(bf16[4,32,1216]{2,1,0:T(8,128)(2,1)} %broadcast_in_dim.71), calls=%async_computation.1 | async-start | bytes 655360 | tf_op jit(solution)/shard_map/all_to_all | solution.py:250
  53.7 1.0 copy-start.3
  95.5 7.9 %copy-start.6 = (f32[256,64]{0,1:T(8,128)S(1)}, f32[256,64]{0,1:T(8,128)}, u32[]{:S(2)}) copy-start(f32[256,64]{0,1:T(8,128)} %param.4) | copy-start | bytes 196612
  95.5 38.4 %all-to-all-start.4 = ((f32[32,5,16,128]{3,2,1,0:T(8,128)}), f32[32,5,16,128]{3,2,1,0:T(8,128)S(1)}, u32[]{:S(2)}, u32[]{:S(2)}) async-start(f32[32,5,16,128]{3,2,1,0:T(8,128)} %broadcast_in_dim.76), calls=%async_computation.4 | async-start | bytes 2621440 | tf_op jit(solution)/shard_map/all_to_all | solution.py:250
  103.3 106.6 %reduce-scatter.2.cloned.1.call-start = ((), (), s32[]{:S(2)}) async-start(), calls=%async_computation.10 | async-start | bytes 1114112 | tf_op jit(solution)/shard_map/reduce_scatter | solution.py:341
  104.9 13.4 %copy-start.4 = (bf16[608,256]{1,0:T(8,128)(2,1)}, bf16[608,256]{1,0:T(8,128)(2,1)S(1)}, u32[]{:S(2)}) copy-start(bf16[608,256]{1,0:T(8,128)(2,1)S(1)} %constant_dynamic-update-slice_fusion.2) | copy-start | bytes 933892
  104.9 17.2 %collective-permute-start.2 = (bf16[608,128]{1,0:T(8,128)(2,1)}, bf16[608,128]{1,0:T(8,128)(2,1)}, u32[]{:S(2)}, u32[]{:S(2)}) collective-permute-start(bf16[608,128]{1,0:T(8,128)(2,1)} %get-tuple-element.34), channel_id=1, source_target_pairs={{0,16},{1,48},{2,80},{3,112},{4,144},{5,176},{6,208},{7,240},{8,27... | collective-permute-start | bytes 466952 | tf_op jit(solution)/shard_map/ppermute | solution.py:324
  111.0 19.7 %collective-permute-start.3 = (bf16[608,128]{1,0:T(8,128)(2,1)}, bf16[608,128]{1,0:T(8,128)(2,1)}, u32[]{:S(2)}, u32[]{:S(2)}) collective-permute-start(bf16[608,128]{1,0:T(8,128)(2,1)} %get-tuple-element.35), channel_id=1, source_target_pairs={{0,272},{1,304},{2,336},{3,368},{4,400},{5,432},{6,464},{7,496},{8... | collective-permute-start | bytes 466952 | tf_op jit(solution)/shard_map/ppermute | solution.py:324
  118.3 2.0 copy-start.1
  118.3 2.0 copy-start.5
  145.2 64.7 %all-to-all-start.5 = ((f32[16,16,1024]{2,1,0:T(8,128)}), f32[16,16,1024]{2,1,0:T(8,128)S(1)}, u32[]{:S(2)}, u32[]{:S(2)}) async-start(f32[16,16,1024]{2,1,0:T(8,128)} %bitcast.51), calls=%async_computation.5 | async-start | bytes 2097152 | tf_op jit(solution)/shard_map/all_to_all | solution.py:344
  166.8 4.9 %collective-permute-start.4 = (f32[32,5,16,128]{3,2,1,0:T(8,128)S(1)}, f32[32,5,16,128]{3,2,1,0:T(8,128)S(1)}, u32[]{:S(2)}, u32[]{:S(2)}) collective-permute-start(f32[32,5,16,128]{3,2,1,0:T(8,128)S(1)} %all-to-all-done.4.mine_ref), channel_id=1, source_target_pairs={{0,1},{1,0},{2,3},{3,2},{4,5},{5,4},{6,7},{7,6},{8,9},{9,8},{10,11... | collective-permute-start | bytes 3932168 | tf_op jit(solution)/shard_map/ppermute | solution.py:340
  209.9 0.8 copy-start
  216.8 13.6 %all-to-all-start.6 = ((f32[32,1,512]{2,1,0:T(1,128)}), f32[32,1,512]{2,1,0:T(1,128)S(1)}, u32[]{:S(2)}, u32[]{:S(2)}) async-start(f32[32,1,512]{2,1,0:T(1,128)} %reshape.156), calls=%async_computation.7 | async-start | bytes 131072 | tf_op jit(solution)/shard_map/all_to_all | solution.py:351
Sparse Core Ops, SparseCore 0:
  43.7 46.4 all-gather.1
  122.2 66.7 reduce-scatter.1

commit v12 on v10

--- a/solution.py
+++ b/solution.py
@@ -287,7 +287,6 @@
                     to_row = per_col * c + (r + turn) % per_col + q * (row_count // spread)
                     pairs.append((r * col_count + c, to_row % row_count * col_count + r // per_col))
             routes.append(pairs)
-    own, *sends = lax.optimization_barrier((own, *sends))
     parts = [lax.ppermute(sent, ("row", "col"), pairs) for sent, pairs in zip(sends, routes)]
     from_y, *parts = lax.optimization_barrier((collect(own, "row", tall, along_y), *parts))
     packed = jnp.concatenate([own] + split_three(gram_panel[:block_rows]), axis=1)

time: 246 us -> 243 us (0.988)
  blocking collectives: 49.3 us -> 58.1 us
  waiting for transfers between devices: 50.6 us -> 42.9 us
    all_to_all x1, blocking collectives: 22 us -> 30.8 us  [body(): own_diag = jnp.sum(lax.all_to_all(partial, 'col', 0, 0), axis=0)]
    ppermute x4, waiting for transfers between devices: 14.1 us -> 6.87 us  [body(): lax.ppermute(sent, ('row', 'col'), pairs)]
where the time goes in v12:
time: 243 us; the launch traced here: 242 us
  starting transfers between devices  60.7 us (25%)
  blocking collectives  58.1 us (24%)
  Pallas kernels  43.1 us (18%)
  waiting for transfers between devices  42.9 us (18%)
  local copies, waits for them, and re-layouts  16 us (7%)
  between operations  14.6 us (6%)
  matrix products  5.21 us (2%)
    pallas_call x1, Pallas kernels, factor(): pl.pallas_call(factor_kernel, out_shape=pltpu.HBM((big, panel, 256), jnp....  38.1 us
    all_to_all x1, blocking collectives, body(): own_diag = jnp.sum(lax.all_to_all(partial, 'col', 0, 0), axis=0)  30.8 us
    ppermute x4, starting transfers between devices, body(): lax.ppermute(sent, ('row', 'col'), pairs)  28 us
    all_to_all x3, waiting for transfers between devices, collect(): return lax.all_to_all(many, axis, 0, 0, axis_index_groups=groups)  24.3 us
    all_to_all x3, starting transfers between devices, collect(): return lax.all_to_all(many, axis, 0, 0, axis_index_groups=groups)  17.7 us
    all_to_all x1, blocking collectives, body(): lax.all_to_all(both.reshape(col_count, -1, 128), 'col', 0, 0)  17.7 us
    all_to_all x1, blocking collectives, collect(): return lax.all_to_all(many, axis, 0, 0, axis_index_groups=groups)  9.7 us
    all_to_all x1, waiting for transfers between devices, body(): vox_out = lax.all_to_all(vox_out, 'row', 0, 0)  8.58 us
  transfers between devices with their start and end apart: 12, of which 5 were waited for; matrix products, arithmetic and copies ran while one was open for 6% of the time, Pallas kernels for 16%

profile of v12, /device:TPU:1, one launch (start us, length us, event | category | flops | bytes accessed | tf_op | source)
XLA Modules:
  0.0 242.0 jit_solution(17377151143109273905)
XLA Ops:
  7.2 0.9 slice.51
  8.1 0.9 broadcast_in_dim.70
  9.0 7.7 %all-to-all-start = ((bf16[8,32,1024]{2,1,0:T(8,128)(2,1)}), bf16[8,32,1024]{2,1,0:T(8,128)(2,1)S(1)}, u32[]{:S(2)}, u32[]{:S(2)}) async-start(bf16[8,32,1024]{2,1,0:T(8,128)(2,1)} %broadcast_in_dim.70), calls=%async_computation | async-start | bytes 1048576 | tf_op jit(solution)/shard_map/all_to_all | solution.py:250
  16.8 10.6 %collective-permute-start.3 = (bf16[608,128]{1,0:T(8,128)(2,1)S(1)}, bf16[608,128]{1,0:T(8,128)(2,1)S(1)}, u32[]{:S(2)}, u32[]{:S(2)}) collective-permute-start(bf16[608,128]{1,0:T(8,128)(2,1)S(1)} %get-tuple-element.36), channel_id=1, source_target_pairs={{0,272},{1,304},{2,336},{3,368},{4,400},{5,432},{6,464},{7,496},{8... | collective-permute-start | bytes 466952 | tf_op jit(solution)/shard_map/ppermute | solution.py:290
  27.4 1.9 collective-permute-start.2
  29.4 10.0 %collective-permute-start.1 = (bf16[608,128]{1,0:T(8,128)(2,1)S(1)}, bf16[608,128]{1,0:T(8,128)(2,1)S(1)}, u32[]{:S(2)}, u32[]{:S(2)}) collective-permute-start(bf16[608,128]{1,0:T(8,128)(2,1)S(1)} %get-tuple-element.38), channel_id=1, source_target_pairs={{0,256},{1,288},{2,320},{3,352},{4,384},{5,416},{6,448},{7,480},{8... | collective-permute-start | bytes 466952 | tf_op jit(solution)/shard_map/ppermute | solution.py:290
  39.4 5.5 %collective-permute-start = (bf16[608,128]{1,0:T(8,128)(2,1)S(1)}, bf16[608,128]{1,0:T(8,128)(2,1)S(1)}, u32[]{:S(2)}, u32[]{:S(2)}) collective-permute-start(bf16[608,128]{1,0:T(8,128)(2,1)S(1)} %get-tuple-element.39), channel_id=1, source_target_pairs={{0,0},{1,32},{2,64},{3,96},{4,128},{5,160},{6,192},{7,224},{8,256}... | collective-permute-start | bytes 466952 | tf_op jit(solution)/shard_map/ppermute | solution.py:290
  45.1 6.9 %collective-permute-done.1 = bf16[608,128]{1,0:T(8,128)(2,1)S(1)} collective-permute-done((bf16[608,128]{1,0:T(8,128)(2,1)S(1)}, bf16[608,128]{1,0:T(8,128)(2,1)S(1)}, u32[]{:S(2)}, u32[]{:S(2)}) %collective-permute-start.1) | collective-permute-done | bytes 155680 | tf_op jit(solution)/shard_map/ppermute | solution.py:290
  52.0 0.8 broadcast_in_dim.71
  52.8 3.5 %all-to-all-start.1 = ((bf16[4,32,1216]{2,1,0:T(8,128)(2,1)}), bf16[4,32,1216]{2,1,0:T(8,128)(2,1)S(1)}, u32[]{:S(2)}, u32[]{:S(2)}) async-start(bf16[4,32,1216]{2,1,0:T(8,128)(2,1)} %broadcast_in_dim.71), calls=%async_computation.1 | async-start | bytes 655360 | tf_op jit(solution)/shard_map/all_to_all | solution.py:250
  57.0 5.1 %all-to-all-done.1 = bf16[4,32,1216]{2,1,0:T(8,128)(2,1)S(1)} async-done(((bf16[4,32,1216]{2,1,0:T(8,128)(2,1)}), bf16[4,32,1216]{2,1,0:T(8,128)(2,1)S(1)}, u32[]{:S(2)}, u32[]{:S(2)}) %all-to-all-start.1) | async-done | bytes 311328 | tf_op jit(solution)/shard_map/all_to_all | solution.py:250
  63.5 30.8 %all_to_all.40 = f32[16,16,128]{2,1,0:T(8,128)S(1)} all-to-all(f32[16,16,128]{2,1,0:T(8,128)S(1)} %bitcast.60), channel_id=1, replica_groups=mesh['row'=32,'col'=16] {'col'}, dimensions={0} | all-to-all | bytes 262144 | tf_op jit(solution)/shard_map/all_to_all | solution.py:320
  94.3 9.7 %all_to_all.41 = f32[8,16,128]{2,1,0:T(8,128)S(1)} all-to-all(f32[8,16,128]{2,1,0:T(8,128)S(1)} %broadcast_in_dim.75), channel_id=1, replica_groups={{0,2,4,6,8,10,12,14},{1,3,5,7,9,11,13,15},{16,18,20,22,24,26,28,30},{17..., dimensions={0} | all-to-all | bytes 131072 | tf_op jit(solution)/shard_map/all_to_all | solution.py:250
  104.0 1.2 broadcast_in_dim.76
  105.2 6.6 %all-to-all-start.4 = ((f32[32,5,16,128]{3,2,1,0:T(8,128)}), f32[32,5,16,128]{3,2,1,0:T(8,128)S(1)}, u32[]{:S(2)}, u32[]{:S(2)}) async-start(f32[32,5,16,128]{3,2,1,0:T(8,128)} %broadcast_in_dim.76), calls=%async_computation.4 | async-start | bytes 2621440 | tf_op jit(solution)/shard_map/all_to_all | solution.py:250
  112.0 1.3 copy.36
  115.1 1.3 copy.34
  116.4 1.9 copy.35
  118.4 1.8 fusion
  120.2 3.1 %convolution_subtract_fusion = f32[256,1024]{1,0:T(8,128)} fusion(bf16[1024,1024]{1,0:T(8,128)(2,1)S(1)} %bitcast.48, f32[256,1024]{1,0:T(8,128)} %copy.34, bf16[512,256]{1,0:T(8,128)(2,1)} %slice.80, bf16[512,256]{1,0:T(8,128)(2,1)} %slice.79, pred[1024]{0:T(1024)(128)(4,1)S(1)} %fusion.8), kind=kOutput, calls=%fused_computation.2 | convolution fusion | flops 538443776 | bytes 4719616 | tf_op jit(solution)/shard_map/dot_general | solution.py:331
  123.4 19.2 %all-to-all-done.4.mine_ref = f32[32,5,16,128]{3,2,1,0:T(8,128)S(1)} async-done(((f32[32,5,16,128]{3,2,1,0:T(8,128)}), f32[32,5,16,128]{3,2,1,0:T(8,128)S(1)}, u32[]{:S(2)}, u32[]{:S(2)}) %all-to-all-start.4) | async-done | bytes 1310752 | tf_op jit(solution)/shard_map/all_to_all | solution.py:250
  142.6 7.2 %all-to-all-start.5 = ((f32[16,16,1024]{2,1,0:T(8,128)}), f32[16,16,1024]{2,1,0:T(8,128)S(1)}, u32[]{:S(2)}, u32[]{:S(2)}) async-start(f32[16,16,1024]{2,1,0:T(8,128)} %bitcast.51), calls=%async_computation.5 | async-start | bytes 2097152 | tf_op jit(solution)/shard_map/all_to_all | solution.py:340
  149.8 2.3 collective-permute-start.4
  152.1 2.6 %collective-permute-done.4.other_ref = f32[32,5,16,128]{3,2,1,0:T(8,128)S(1)} collective-permute-done((f32[32,5,16,128]{3,2,1,0:T(8,128)S(1)}, f32[32,5,16,128]{3,2,1,0:T(8,128)S(1)}, u32[]{:S(2)}, u32[]{:S(2)}) %collective-permute-start.4) | collective-permute-done | bytes 1310752 | tf_op jit(solution)/shard_map/ppermute | solution.py:336
  154.7 38.1 %shard_map.59.from_ref = f32[4,1024,256]{2,1,0:T(8,128)} custom-call(s32[1]{0:T(128)} %bitcast.core_ref, f32[32,5,16,128]{3,2,1,0:T(8,128)S(1)} %all-to-all-done.4.mine_ref, f32[32,5,16,128]{3,2,1,0:T(8,128)S(1)} %collective-permute-done.4.other_ref), custom_call_target="tpu_custom_call" | custom-call | flops 1073741824 | bytes 8388608 | tf_op jit(solution)/shard_map/pallas_call | solution.py:208
  192.9 0.8 copy-done
  193.8 5.0 %shard_map.60 = (f32[16,1024]{1,0:T(8,128)S(1)}, f32[16,1024]{1,0:T(8,128)S(1)}) custom-call(f32[4,1024,256]{2,1,0:T(8,128)} %shard_map.59.from_ref, f32[16,1024]{1,0:T(8,128)S(1)} %copy-done, f32[16,1024]{1,0:T(8,128)S(1)} %reduce_sum.19.v_ref), custom_call_target="tpu_custom_call" | custom-call | tf_op jit(solution)/shard_map/pallas_call | solution.py:227
  199.0 0.8 reshape.156
  199.8 5.4 %all-to-all-start.6 = ((f32[32,1,512]{2,1,0:T(1,128)}), f32[32,1,512]{2,1,0:T(1,128)S(1)}, u32[]{:S(2)}, u32[]{:S(2)}) async-start(f32[32,1,512]{2,1,0:T(1,128)} %reshape.156), calls=%async_computation.7 | async-start | bytes 131072 | tf_op jit(solution)/shard_map/all_to_all | solution.py:347
  205.5 8.6 %all-to-all-done.6 = f32[32,1,512]{2,1,0:T(1,128)S(1)} async-done(((f32[32,1,512]{2,1,0:T(1,128)}), f32[32,1,512]{2,1,0:T(1,128)S(1)}, u32[]{:S(2)}, u32[]{:S(2)}) %all-to-all-start.6) | async-done | bytes 65568 | tf_op jit(solution)/shard_map/all_to_all | solution.py:347
  214.6 0.8 reduce
  215.7 17.7 %all_to_all.42 = f32[16,16,128]{2,1,0:T(8,128)S(1)} all-to-all(f32[16,16,128]{2,1,0:T(8,128)S(1)} %pad_maximum_fusion.1), channel_id=1, replica_groups=mesh['row'=32,'col'=16] {'col'}, dimensions={0} | all-to-all | bytes 262144 | tf_op jit(solution)/shard_map/all_to_all | solution.py:353
  (86 shorter events, 7.5 us)
Async XLA Ops:
  7.2 9.5 %copy-start.7 = (f32[32,512]{1,0:T(8,128)S(1)}, f32[32,512]{1,0:T(8,128)}, u32[]{:S(2)}) copy-start(f32[32,512]{1,0:T(8,128)} %param.7) | copy-start | bytes 196612
  7.2 9.5 %copy-start.5 = (bf16[512,512]{1,0:T(8,128)(2,1)S(1)}, bf16[512,512]{1,0:T(8,128)(2,1)}, u32[]{:S(2)}) copy-start(bf16[512,512]{1,0:T(8,128)(2,1)} %param.6) | copy-start | bytes 1572868
  9.0 43.0 %all-to-all-start = ((bf16[8,32,1024]{2,1,0:T(8,128)(2,1)}), bf16[8,32,1024]{2,1,0:T(8,128)(2,1)S(1)}, u32[]{:S(2)}, u32[]{:S(2)}) async-start(bf16[8,32,1024]{2,1,0:T(8,128)(2,1)} %broadcast_in_dim.70), calls=%async_computation | async-start | bytes 1048576 | tf_op jit(solution)/shard_map/all_to_all | solution.py:250
  16.6 28.3 %slice-start = ((f32[256,64]{0,1:T(8,128)}), f32[32,64]{0,1:T(8,128)S(1)}, s32[]{:S(2)}) async-start(f32[256,64]{0,1:T(8,128)} %param.4), calls=%async_computation.11 | async-start | bytes 65536 | tf_op jit(solution)/shard_map/slice | solution.py:292
  16.8 28.2 %collective-permute-start.3 = (bf16[608,128]{1,0:T(8,128)(2,1)S(1)}, bf16[608,128]{1,0:T(8,128)(2,1)S(1)}, u32[]{:S(2)}, u32[]{:S(2)}) collective-permute-start(bf16[608,128]{1,0:T(8,128)(2,1)S(1)} %get-tuple-element.36), channel_id=1, source_target_pairs={{0,272},{1,304},{2,336},{3,368},{4,400},{5,432},{6,464},{7,496},{8... | collective-permute-start | bytes 466952 | tf_op jit(solution)/shard_map/ppermute | solution.py:290
  27.4 17.7 %collective-permute-start.2 = (bf16[608,128]{1,0:T(8,128)(2,1)S(1)}, bf16[608,128]{1,0:T(8,128)(2,1)S(1)}, u32[]{:S(2)}, u32[]{:S(2)}) collective-permute-start(bf16[608,128]{1,0:T(8,128)(2,1)S(1)} %get-tuple-element.37), channel_id=1, source_target_pairs={{0,16},{1,48},{2,80},{3,112},{4,144},{5,176},{6,208},{7,240},{8,27... | collective-permute-start | bytes 466952 | tf_op jit(solution)/shard_map/ppermute | solution.py:290
  29.4 22.6 %collective-permute-start.1 = (bf16[608,128]{1,0:T(8,128)(2,1)S(1)}, bf16[608,128]{1,0:T(8,128)(2,1)S(1)}, u32[]{:S(2)}, u32[]{:S(2)}) collective-permute-start(bf16[608,128]{1,0:T(8,128)(2,1)S(1)} %get-tuple-element.38), channel_id=1, source_target_pairs={{0,256},{1,288},{2,320},{3,352},{4,384},{5,416},{6,448},{7,480},{8... | collective-permute-start | bytes 466952 | tf_op jit(solution)/shard_map/ppermute | solution.py:290
  39.4 12.6 %collective-permute-start = (bf16[608,128]{1,0:T(8,128)(2,1)S(1)}, bf16[608,128]{1,0:T(8,128)(2,1)S(1)}, u32[]{:S(2)}, u32[]{:S(2)}) collective-permute-start(bf16[608,128]{1,0:T(8,128)(2,1)S(1)} %get-tuple-element.39), channel_id=1, source_target_pairs={{0,0},{1,32},{2,64},{3,96},{4,128},{5,160},{6,192},{7,224},{8,256}... | collective-permute-start | bytes 466952 | tf_op jit(solution)/shard_map/ppermute | solution.py:290
  52.0 4.6 %copy-start.2 = (bf16[8,32,1024]{2,1,0:T(8,128)(2,1)}, bf16[8,32,1024]{2,1,0:T(8,128)(2,1)S(1)}, u32[]{:S(2)}) copy-start(bf16[8,32,1024]{2,1,0:T(8,128)(2,1)S(1)} %all-to-all-done) | copy-start | bytes 1572868
  52.8 9.3 %all-to-all-start.1 = ((bf16[4,32,1216]{2,1,0:T(8,128)(2,1)}), bf16[4,32,1216]{2,1,0:T(8,128)(2,1)S(1)}, u32[]{:S(2)}, u32[]{:S(2)}) async-start(bf16[4,32,1216]{2,1,0:T(8,128)(2,1)} %broadcast_in_dim.71), calls=%async_computation.1 | async-start | bytes 655360 | tf_op jit(solution)/shard_map/all_to_all | solution.py:250
  56.2 60.2 %all-gather.2.cloned.1.call-start = ((), (), s32[]{:S(2)}) async-start(), calls=%async_computation.9 | async-start | bytes 2621440 | tf_op jit(solution)/shard_map/all_gather | solution.py:323
  62.1 1.0 copy-start.3
  105.2 6.7 %copy-start.6 = (f32[256,64]{0,1:T(8,128)S(1)}, f32[256,64]{0,1:T(8,128)}, u32[]{:S(2)}) copy-start(f32[256,64]{0,1:T(8,128)} %param.4) | copy-start | bytes 196612
  105.2 37.4 %all-to-all-start.4 = ((f32[32,5,16,128]{3,2,1,0:T(8,128)}), f32[32,5,16,128]{3,2,1,0:T(8,128)S(1)}, u32[]{:S(2)}, u32[]{:S(2)}) async-start(f32[32,5,16,128]{3,2,1,0:T(8,128)} %broadcast_in_dim.76), calls=%async_computation.4 | async-start | bytes 2621440 | tf_op jit(solution)/shard_map/all_to_all | solution.py:250
  111.8 81.0 %reduce-scatter.2.cloned.1.call-start = ((), (), s32[]{:S(2)}) async-start(), calls=%async_computation.10 | async-start | bytes 1114112 | tf_op jit(solution)/shard_map/reduce_scatter | solution.py:337
  116.4 1.9 copy-start.1
  116.4 2.0 copy-start.4
  142.6 50.2 %all-to-all-start.5 = ((f32[16,16,1024]{2,1,0:T(8,128)}), f32[16,16,1024]{2,1,0:T(8,128)S(1)}, u32[]{:S(2)}, u32[]{:S(2)}) async-start(f32[16,16,1024]{2,1,0:T(8,128)} %bitcast.51), calls=%async_computation.5 | async-start | bytes 2097152 | tf_op jit(solution)/shard_map/all_to_all | solution.py:340
  149.8 4.9 %collective-permute-start.4 = (f32[32,5,16,128]{3,2,1,0:T(8,128)S(1)}, f32[32,5,16,128]{3,2,1,0:T(8,128)S(1)}, u32[]{:S(2)}, u32[]{:S(2)}) collective-permute-start(f32[32,5,16,128]{3,2,1,0:T(8,128)S(1)} %all-to-all-done.4.mine_ref), channel_id=1, source_target_pairs={{0,1},{1,0},{2,3},{3,2},{4,5},{5,4},{6,7},{7,6},{8,9},{9,8},{10,11... | collective-permute-start | bytes 3932168 | tf_op jit(solution)/shard_map/ppermute | solution.py:336
  192.9 0.8 copy-start
  199.8 14.2 %all-to-all-start.6 = ((f32[32,1,512]{2,1,0:T(1,128)}), f32[32,1,512]{2,1,0:T(1,128)S(1)}, u32[]{:S(2)}, u32[]{:S(2)}) async-start(f32[32,1,512]{2,1,0:T(1,128)} %reshape.156), calls=%async_computation.7 | async-start | bytes 131072 | tf_op jit(solution)/shard_map/all_to_all | solution.py:347
Sparse Core Ops, SparseCore 0:
  59.2 49.4 all-gather.1
  120.3 63.4 reduce-scatter.1
